TPU v7x, 128 devices: a whole 4x4x4 slice. The times are simulated.
128 devices in a mesh: tm: 16 (over x, y), batch: 8 (over z, core).
Axes of the slice: x: 4, y: 4, z: 4, core: 2. Of those that a mesh axis runs over, the one named last changes fastest.
Arguments:
- rgb_maps: bfloat16 [32, 64, 16, 16, 128], P('batch', 'tm'), may hold values from -6 to 6
- flow_maps: bfloat16 [32, 64, 16, 16, 128], P('batch', 'tm'), may hold values from -6 to 6
- in_weights: bfloat16 [2, 1152, 128], replicated, may hold values from -0.1875 to 0.1875
- out_weights: bfloat16 [2, 1152, 128], replicated, may hold values from -0.1875 to 0.1875
- decay: float32 [2, 64, 128], P(None, 'tm'), may hold values from 0 to 1, as said below
- skip: float32 [2, 128], replicated, may hold values from 0.5 to 1.5
- proj_in: float32 [128, 2048], replicated, may hold values from -0.5 to 0.5
- proj_gain: float32 [2048], replicated, may hold values from 0.1 to 1.9
- proj_out: bfloat16 [2048, 2048], replicated, may hold values from -0.125 to 0.125
Outputs:
- grad_in: float32 [2, 1152, 128], replicated
- grad_out: float32 [2, 1152, 128], replicated
Inputs may be any that keep to these rules, and one draw needn't show every extreme that they name: Every entry of decay is a retention factor between 0 and 1.
All inputs are finite; a program needn't handle non-finite values.
Results may differ from a plain program's by a relative error of at most 0.015.
The roundings to bfloat16 on the way count: a program that leaves them out, or rounds other values in their place, can miss the bound.
Values may be sent and summed in bfloat16 or wider, within the bound.
No kernel may reach another device: no remote copies, remote signals or barrier semaphores. Data moves between devices by JAX's collectives and lax.ppermute only.
A program may use at most 192 MiB of HBM per device.

v0:
```python
import jax
import jax.numpy as jnp
from jax import lax
from jax.experimental import pallas as pl
from jax.experimental.pallas import tpu as pltpu
from jax.sharding import Mesh
from jax.sharding import PartitionSpec as P

TIME = ("xl", "y")
PLANE = ("xh", "xl")


LAMBDA_OFF = 0.0051
EPSILON = 1e-05
HIGHEST = lax.Precision.HIGHEST


BF16, F32 = jnp.bfloat16, jnp.float32


def pair_weights(weights):
    empty = jnp.zeros((weights.shape[0] // 3, weights.shape[1]), weights.dtype)
    upper = jnp.concatenate([weights, empty], axis=0)
    lower = jnp.concatenate([empty, weights], axis=0)
    return jnp.concatenate([upper, lower], axis=1)


def flipped(weights):
    channels = weights.shape[1]
    blocks = weights.reshape(9, channels, channels)[::-1]
    return blocks.transpose(0, 2, 1).reshape(9 * channels, channels)


def clear_edges(cols_ref):
    frames, _, _, side, lanes = cols_ref.shape
    cols_ref[:, 0, 0] = jnp.zeros((frames, side, lanes), BF16)
    cols_ref[:, side // 2, 1] = jnp.zeros((frames, side, lanes), BF16)


def spread_columns(maps, cols_ref):
    frames, pairs, _, side, channels = maps.shape
    flat = maps.astype(F32).reshape(frames * side * side, channels)
    column = lax.broadcasted_iota(jnp.int32, flat.shape, 0) & (side - 1)
    left = jnp.where(column == 0, 0.0, pltpu.roll(flat, 1, 0))
    right = jnp.where(column == side - 1, 0.0, pltpu.roll(flat, flat.shape[0] - 1, 0))
    for k, shifted in enumerate((left, flat, right)):
        rows = shifted.astype(BF16).reshape(frames, pairs, 2, side, channels)
        lanes = slice(k * channels, (k + 1) * channels)
        cols_ref[:, 0:pairs, 1, :, lanes] = rows[:, :, 0]
        cols_ref[:, 1 : pairs + 1, 0, :, lanes] = rows[:, :, 1]


def pair_patches(cols_ref):
    frames, ends, _, side, lanes = cols_ref.shape
    pairs = ends - 1
    pieces = [cols_ref[:, a : a + pairs, b].reshape(frames * pairs * side, lanes) for a in (0, 1) for b in (0, 1)]
    return jnp.concatenate(pieces, axis=1)


def pair_convolve(cols_ref, weights_ref):
    frames, ends, _, side, lanes = cols_ref.shape
    channels = lanes // 3
    both = jnp.dot(pair_patches(cols_ref), weights_ref[...], preferred_element_type=F32)
    shape = (frames, ends - 1, side, channels)
    return both[:, :channels].reshape(shape), both[:, channels:].reshape(shape)


def add_weight_product(cols_ref, grads, acc_ref):
    frames, pairs, _, side, channels = grads.shape
    rows = frames * pairs * side
    both = [grads[:, :, k].reshape(rows, channels) for k in range(2)]
    acc_ref[...] += lax.dot_general(
        jnp.concatenate(both, axis=1),
        pair_patches(cols_ref),
        (((0,), (0,)), ((), ())),
        preferred_element_type=F32,
    )


def folded(acc_ref):
    channels = acc_ref.shape[0] // 2
    width = acc_ref.shape[1] // 4
    total = acc_ref[:channels, : 3 * width] + acc_ref[channels:, width:]
    return total.T


def inputs_kernel(got_ref, weights_ref, inputs_ref, decays_ref, end_ref, cols_ref, carry_ref):
    step = pl.program_id(0)
    frames, pairs, _, side, channels = inputs_ref.shape
    cells = frames * side * side

    @pl.when(step == 0)
    def _():
        clear_edges(cols_ref)
        carry_ref[...] = jnp.zeros_like(carry_ref)

    spread_columns(got_ref[0, :cells].reshape(inputs_ref.shape), cols_ref)
    parts = got_ref[0, cells:].astype(F32)
    decays = parts[:frames] + parts[frames : 2 * frames] + parts[2 * frames : 3 * frames]
    decays_ref[0] = decays
    for k, rows in enumerate(pair_convolve(cols_ref, weights_ref)):
        inputs_ref[:, :, k] = rows.astype(BF16)
    carried = carry_ref[...]
    for t in range(frames):
        carried = decays[t : t + 1] * carried + inputs_ref[t].astype(F32)
    carry_ref[...] = carried

    @pl.when(step == pl.num_programs(0) - 1)
    def _():
        end_ref[...] = carried


def mixed_kernel(inputs_ref, decays_ref, income_ref, skip_ref, weights_ref, states_ref, slope_ref, pooled_ref, cols_ref, carry_ref, sum_ref):
    step = pl.program_id(0)
    frames = inputs_ref.shape[0]

    @pl.when(step == 0)
    def _():
        clear_edges(cols_ref)
        carry_ref[...] = income_ref[...]
        sum_ref[...] = jnp.zeros_like(sum_ref)

    carried = carry_ref[...]
    for t in range(frames):
        carried = decays_ref[0, t : t + 1] * carried + inputs_ref[t].astype(F32)
        states_ref[t] = carried.astype(BF16)
    carry_ref[...] = carried
    spread_columns(states_ref[...], cols_ref)
    total = sum_ref[...]
    for k, rows in enumerate(pair_convolve(cols_ref, weights_ref)):
        mixed = rows + skip_ref[...] * inputs_ref[:, :, k].astype(F32)
        sigma = jax.nn.sigmoid(mixed)
        slope_ref[:, :, k] = sigma * (1.0 + mixed * (1.0 - sigma))
        total = total + jnp.sum(mixed * sigma, axis=(0, 1))
    sum_ref[...] = total

    @pl.when(step == pl.num_programs(0) - 1)
    def _():
        pooled_ref[...] = jnp.sum(total, axis=0, keepdims=True)


def from_out_kernel(slope_ref, decays_ref, dpool_ref, weights_ref, dmix_ref, source_ref, end_ref, cols_ref, carry_ref):
    step = pl.program_id(0)
    frames = slope_ref.shape[0]

    @pl.when(step == 0)
    def _():
        clear_edges(cols_ref)
        carry_ref[...] = jnp.zeros_like(carry_ref)

    dmix_ref[...] = (dpool_ref[...] * slope_ref[...]).astype(BF16)
    spread_columns(dmix_ref[...], cols_ref)
    for k, rows in enumerate(pair_convolve(cols_ref, weights_ref)):
        source_ref[:, :, k] = rows
    carried = carry_ref[...]
    for t in reversed(range(frames)):
        carried = decays_ref[0, t : t + 1] * (source_ref[t] + carried)
    carry_ref[...] = carried

    @pl.when(step == pl.num_programs(0) - 1)
    def _():
        end_ref[...] = carried


def out_grad_kernel(states_ref, dmix_ref, grad_ref, cols_ref, acc_ref):
    step = pl.program_id(0)

    @pl.when(step == 0)
    def _():
        clear_edges(cols_ref)
        acc_ref[...] = jnp.zeros_like(acc_ref)

    spread_columns(states_ref[...], cols_ref)
    add_weight_product(cols_ref, dmix_ref[...], acc_ref)

    @pl.when(step == pl.num_programs(0) - 1)
    def _():
        grad_ref[...] = folded(acc_ref)


def in_grad_kernel(got_ref, slope_ref, source_ref, decays_ref, income_ref, dpool_ref, skip_ref, grad_ref, cols_ref, carry_ref, dinput_ref, acc_ref):
    step = pl.program_id(0)
    frames, _, _, side, _ = slope_ref.shape

    @pl.when(step == 0)
    def _():
        clear_edges(cols_ref)
        carry_ref[...] = income_ref[...]
        acc_ref[...] = jnp.zeros_like(acc_ref)

    spread_columns(got_ref[0, : frames * side * side].reshape(slope_ref.shape), cols_ref)
    carried = carry_ref[...]
    for t in reversed(range(frames)):
        carried = source_ref[t] + carried
        dmix = dpool_ref[...] * slope_ref[t]
        dinput_ref[t] = (carried + skip_ref[...] * dmix).astype(BF16)
        carried = decays_ref[0, t : t + 1] * carried
    carry_ref[...] = carried
    add_weight_product(cols_ref, dinput_ref[...], acc_ref)

    @pl.when(step == pl.num_programs(0) - 1)
    def _():
        grad_ref[...] = folded(acc_ref)


class Plan:
    def __init__(self, steps, frames, side, channels):
        self.steps, self.frames, self.side, self.channels = steps, frames, side, channels
        self.map = (side // 2, 2, side, channels)

    def whole(self, shape):
        return pl.BlockSpec(shape, lambda i: (0,) * len(shape))

    def order(self, back):
        return (lambda i: self.steps - 1 - i) if back else (lambda i: i)

    def maps(self, back=False):
        at = self.order(back)
        return pl.BlockSpec((self.frames, *self.map), lambda i: (at(i), 0, 0, 0, 0))

    def got(self, rows, back=False):
        at = self.order(back)
        return pl.BlockSpec((1, rows, self.channels), lambda i: (at(i), 0, 0))

    def decays(self, back=False):
        return self.got(self.frames, back)

    def maps_of(self, dtype):
        return jax.ShapeDtypeStruct((self.steps * self.frames, *self.map), dtype)

    def carry_of(self):
        return jax.ShapeDtypeStruct(self.map, F32)

    def decays_of(self):
        return jax.ShapeDtypeStruct((self.steps, self.frames, self.channels), F32)

    def grad_of(self):
        return jax.ShapeDtypeStruct((9 * self.channels, self.channels), F32)

    def cols(self):
        return pltpu.VMEM((self.frames, self.side // 2 + 1, 2, self.side, 3 * self.channels), BF16)

    def carry(self):
        return pltpu.VMEM(self.map, F32)

    def acc(self):
        return pltpu.VMEM((2 * self.channels, 12 * self.channels), F32)

    def row(self):
        return self.whole((1, self.channels))

    def weights(self):
        return self.whole((12 * self.channels, 2 * self.channels))

    def call(self, kernel, in_specs, out_shape, out_specs, scratch):
        cells = self.steps * self.frames * self.side * self.side
        work = 2 * 9 * cells * self.channels * self.channels
        return pl.pallas_call(
            kernel,
            grid=(self.steps,),
            in_specs=in_specs,
            out_specs=out_specs,
            out_shape=out_shape,
            scratch_shapes=scratch,
            cost_estimate=pl.CostEstimate(flops=2 * work, transcendentals=0, bytes_accessed=4 * cells * self.channels),
            compiler_params=pltpu.CompilerParams(dimension_semantics=("arbitrary",), vmem_limit_bytes=48 << 20),
        )


def swapped(x):
    return lax.ppermute(x, "core", [(0, 1), (1, 0)])


def from_cores(x):
    here, there = x, swapped(x)
    first = lax.axis_index("core") == 0
    return jnp.stack([jnp.where(first, here, there), jnp.where(first, there, here)])


def from_all(x, axes):
    peers = lax.axis_size(axes)
    return lax.all_to_all(jnp.broadcast_to(x[None], (peers, *x.shape)), axes, 0, 0, tiled=True)


def in_parts(x):
    high = lax.reduce_precision(x, 8, 7)
    middle = lax.reduce_precision(x - high, 8, 7)
    low = x - high - middle
    return jnp.concatenate([high, middle, low], axis=-2).astype(jnp.bfloat16)


def clips_to_devices(rgb_maps, flow_maps, decay, half):
    clips, frames, side, _, channels = rgb_maps.shape
    straight = half == 0
    first = jnp.where(straight, rgb_maps, flow_maps)
    second = jnp.where(straight, flow_maps, rgb_maps)
    pieces = jnp.stack([first, second]).reshape(2, clips, frames * side * side, channels)
    parts = in_parts(jnp.where(straight, decay, decay[::-1]))
    parts = jnp.pad(parts, ((0, 0), (0, 16 - 3 * frames), (0, 0)))
    parts = jnp.broadcast_to(parts[:, None], (2, clips, 16, channels))
    sent = jnp.concatenate([pieces, parts], axis=2).reshape(2 * clips, -1, channels)
    return lax.all_to_all(sent, TIME, 0, 0, tiled=True)


def batch_norm(values):
    center = jnp.mean(values, axis=1, keepdims=True)
    centered = values - center
    scale = lax.rsqrt(jnp.mean(centered * centered, axis=1, keepdims=True) + EPSILON)
    return centered * scale, scale


def norm_back(grad, normed, scale):
    mean = jnp.mean(grad, axis=0, keepdims=True)
    along = jnp.mean(grad * normed, axis=0, keepdims=True)
    return (grad - mean - normed * along) * scale


def projector_back(pooled, proj_in, proj_gain, proj_out, view):
    _, clips, channels = pooled.shape
    width = proj_in.shape[1]
    hidden = jnp.dot(
        pooled.reshape(2 * clips, channels), proj_in, precision=HIGHEST, preferred_element_type=jnp.float32
    )
    hidden_x, hidden_s = batch_norm(hidden.reshape(2, clips, width))
    hidden_n = hidden_x * proj_gain
    relu_b = jnp.maximum(hidden_n, 0.0).astype(jnp.bfloat16)
    z = jnp.dot(relu_b.reshape(2 * clips, width), proj_out, preferred_element_type=jnp.float32)
    z_x, z_s = batch_norm(z.reshape(2, clips, width))
    zn = z_x.astype(jnp.bfloat16)
    first = view == 0
    own = jnp.where(first, zn[0], zn[1])
    other = jnp.where(first, zn[1], zn[0])
    own_wide = own.astype(jnp.float32)
    other_wide = other.astype(jnp.float32)
    corr_diag = jnp.sum(own_wide * other_wide, axis=0) / clips
    extra = -2.0 * (1.0 - corr_diag) - 2.0 * LAMBDA_OFF * corr_diag
    gram = lax.dot_general(other, other, (((1,), (1,)), ((), ())), preferred_element_type=jnp.float32)
    spread = jnp.dot(gram, own_wide, precision=HIGHEST, preferred_element_type=jnp.float32)
    dzn = spread * (2.0 * LAMBDA_OFF / (clips * clips)) + other_wide * (extra / clips)
    dz_b = norm_back(
        dzn, jnp.where(first, z_x[0], z_x[1]), jnp.where(first, z_s[0], z_s[1])
    ).astype(jnp.bfloat16)
    drelu = lax.dot_general(dz_b, proj_out, (((1,), (1,)), ((), ())), preferred_element_type=jnp.float32)
    own_x = jnp.where(first, hidden_x[0], hidden_x[1])
    own_s = jnp.where(first, hidden_s[0], hidden_s[1])
    own_n = jnp.where(first, hidden_n[0], hidden_n[1])
    dxh = jnp.where(own_n > 0, drelu, 0.0) * proj_gain
    dhidden = norm_back(dxh, own_x, own_s)
    return dhidden


def summed(grads):
    rows, channels = grads.shape
    core = lax.axis_index("core")
    halves = grads.reshape(2, rows // 2, channels)
    mine = lax.dynamic_index_in_dim(halves, core, 0, False)
    given = lax.dynamic_index_in_dim(halves, 1 - core, 0, False)
    total = mine + swapped(given)
    pieces = total.astype(jnp.bfloat16).reshape(4, rows // 8, channels)
    total = jnp.sum(lax.all_to_all(pieces, "z", 0, 0, tiled=True).astype(jnp.float32), axis=0)
    total = jnp.sum(from_all(total.astype(jnp.bfloat16), "y").astype(jnp.float32), axis=0)
    seen = from_all(total.astype(jnp.bfloat16), PLANE).astype(jnp.float32)
    both = jnp.stack([seen[0] + seen[3], seen[1] + seen[2]]).astype(jnp.bfloat16)
    whole = from_cores(from_all(both, "z"))
    return whole.transpose(2, 0, 1, 3, 4).reshape(2, rows, channels).astype(jnp.float32)


def per_device(
    rgb_maps, flow_maps, in_weights, out_weights, decay, skip, proj_in, proj_gain, proj_out
):
    half = lax.axis_index("xh")
    view = lax.axis_index("xl") ^ half
    clip = lax.axis_index("y")
    batch = lax.axis_index(("z", "core"))
    clips_here = rgb_maps.shape[0]
    _, frames_here, side, _, channels = rgb_maps.shape
    got = clips_to_devices(rgb_maps, flow_maps, decay, half)
    steps, rows, _ = got.shape
    cell_count = 2 * steps * frames_here * side * side
    plan = Plan(steps, frames_here, side, channels)
    in_w = lax.dynamic_index_in_dim(in_weights, view, 0, False)
    out_w = lax.dynamic_index_in_dim(out_weights, view, 0, False)
    skip_v = lax.dynamic_index_in_dim(skip, view, 0, True)
    carry_spec = plan.whole(plan.map)

    inputs, decays, end = plan.call(
        inputs_kernel,
        [plan.got(rows), plan.weights()],
        [plan.maps_of(BF16), plan.decays_of(), plan.carry_of()],
        [plan.maps(), plan.decays(), carry_spec],
        [plan.cols(), plan.carry()],
    )(got, pair_weights(in_w))
    income = lax.ppermute(end, PLANE, [(0, 3), (1, 2)])
    states_b, slope, pooled_part = plan.call(
        mixed_kernel,
        [plan.maps(), plan.decays(), carry_spec, plan.row(), plan.weights()],
        [plan.maps_of(BF16), plan.maps_of(F32), jax.ShapeDtypeStruct((1, channels), F32)],
        [plan.maps(), plan.maps(), plan.row()],
        [plan.cols(), plan.carry(), pltpu.VMEM((side, channels), F32)],
    )(inputs, decays, income, skip_v, pair_weights(out_w))

    seen = from_all(from_cores(pooled_part[0]), ("xh", "xl", "y", "z"))
    seen = seen.reshape(2, 2, clips_here, 4, 2, channels)
    views = jnp.stack([seen[0, 0] + seen[1, 1], seen[0, 1] + seen[1, 0]]) / cell_count
    pooled = views.transpose(0, 2, 3, 1, 4).reshape(2, -1, channels)
    dhidden = projector_back(pooled, proj_in, proj_gain, proj_out, view)
    own_row = lax.dynamic_slice_in_dim(dhidden, batch * clips_here + clip, 1, 0)
    dpooled = lax.dot_general(own_row, proj_in, (((1,), (1,)), ((), ())), precision=HIGHEST)

    dpool = dpooled / cell_count
    dmix_b, source, end = plan.call(
        from_out_kernel,
        [plan.maps(True), plan.decays(True), plan.row(), plan.weights()],
        [plan.maps_of(BF16), plan.maps_of(F32), plan.carry_of()],
        [plan.maps(True), plan.maps(True), carry_spec],
        [plan.cols(), plan.carry()],
    )(slope, decays, dpool, pair_weights(flipped(out_w)))
    income = lax.ppermute(end, PLANE, [(3, 0), (2, 1)])
    out_grad = plan.call(
        out_grad_kernel,
        [plan.maps(), plan.maps()],
        plan.grad_of(),
        plan.whole((9 * channels, channels)),
        [plan.cols(), plan.acc()],
    )(states_b, dmix_b)
    in_grad = plan.call(
        in_grad_kernel,
        [plan.got(rows, True), plan.maps(True), plan.maps(True), plan.decays(True), carry_spec, plan.row(), plan.row()],
        plan.grad_of(),
        plan.whole((9 * channels, channels)),
        [plan.cols(), plan.carry(), pltpu.VMEM((frames_here, *plan.map), BF16), plan.acc()],
    )(got, slope, source, decays, income, dpool, skip_v)
    whole = summed(jnp.concatenate([in_grad, out_grad]))
    taps = in_grad.shape[0]
    return (whole[:, :taps], whole[:, taps:])


def solution(mesh):
    finer = Mesh(mesh.devices.reshape(2, 2, 4, 4, 2), ("xh", "xl", "y", "z", "core"))
    frames = ("xh", "xl", "y")
    return jax.shard_map(
        per_device,
        mesh=finer,
        in_specs=(
            P(("z", "core"), frames, None, None, None),
            P(("z", "core"), frames, None, None, None),
            P(),
            P(),
            P(None, frames, None),
            P(),
            P(),
            P(),
            P(),
        ),
        out_specs=(P(), P()),
        check_vma=False,
    )
```

profile of v0, /device:TPU:1, one launch (start us, length us, event | category | flops | bytes accessed | tf_op | source)
XLA Modules:
  0.0 167.7 jit_solution(17957268860980618810)
XLA Ops:
  1.5 1.7 %broadcast_select_fusion.1 = (bf16[4,4,16,16,128]{4,3,2,1,0:T(8,128)(2,1)S(1)}, bf16[4,4,16,16,128]{4,3,2,1,0:T(8,128)(2,1)S(1)}) fusion(bf16[4,4,16,16,128]{4,3,2,1,0:T(8,128)(2,1)} %param.9, bf16[4,4,16,16,128]{4,3,2,1,0:T(8,128)(2,1)} %param.10, pred[]{:T(512)S(6)} %eq.11), kind=kLoop, calls=%fused_computation.23 | loop fusion | flops 1048576 | bytes 4194305 | tf_op jit(solution)/shard_map/jit(_where)/select_n | solution.py:295
  3.2 1.5 pad_maximum_fusion
  4.7 5.9 %all-to-all-start = ((bf16[8,1040,128]{2,1,0:T(8,128)(2,1)}), bf16[8,1040,128]{2,1,0:T(8,128)(2,1)S(1)}, u32[]{:S(2)}, u32[]{:S(2)}) async-start(bf16[8,1040,128]{2,1,0:T(8,128)(2,1)} %bitcast.110), calls=%async_computation | async-start | bytes 4259840 | tf_op jit(solution)/shard_map/all_to_all | solution.py:302
  10.6 1.0 dynamic-slice_bitcast_fusion.1
  11.6 1.0 fusion.65
  12.6 0.9 fusion.14.weights_ref
  14.5 22.7 %all-to-all-done.got_ref = bf16[8,1040,128]{2,1,0:T(8,128)(2,1)S(1)} async-done(((bf16[8,1040,128]{2,1,0:T(8,128)(2,1)}), bf16[8,1040,128]{2,1,0:T(8,128)(2,1)S(1)}, u32[]{:S(2)}, u32[]{:S(2)}) %all-to-all-start) | async-done | bytes 2129952 | tf_op jit(solution)/shard_map/all_to_all | solution.py:302
  37.2 1.1 copy-done.3
  38.3 5.0 %shard_map.104 = (bf16[32,8,2,16,128]{4,3,2,1,0:T(8,128)(2,1)S(1)}, f32[8,4,128]{2,1,0:T(4,128)S(1)}, f32[8,2,16,128]{3,2,1,0:T(8,128)S(1)}) custom-call(bf16[8,1040,128]{2,1,0:T(8,128)(2,1)S(1)} %all-to-all-done.got_ref, bf16[1536,256]{1,0:T(8,128)(2,1)S(1)} %copy-done.3), custom_call_target="tpu_custom_call" | custom-call | flops 4831838208 | bytes 4194304 | tf_op jit(solution)/shard_map/pallas_call | solution.py:386
  43.3 4.4 %collective-permute-start = (f32[8,2,16,128]{3,2,1,0:T(8,128)S(1)}, f32[8,2,16,128]{3,2,1,0:T(8,128)S(1)}, u32[]{:S(2)}, u32[]{:S(2)}) collective-permute-start(f32[8,2,16,128]{3,2,1,0:T(8,128)S(1)} %get-tuple-element.13), channel_id=1, source_target_pairs={{0,96},{32,64},{1,97},{33,65},{2,98},{34,66},{3,99},{35,67},{4,100... | collective-permute-start | bytes 393224 | tf_op jit(solution)/shard_map/ppermute | solution.py:393
  47.7 1.8 %collective-permute-done.income_ref = f32[8,2,16,128]{3,2,1,0:T(8,128)S(1)} collective-permute-done((f32[8,2,16,128]{3,2,1,0:T(8,128)S(1)}, f32[8,2,16,128]{3,2,1,0:T(8,128)S(1)}, u32[]{:S(2)}, u32[]{:S(2)}) %collective-permute-start) | collective-permute-done | bytes 131104 | tf_op jit(solution)/shard_map/ppermute | solution.py:393
  49.6 6.9 %shard_map.105 = (bf16[32,8,2,16,128]{4,3,2,1,0:T(8,128)(2,1)S(1)}, f32[32,8,2,16,128]{4,3,2,1,0:T(8,128)}, f32[1,128]{1,0:T(1,128)S(1)}) custom-call(bf16[32,8,2,16,128]{4,3,2,1,0:T(8,128)(2,1)S(1)} %get-tuple-element.11.inputs_ref, f32[8,4,128]{2,1,0:T(4,128)S(1)} %get-tuple-element.12.decays_ref, f32[8,2,16,128]{3,2,1,0:T(8,128)S(1)} %collective-permute-done.income_ref, ...), custom_call_target="tpu_custom_call" | custom-call | flops 4831838208 | bytes 4194304 | tf_op jit(solution)/shard_map/pallas_call | solution.py:394
  56.4 1.4 copy-done.4
  57.8 1.8 %collective-permute-start.1 = (f32[128]{0:T(128)S(1)}, f32[128]{0:T(128)S(1)}, u32[]{:S(2)}, u32[]{:S(2)}) collective-permute-start(f32[128]{0:T(128)S(1)} %bitcast.106), channel_id=1, source_target_pairs={{0,1},{1,0},{2,3},{3,2},{4,5},{5,4},{6,7},{7,6},{8,9},{9,8},{10,11... | collective-permute-start | bytes 1544 | tf_op jit(solution)/shard_map/ppermute | solution.py:271
  61.1 10.4 %all-to-all-start.1 = ((f32[64,2,128]{2,1,0:T(2,128)}), f32[64,2,128]{2,1,0:T(2,128)S(1)}, u32[]{:S(2)}, u32[]{:S(2)}) async-start(f32[64,2,128]{2,1,0:T(2,128)} %broadcast_in_dim.12), calls=%async_computation.1 | async-start | bytes 131072 | tf_op jit(solution)/shard_map/all_to_all | solution.py:282
  71.5 2.0 %fusion.16.weights_ref = bf16[1536,256]{1,0:T(8,128)(2,1)} fusion(bf16[1152,128]{1,0:T(8,128)(2,1)} %bitcast.116), kind=kLoop, calls=%fused_computation.26 | loop fusion | flops 3145728 | bytes 1081344 | tf_op jit(solution)/shard_map/concatenate | solution.py:25
  73.5 6.4 %all-to-all-done.1 = f32[64,2,128]{2,1,0:T(2,128)S(1)} async-done(((f32[64,2,128]{2,1,0:T(2,128)}), f32[64,2,128]{2,1,0:T(2,128)S(1)}, u32[]{:S(2)}, u32[]{:S(2)}) %all-to-all-start.1) | async-done | bytes 65568 | tf_op jit(solution)/shard_map/all_to_all | solution.py:282
  81.0 5.1 %fusion.60 = (f32[2,2048]{1,0:T(2,128)S(1)}, f32[2,32,2048]{2,1,0:T(8,128)S(1)}) fusion(bf16[2048,2048]{1,0:T(8,128)(2,1)} %param.17, f32[2,32,2048]{2,1,0:T(8,128)S(1)} %get-tuple-element.29), kind=kOutput, calls=%fused_computation.120 | convolution fusion | flops 537260032 | bytes 9453568 | tf_op jit(solution)/shard_map/dot_general | solution.py:327
  87.1 2.6 %fusion.2 = f32[32,2048]{1,0:T(8,128)S(1)} fusion(bf16[2048,2048]{1,0:T(8,128)(2,1)S(1)} %bitcast.108, f32[2,32,2048]{2,1,0:T(8,128)S(1)} %get-tuple-element.29, f32[32,2048]{1,0:T(8,128)S(1)} %get-tuple-element.48, f32[2048]{0:T(1024)S(1)} %copy-done.7, f32[2048]{0:T(1024)S(1)} %bitcast.122, f32[2048]{0:T(1024)S(1)} %get-tuple-element.51, ...), kind=kOutput, calls=%fused_computation.3 | convolution fusion | flops 269090816 | bytes 9995264 | tf_op jit(solution)/shard_map/dot_general | solution.py:343
  90.8 9.1 %shard_map.106 = (bf16[32,8,2,16,128]{4,3,2,1,0:T(8,128)(2,1)S(1)}, f32[32,8,2,16,128]{4,3,2,1,0:T(8,128)}, f32[8,2,16,128]{3,2,1,0:T(8,128)S(1)}) custom-call(f32[32,8,2,16,128]{4,3,2,1,0:T(8,128)} %get-tuple-element.14.slope_ref, f32[8,4,128]{2,1,0:T(4,128)S(1)} %get-tuple-element.12.decays_ref, f32[1,128]{1,0:T(1,128)S(1)} %fusion.11.dpool_ref, ...), custom_call_target="tpu_custom_call" | custom-call | flops 4831838208 | bytes 4194304 | tf_op jit(solution)/shard_map/pallas_call | solution.py:411
  99.9 1.3 collective-permute-start.2
  101.2 6.2 %shard_map.108 = f32[1152,128]{1,0:T(8,128)S(1)} custom-call(bf16[32,8,2,16,128]{4,3,2,1,0:T(8,128)(2,1)S(1)} %copy-done.5, bf16[32,8,2,16,128]{4,3,2,1,0:T(8,128)(2,1)S(1)} %get-tuple-element.19.dmix_ref), custom_call_target="tpu_custom_call" | custom-call | flops 4831838208 | bytes 4194304 | tf_op jit(solution)/shard_map/pallas_call | solution.py:419
  107.4 9.7 %shard_map.107 = f32[1152,128]{1,0:T(8,128)S(1)} custom-call(bf16[8,1040,128]{2,1,0:T(8,128)(2,1)S(1)} %all-to-all-done.got_ref, f32[32,8,2,16,128]{4,3,2,1,0:T(8,128)} %get-tuple-element.14.slope_ref, f32[32,8,2,16,128]{4,3,2,1,0:T(8,128)} %get-tuple-element.16.source_ref, f32[8,4,128]{2,1,0:T(4,128)S(1)} %get-tuple-element.12.decays_ref, ...), custom_call_target="tpu_custom_call" | custom-call | flops 4831838208 | bytes 4194304 | tf_op jit(solution)/shard_map/pallas_call | solution.py:426
  118.0 2.2 %collective-permute-start.3 = (f32[1152,128]{1,0:T(8,128)}, f32[1152,128]{1,0:T(8,128)S(1)}, u32[]{:S(2)}, u32[]{:S(2)}) collective-permute-start(f32[1152,128]{1,0:T(8,128)} %dynamic-slice_bitcast_fusion), channel_id=1, source_target_pairs={{0,1},{1,0},{2,3},{3,2},{4,5},{5,4},{6,7},{7,6},{8,9},{9,8},{10,11... | collective-permute-start | bytes 1769480 | tf_op jit(solution)/shard_map/ppermute | solution.py:271
  120.2 1.8 %collective-permute-done.3 = f32[1152,128]{1,0:T(8,128)S(1)} collective-permute-done((f32[1152,128]{1,0:T(8,128)}, f32[1152,128]{1,0:T(8,128)S(1)}, u32[]{:S(2)}, u32[]{:S(2)}) %collective-permute-start.3) | collective-permute-done | bytes 589856 | tf_op jit(solution)/shard_map/ppermute | solution.py:271
  122.2 9.0 %all_to_all.30 = bf16[4,288,128]{2,1,0:T(8,128)(2,1)S(1)} all-to-all(bf16[4,288,128]{2,1,0:T(8,128)(2,1)S(1)} %bitcast.117), channel_id=1, replica_groups=mesh['xh'=2,'xl'=2,'y'=4,'z'=4,'core'=2] {'z'}, dimensions={0} | all-to-all | bytes 589824 | tf_op jit(solution)/shard_map/all_to_all | solution.py:360
  131.3 8.1 %all_to_all.31 = bf16[4,288,128]{2,1,0:T(8,128)(2,1)S(1)} all-to-all(bf16[4,288,128]{2,1,0:T(8,128)(2,1)S(1)} %broadcast_in_dim.13), channel_id=1, replica_groups=mesh['xh'=2,'xl'=2,'y'=4,'z'=4,'core'=2] {'y'}, dimensions={0} | all-to-all | bytes 589824 | tf_op jit(solution)/shard_map/all_to_all | solution.py:282
  139.4 9.8 %all_to_all.32 = bf16[4,288,128]{2,1,0:T(8,128)(2,1)S(1)} all-to-all(bf16[4,288,128]{2,1,0:T(8,128)(2,1)S(1)} %broadcast_in_dim.14), channel_id=1, replica_groups=mesh['xh'=2,'xl'=2,'y'=4,'z'=4,'core'=2] {'xh','xl'}, dimensions={0} | all-to-all | bytes 589824 | tf_op jit(solution)/shard_map/all_to_all | solution.py:282
  149.4 9.7 %all_to_all.33 = bf16[4,2,288,128]{3,2,1,0:T(8,128)(2,1)S(1)} all-to-all(bf16[4,2,288,128]{3,2,1,0:T(8,128)(2,1)S(1)} %broadcast_in_dim.15), channel_id=1, replica_groups=mesh['xh'=2,'xl'=2,'y'=4,'z'=4,'core'=2] {'z'}, dimensions={0} | all-to-all | bytes 1179648 | tf_op jit(solution)/shard_map/all_to_all | solution.py:282
  159.1 5.1 %collective-permute-start.4 = (bf16[4,2,288,128]{3,2,0,1:T(8,128)(2,1)S(1)}, bf16[4,2,288,128]{3,2,0,1:T(8,128)(2,1)S(1)}, u32[]{:S(2)}, u32[]{:S(2)}) collective-permute-start(bf16[4,2,288,128]{3,2,0,1:T(8,128)(2,1)S(1)} %copy.37), channel_id=1, source_target_pairs={{0,1},{1,0},{2,3},{3,2},{4,5},{5,4},{6,7},{7,6},{8,9},{9,8},{10,11... | collective-permute-start | bytes 1769480 | tf_op jit(solution)/shard_map/ppermute | solution.py:271
  164.2 1.6 collective-permute-done.4
  166.2 1.6 fusion.58
  (72 shorter events, 7.9 us)
Async XLA Ops:
  0.6 79.4 %copy-start = (f32[128,2048]{1,0:T(8,128)S(1)}, f32[128,2048]{1,0:T(8,128)}, u32[]{:S(2)}) copy-start(f32[128,2048]{1,0:T(8,128)} %param.15) | copy-start | bytes 3145732
  4.7 32.5 %all-to-all-start = ((bf16[8,1040,128]{2,1,0:T(8,128)(2,1)}), bf16[8,1040,128]{2,1,0:T(8,128)(2,1)S(1)}, u32[]{:S(2)}, u32[]{:S(2)}) async-start(bf16[8,1040,128]{2,1,0:T(8,128)(2,1)} %bitcast.110), calls=%async_computation | async-start | bytes 4259840 | tf_op jit(solution)/shard_map/all_to_all | solution.py:302
  37.2 1.1 copy-start.3
  38.3 9.4 %copy-start.6 = (bf16[2,1152,128]{2,1,0:T(8,128)(2,1)S(1)}, bf16[2,1152,128]{2,1,0:T(8,128)(2,1)}, u32[]{:S(2)}) copy-start(bf16[2,1152,128]{2,1,0:T(8,128)(2,1)} %param.12) | copy-start | bytes 1769476
  38.3 9.4 %copy-start.8 = (f32[2,128]{1,0:T(2,128)S(1)}, f32[2,128]{1,0:T(2,128)}, u32[]{:S(2)}) copy-start(f32[2,128]{1,0:T(2,128)} %param.14) | copy-start | bytes 3076
  38.3 11.3 %copy-start.2 = (bf16[1536,256]{1,0:T(8,128)(2,1)S(1)}, bf16[1536,256]{1,0:T(8,128)(2,1)}, u32[]{:S(2)}) copy-start(bf16[1536,256]{1,0:T(8,128)(2,1)} %fusion.15.weights_ref) | copy-start | bytes 2359300
  43.3 6.3 %collective-permute-start = (f32[8,2,16,128]{3,2,1,0:T(8,128)S(1)}, f32[8,2,16,128]{3,2,1,0:T(8,128)S(1)}, u32[]{:S(2)}, u32[]{:S(2)}) collective-permute-start(f32[8,2,16,128]{3,2,1,0:T(8,128)S(1)} %get-tuple-element.13), channel_id=1, source_target_pairs={{0,96},{32,64},{1,97},{33,65},{2,98},{34,66},{3,99},{35,67},{4,100... | collective-permute-start | bytes 393224 | tf_op jit(solution)/shard_map/ppermute | solution.py:393
  56.4 1.4 copy-start.4
  57.8 2.7 %collective-permute-start.1 = (f32[128]{0:T(128)S(1)}, f32[128]{0:T(128)S(1)}, u32[]{:S(2)}, u32[]{:S(2)}) collective-permute-start(f32[128]{0:T(128)S(1)} %bitcast.106), channel_id=1, source_target_pairs={{0,1},{1,0},{2,3},{3,2},{4,5},{5,4},{6,7},{7,6},{8,9},{9,8},{10,11... | collective-permute-start | bytes 1544 | tf_op jit(solution)/shard_map/ppermute | solution.py:271
  61.1 18.8 %all-to-all-start.1 = ((f32[64,2,128]{2,1,0:T(2,128)}), f32[64,2,128]{2,1,0:T(2,128)S(1)}, u32[]{:S(2)}, u32[]{:S(2)}) async-start(f32[64,2,128]{2,1,0:T(2,128)} %broadcast_in_dim.12), calls=%async_computation.1 | async-start | bytes 131072 | tf_op jit(solution)/shard_map/all_to_all | solution.py:282
  73.5 7.3 %copy-start.7 = (f32[2048]{0:T(1024)S(1)}, f32[2048]{0:T(1024)}, u32[]{:S(2)}) copy-start(f32[2048]{0:T(1024)} %param.16) | copy-start | bytes 24580
  81.0 6.0 %slice-start = ((s8[8388608]{0:T(1024)(128)(4,1)}), s8[4194304]{0:T(1024)(128)(4,1)S(1)}, s32[]{:S(2)}) async-start(s8[8388608]{0:T(1024)(128)(4,1)} %bitcast.107), calls=%async_computation.6 | async-start | bytes 8388608
  81.0 6.0 %slice-start.1 = ((s8[8388608]{0:T(1024)(128)(4,1)}), s8[4194304]{0:T(1024)(128)(4,1)S(1)}, s32[]{:S(2)}) async-start(s8[8388608]{0:T(1024)(128)(4,1)} %bitcast.107), calls=%async_computation.7 | async-start | bytes 8388608
  89.6 1.1 copy-start.1
  90.8 10.4 %copy-start.5 = (bf16[32,8,2,16,128]{4,3,2,1,0:T(8,128)(2,1)S(1)}, bf16[32,8,2,16,128]{4,3,2,1,0:T(8,128)(2,1)}, u32[]{:S(2)}) copy-start(bf16[32,8,2,16,128]{4,3,2,1,0:T(8,128)(2,1)} %copy-done.4) | copy-start | bytes 6291460
  99.9 7.5 %collective-permute-start.2 = (f32[8,2,16,128]{3,2,1,0:T(8,128)S(1)}, f32[8,2,16,128]{3,2,1,0:T(8,128)S(1)}, u32[]{:S(2)}, u32[]{:S(2)}) collective-permute-start(f32[8,2,16,128]{3,2,1,0:T(8,128)S(1)} %get-tuple-element.17), channel_id=1, source_target_pairs={{96,0},{64,32},{97,1},{65,33},{98,2},{66,34},{99,3},{67,35},{100,4... | collective-permute-start | bytes 393224 | tf_op jit(solution)/shard_map/ppermute | solution.py:418
  118.0 4.1 %collective-permute-start.3 = (f32[1152,128]{1,0:T(8,128)}, f32[1152,128]{1,0:T(8,128)S(1)}, u32[]{:S(2)}, u32[]{:S(2)}) collective-permute-start(f32[1152,128]{1,0:T(8,128)} %dynamic-slice_bitcast_fusion), channel_id=1, source_target_pairs={{0,1},{1,0},{2,3},{3,2},{4,5},{5,4},{6,7},{7,6},{8,9},{9,8},{10,11... | collective-permute-start | bytes 1769480 | tf_op jit(solution)/shard_map/ppermute | solution.py:271
  159.1 6.8 %collective-permute-start.4 = (bf16[4,2,288,128]{3,2,0,1:T(8,128)(2,1)S(1)}, bf16[4,2,288,128]{3,2,0,1:T(8,128)(2,1)S(1)}, u32[]{:S(2)}, u32[]{:S(2)}) collective-permute-start(bf16[4,2,288,128]{3,2,0,1:T(8,128)(2,1)S(1)} %copy.37), channel_id=1, source_target_pairs={{0,1},{1,0},{2,3},{3,2},{4,5},{5,4},{6,7},{7,6},{8,9},{9,8},{10,11... | collective-permute-start | bytes 1769480 | tf_op jit(solution)/shard_map/ppermute | solution.py:271
where the time goes:
time: 169 us; the launch traced here: 168 us
  Pallas kernels  36.8 us (22%)
  blocking collectives  36.5 us (22%)
  waiting for transfers between devices  34.4 us (20%)
  starting transfers between devices  31.1 us (18%)
  matrix products  9.81 us (6%)
  other arithmetic  9.15 us (5%)
  local copies, waits for them, and re-layouts  8.85 us (5%)
    all_to_all x3, blocking collectives, from_all(): lax.all_to_all(jnp.broadcast_to(x[None], (peers, *x.shape)), axes, 0, 0,...  27.5 us
    all_to_all x1, waiting for transfers between devices, clips_to_devices(): return lax.all_to_all(sent, TIME, 0, 0, tiled=True)  22.7 us
    all_to_all x1, starting transfers between devices, from_all(): lax.all_to_all(jnp.broadcast_to(x[None], (peers, *x.shape)), axes, 0, 0,...  10.4 us
    pallas_call x1, Pallas kernels, per_device(): plan.call(in_grad_kernel, [plan.got(rows, True), plan.maps(True), plan.ma...  9.7 us
    ppermute x3, starting transfers between devices, swapped(): return lax.ppermute(x, 'core', [(0, 1), (1, 0)])  9.11 us
    pallas_call x1, Pallas kernels, per_device(): plan.call(from_out_kernel, [plan.maps(True), plan.decays(True), plan.row(...  9.1 us
    all_to_all x1, blocking collectives, summed(): lax.all_to_all(pieces, 'z', 0, 0, tiled=True).astype(jnp.float32)  9.01 us
    pallas_call x1, Pallas kernels, per_device(): plan.call(mixed_kernel, [plan.maps(), plan.decays(), carry_spec, plan.row...  6.86 us
  transfers between devices with their start and end apart: 7, of which 5 were waited for; matrix products, arithmetic and copies ran while one was open for 4% of the time, Pallas kernels for 4%

commit v1 on v0

--- a/solution.py
+++ b/solution.py
@@ -18,17 +18,34 @@
 BF16, F32 = jnp.bfloat16, jnp.float32
 
 
-def pair_weights(weights):
-    empty = jnp.zeros((weights.shape[0] // 3, weights.shape[1]), weights.dtype)
-    upper = jnp.concatenate([weights, empty], axis=0)
-    lower = jnp.concatenate([empty, weights], axis=0)
-    return jnp.concatenate([upper, lower], axis=1)
-
-
-def flipped(weights):
-    channels = weights.shape[1]
-    blocks = weights.reshape(9, channels, channels)[::-1]
-    return blocks.transpose(0, 2, 1).reshape(9 * channels, channels)
+def pair_weights(weights_ref, both_ref):
+    taps, channels = weights_ref.shape[1:]
+    third = taps // 3
+    both_ref[:taps, :channels] = weights_ref[0]
+    both_ref[taps:, :channels] = jnp.zeros((third, channels), BF16)
+    both_ref[:third, channels:] = jnp.zeros((third, channels), BF16)
+    both_ref[third:, channels:] = weights_ref[0]
+
+
+def flipped_pair_weights(weights_ref, both_ref):
+    taps, channels = weights_ref.shape[1:]
+    third = taps // 3
+    both_ref[taps:, :channels] = jnp.zeros((third, channels), BF16)
+    both_ref[:third, channels:] = jnp.zeros((third, channels), BF16)
+    for k in range(taps // channels):
+        block = weights_ref[0, taps - (k + 1) * channels : taps - k * channels].astype(F32).T.astype(BF16)
+        both_ref[k * channels : (k + 1) * channels, :channels] = block
+        both_ref[third + k * channels : third + (k + 1) * channels, channels:] = block
+
+
+def take_carry(carry_ref, income_ref, has_income):
+    @pl.when(has_income)
+    def _():
+        carry_ref[...] = income_ref[...]
+
+    @pl.when(jnp.logical_not(has_income))
+    def _():
+        carry_ref[...] = jnp.zeros_like(carry_ref)
 
 
 def clear_edges(cols_ref):
@@ -84,7 +101,7 @@
     return total.T
 
 
-def inputs_kernel(got_ref, weights_ref, inputs_ref, decays_ref, end_ref, cols_ref, carry_ref):
+def inputs_kernel(place_ref, got_ref, weights_ref, inputs_ref, decays_ref, end_ref, cols_ref, both_ref, carry_ref):
     step = pl.program_id(0)
     frames, pairs, _, side, channels = inputs_ref.shape
     cells = frames * side * side
@@ -92,13 +109,14 @@
     @pl.when(step == 0)
     def _():
         clear_edges(cols_ref)
+        pair_weights(weights_ref, both_ref)
         carry_ref[...] = jnp.zeros_like(carry_ref)
 
     spread_columns(got_ref[0, :cells].reshape(inputs_ref.shape), cols_ref)
     parts = got_ref[0, cells:].astype(F32)
     decays = parts[:frames] + parts[frames : 2 * frames] + parts[2 * frames : 3 * frames]
     decays_ref[0] = decays
-    for k, rows in enumerate(pair_convolve(cols_ref, weights_ref)):
+    for k, rows in enumerate(pair_convolve(cols_ref, both_ref)):
         inputs_ref[:, :, k] = rows.astype(BF16)
     carried = carry_ref[...]
     for t in range(frames):
@@ -110,14 +128,15 @@
         end_ref[...] = carried
 
 
-def mixed_kernel(inputs_ref, decays_ref, income_ref, skip_ref, weights_ref, states_ref, slope_ref, pooled_ref, cols_ref, carry_ref, sum_ref):
+def mixed_kernel(place_ref, inputs_ref, decays_ref, income_ref, skip_ref, weights_ref, states_ref, slope_ref, pooled_ref, cols_ref, both_ref, carry_ref, sum_ref):
     step = pl.program_id(0)
     frames = inputs_ref.shape[0]
 
     @pl.when(step == 0)
     def _():
         clear_edges(cols_ref)
-        carry_ref[...] = income_ref[...]
+        pair_weights(weights_ref, both_ref)
+        take_carry(carry_ref, income_ref, place_ref[0] == 1)
         sum_ref[...] = jnp.zeros_like(sum_ref)
 
     carried = carry_ref[...]
@@ -127,8 +146,8 @@
     carry_ref[...] = carried
     spread_columns(states_ref[...], cols_ref)
     total = sum_ref[...]
-    for k, rows in enumerate(pair_convolve(cols_ref, weights_ref)):
-        mixed = rows + skip_ref[...] * inputs_ref[:, :, k].astype(F32)
+    for k, rows in enumerate(pair_convolve(cols_ref, both_ref)):
+        mixed = rows + skip_ref[0] * inputs_ref[:, :, k].astype(F32)
         sigma = jax.nn.sigmoid(mixed)
         slope_ref[:, :, k] = sigma * (1.0 + mixed * (1.0 - sigma))
         total = total + jnp.sum(mixed * sigma, axis=(0, 1))
@@ -139,18 +158,19 @@
         pooled_ref[...] = jnp.sum(total, axis=0, keepdims=True)
 
 
-def from_out_kernel(slope_ref, decays_ref, dpool_ref, weights_ref, dmix_ref, source_ref, end_ref, cols_ref, carry_ref):
+def from_out_kernel(place_ref, slope_ref, decays_ref, dpool_ref, weights_ref, dmix_ref, source_ref, end_ref, cols_ref, both_ref, carry_ref):
     step = pl.program_id(0)
     frames = slope_ref.shape[0]
 
     @pl.when(step == 0)
     def _():
         clear_edges(cols_ref)
+        flipped_pair_weights(weights_ref, both_ref)
         carry_ref[...] = jnp.zeros_like(carry_ref)
 
     dmix_ref[...] = (dpool_ref[...] * slope_ref[...]).astype(BF16)
     spread_columns(dmix_ref[...], cols_ref)
-    for k, rows in enumerate(pair_convolve(cols_ref, weights_ref)):
+    for k, rows in enumerate(pair_convolve(cols_ref, both_ref)):
         source_ref[:, :, k] = rows
     carried = carry_ref[...]
     for t in reversed(range(frames)):
@@ -162,7 +182,7 @@
         end_ref[...] = carried
 
 
-def out_grad_kernel(states_ref, dmix_ref, grad_ref, cols_ref, acc_ref):
+def out_grad_kernel(place_ref, states_ref, dmix_ref, grad_ref, cols_ref, acc_ref):
     step = pl.program_id(0)
 
     @pl.when(step == 0)
@@ -178,14 +198,14 @@
         grad_ref[...] = folded(acc_ref)
 
 
-def in_grad_kernel(got_ref, slope_ref, source_ref, decays_ref, income_ref, dpool_ref, skip_ref, grad_ref, cols_ref, carry_ref, dinput_ref, acc_ref):
+def in_grad_kernel(place_ref, got_ref, slope_ref, source_ref, decays_ref, income_ref, dpool_ref, skip_ref, grad_ref, cols_ref, carry_ref, dinput_ref, acc_ref):
     step = pl.program_id(0)
     frames, _, _, side, _ = slope_ref.shape
 
     @pl.when(step == 0)
     def _():
         clear_edges(cols_ref)
-        carry_ref[...] = income_ref[...]
+        take_carry(carry_ref, income_ref, place_ref[0] == 0)
         acc_ref[...] = jnp.zeros_like(acc_ref)
 
     spread_columns(got_ref[0, : frames * side * side].reshape(slope_ref.shape), cols_ref)
@@ -193,7 +213,7 @@
     for t in reversed(range(frames)):
         carried = source_ref[t] + carried
         dmix = dpool_ref[...] * slope_ref[t]
-        dinput_ref[t] = (carried + skip_ref[...] * dmix).astype(BF16)
+        dinput_ref[t] = (carried + skip_ref[0] * dmix).astype(BF16)
         carried = decays_ref[0, t : t + 1] * carried
     carry_ref[...] = carried
     add_weight_product(cols_ref, dinput_ref[...], acc_ref)
@@ -209,22 +229,25 @@
         self.map = (side // 2, 2, side, channels)
 
     def whole(self, shape):
-        return pl.BlockSpec(shape, lambda i: (0,) * len(shape))
+        return pl.BlockSpec(shape, lambda i, place: (0,) * len(shape))
 
     def order(self, back):
         return (lambda i: self.steps - 1 - i) if back else (lambda i: i)
 
     def maps(self, back=False):
         at = self.order(back)
-        return pl.BlockSpec((self.frames, *self.map), lambda i: (at(i), 0, 0, 0, 0))
+        return pl.BlockSpec((self.frames, *self.map), lambda i, place: (at(i), 0, 0, 0, 0))
 
     def got(self, rows, back=False):
         at = self.order(back)
-        return pl.BlockSpec((1, rows, self.channels), lambda i: (at(i), 0, 0))
+        return pl.BlockSpec((1, rows, self.channels), lambda i, place: (at(i), 0, 0))
 
     def decays(self, back=False):
         return self.got(self.frames, back)
 
+    def of_view(self, rows):
+        return pl.BlockSpec((1, rows, self.channels), lambda i, place: (place[1], 0, 0))
+
     def maps_of(self, dtype):
         return jax.ShapeDtypeStruct((self.steps * self.frames, *self.map), dtype)
 
@@ -249,21 +272,24 @@
     def row(self):
         return self.whole((1, self.channels))
 
-    def weights(self):
-        return self.whole((12 * self.channels, 2 * self.channels))
+    def both(self):
+        return pltpu.VMEM((12 * self.channels, 2 * self.channels), BF16)
 
     def call(self, kernel, in_specs, out_shape, out_specs, scratch):
         cells = self.steps * self.frames * self.side * self.side
         work = 2 * 9 * cells * self.channels * self.channels
         return pl.pallas_call(
             kernel,
-            grid=(self.steps,),
-            in_specs=in_specs,
-            out_specs=out_specs,
             out_shape=out_shape,
-            scratch_shapes=scratch,
+            grid_spec=pltpu.PrefetchScalarGridSpec(
+                num_scalar_prefetch=1,
+                grid=(self.steps,),
+                in_specs=in_specs,
+                out_specs=out_specs,
+                scratch_shapes=scratch,
+            ),
             cost_estimate=pl.CostEstimate(flops=2 * work, transcendentals=0, bytes_accessed=4 * cells * self.channels),
-            compiler_params=pltpu.CompilerParams(dimension_semantics=("arbitrary",), vmem_limit_bytes=48 << 20),
+            compiler_params=pltpu.CompilerParams(dimension_semantics=("arbitrary",), vmem_limit_bytes=16 << 20),
         )
 
 
@@ -349,20 +375,57 @@
     return dhidden
 
 
-def summed(grads):
-    rows, channels = grads.shape
-    core = lax.axis_index("core")
-    halves = grads.reshape(2, rows // 2, channels)
-    mine = lax.dynamic_index_in_dim(halves, core, 0, False)
-    given = lax.dynamic_index_in_dim(halves, 1 - core, 0, False)
-    total = mine + swapped(given)
-    pieces = total.astype(jnp.bfloat16).reshape(4, rows // 8, channels)
-    total = jnp.sum(lax.all_to_all(pieces, "z", 0, 0, tiled=True).astype(jnp.float32), axis=0)
-    total = jnp.sum(from_all(total.astype(jnp.bfloat16), "y").astype(jnp.float32), axis=0)
-    seen = from_all(total.astype(jnp.bfloat16), PLANE).astype(jnp.float32)
-    both = jnp.stack([seen[0] + seen[3], seen[1] + seen[2]]).astype(jnp.bfloat16)
-    whole = from_cores(from_all(both, "z"))
-    return whole.transpose(2, 0, 1, 3, 4).reshape(2, rows, channels).astype(jnp.float32)
+def from_other_half(x):
+    return lax.ppermute(x, PLANE, [(0, 3), (1, 2), (2, 1), (3, 0)])
+
+
+def from_peer(x, axes, k):
+    return lax.ppermute(x, axes, [(i, i ^ k) for i in range(4)])
+
+
+def from_ring(x, axes):
+    return [x] + [from_peer(x, axes, k) for k in (1, 2, 3)]
+
+
+def total_of(arrays):
+    return sum(a.astype(F32) for a in arrays)
+
+
+def place_kernel(place_ref, *refs):
+    view, core, ring = place_ref[1], place_ref[2], place_ref[3]
+    outs = refs[8:]
+    for shift, pieces in enumerate((refs[:4], refs[4:8])):
+        for k, piece in enumerate(pieces):
+            rows = piece.shape[2]
+            start = pl.multiple_of((4 * (core ^ shift) + (ring ^ k)) * rows, rows)
+            for n, out in enumerate(outs):
+                for v in range(2):
+                    out[view ^ v, pl.ds(start, rows)] = piece[n, v].astype(F32)
+
+
+def summed(grads, place):
+    taps, channels = grads[0].shape
+    core, ring = lax.axis_index("core"), lax.axis_index("z")
+    halves = jnp.stack(grads).reshape(len(grads), 2, 4, taps // 8, channels)
+    mine = lax.dynamic_index_in_dim(halves, core, 1, False)
+    given = lax.dynamic_index_in_dim(halves, 1 - core, 1, False)
+    pieces = (mine + swapped(given)).astype(BF16)
+    parts = [lax.dynamic_index_in_dim(pieces, ring, 1, False)]
+    parts += [from_peer(lax.dynamic_index_in_dim(pieces, ring ^ k, 1, False), "z", k) for k in (1, 2, 3)]
+    parts = from_ring(total_of(parts).astype(BF16), "y")
+    parts = from_ring(total_of(parts).astype(BF16), PLANE)
+    both = jnp.stack([total_of([parts[0], parts[3]]), total_of([parts[1], parts[2]])], axis=1).astype(BF16)
+    mine = from_ring(both, "z")
+    given = [swapped(a) for a in mine]
+    whole = jax.ShapeDtypeStruct((2, taps, channels), F32)
+    return tuple(
+        pl.pallas_call(
+            place_kernel,
+            out_shape=[whole] * len(grads),
+            in_specs=[pl.BlockSpec(memory_space=pltpu.SMEM)] + [pl.BlockSpec(memory_space=pltpu.VMEM)] * 8,
+            compiler_params=pltpu.CompilerParams(vmem_limit_bytes=16 << 20),
+        )(place, *mine, *given)
+    )
 
 
 def per_device(
@@ -378,26 +441,27 @@
     steps, rows, _ = got.shape
     cell_count = 2 * steps * frames_here * side * side
     plan = Plan(steps, frames_here, side, channels)
-    in_w = lax.dynamic_index_in_dim(in_weights, view, 0, False)
-    out_w = lax.dynamic_index_in_dim(out_weights, view, 0, False)
-    skip_v = lax.dynamic_index_in_dim(skip, view, 0, True)
+    taps = in_weights.shape[1]
+    weights = plan.of_view(taps)
+    skips = skip.reshape(2, 1, channels)
+    place = jnp.stack([half, view, lax.axis_index("core"), lax.axis_index("z")]).astype(jnp.int32)
     carry_spec = plan.whole(plan.map)
 
     inputs, decays, end = plan.call(
         inputs_kernel,
-        [plan.got(rows), plan.weights()],
+        [plan.got(rows), weights],
         [plan.maps_of(BF16), plan.decays_of(), plan.carry_of()],
         [plan.maps(), plan.decays(), carry_spec],
-        [plan.cols(), plan.carry()],
-    )(got, pair_weights(in_w))
-    income = lax.ppermute(end, PLANE, [(0, 3), (1, 2)])
+        [plan.cols(), plan.both(), plan.carry()],
+    )(place, got, in_weights)
+    income = from_other_half(end)
     states_b, slope, pooled_part = plan.call(
         mixed_kernel,
-        [plan.maps(), plan.decays(), carry_spec, plan.row(), plan.weights()],
+        [plan.maps(), plan.decays(), carry_spec, plan.of_view(1), weights],
         [plan.maps_of(BF16), plan.maps_of(F32), jax.ShapeDtypeStruct((1, channels), F32)],
         [plan.maps(), plan.maps(), plan.row()],
-        [plan.cols(), plan.carry(), pltpu.VMEM((side, channels), F32)],
-    )(inputs, decays, income, skip_v, pair_weights(out_w))
+        [plan.cols(), plan.both(), plan.carry(), pltpu.VMEM((side, channels), F32)],
+    )(place, inputs, decays, income, skips, out_weights)
 
     seen = from_all(from_cores(pooled_part[0]), ("xh", "xl", "y", "z"))
     seen = seen.reshape(2, 2, clips_here, 4, 2, channels)
@@ -410,29 +474,27 @@
     dpool = dpooled / cell_count
     dmix_b, source, end = plan.call(
         from_out_kernel,
-        [plan.maps(True), plan.decays(True), plan.row(), plan.weights()],
+        [plan.maps(True), plan.decays(True), plan.row(), weights],
         [plan.maps_of(BF16), plan.maps_of(F32), plan.carry_of()],
         [plan.maps(True), plan.maps(True), carry_spec],
-        [plan.cols(), plan.carry()],
-    )(slope, decays, dpool, pair_weights(flipped(out_w)))
-    income = lax.ppermute(end, PLANE, [(3, 0), (2, 1)])
+        [plan.cols(), plan.both(), plan.carry()],
+    )(place, slope, decays, dpool, out_weights)
+    income = from_other_half(end)
     out_grad = plan.call(
         out_grad_kernel,
         [plan.maps(), plan.maps()],
         plan.grad_of(),
         plan.whole((9 * channels, channels)),
         [plan.cols(), plan.acc()],
-    )(states_b, dmix_b)
+    )(place, states_b, dmix_b)
     in_grad = plan.call(
         in_grad_kernel,
-        [plan.got(rows, True), plan.maps(True), plan.maps(True), plan.decays(True), carry_spec, plan.row(), plan.row()],
+        [plan.got(rows, True), plan.maps(True), plan.maps(True), plan.decays(True), carry_spec, plan.row(), plan.of_view(1)],
         plan.grad_of(),
         plan.whole((9 * channels, channels)),
         [plan.cols(), plan.carry(), pltpu.VMEM((frames_here, *plan.map), BF16), plan.acc()],
-    )(got, slope, source, decays, income, dpool, skip_v)
-    whole = summed(jnp.concatenate([in_grad, out_grad]))
-    taps = in_grad.shape[0]
-    return (whole[:, :taps], whole[:, taps:])
+    )(place, got, slope, source, decays, income, dpool, skips)
+    return summed([in_grad, out_grad], place)
 
 
 def solution(mesh):

time: 169 us -> 155 us (0.917)
  blocking collectives: 36.5 us -> 0 us
  starting transfers between devices: 31.1 us -> 48.5 us
  waiting for transfers between devices: 34.4 us -> 50.6 us
  local copies, waits for them, and re-layouts: 8.85 us -> 3.81 us
  other arithmetic: 9.15 us -> 5.81 us
  Pallas kernels: 36.8 us -> 34.9 us
    all_to_all x4 -> x0, blocking collectives: 36.5 us -> none  [the longest x3 27.5 us: from_all(): lax.all_to_all(jnp.broadcast_to(x[None], (peers, *x.shape)), axes, 0, 0,...]
    ppermute x2 -> x14, starting transfers between devices: 5.65 us -> 19.3 us  [the longest x12 15.7 us: from_peer(): return lax.ppermute(x, axes, [(i, i ^ k) for i in range(4)])]
    ppermute x2 -> x14, waiting for transfers between devices: 1.85 us -> 12 us  [the longest x12 9 us: from_peer(): return lax.ppermute(x, axes, [(i, i ^ k) for i in range(4)])]
    ppermute x3 -> x6, starting transfers between devices: 9.11 us -> 13.9 us  [swapped(): return lax.ppermute(x, 'core', [(0, 1), (1, 0)])]
    concatenate x4 -> x0, other arithmetic: 4 us -> none  [the longest x3 3.92 us: pair_weights(): return jnp.concatenate([upper, lower], axis=1)]
    all_to_all x1, waiting for transfers between devices: 22.7 us -> 26.5 us  [clips_to_devices(): return lax.all_to_all(sent, TIME, 0, 0, tiled=True)]
    pallas_call x1, Pallas kernels: 9.1 us -> 6.03 us  [per_device(): plan.call(from_out_kernel, [plan.maps(True), plan.decays(True), plan.row(...]
    squeeze x3 -> x1, local copies, waits for them, and re-layouts: 2.83 us -> 0.03 us  [summed(): lax.dynamic_index_in_dim(pieces, ring ^ k, 1, False)]
  transfers between devices with their start and end apart: 7 -> 22, of which waited for: 5 -> 13; matrix products, arithmetic and copies ran while one was open for 4% -> 0% of each run, Pallas kernels for 4% -> 4%
where the time goes in v1:
time: 155 us; the launch traced here: 154 us
  waiting for transfers between devices  50.6 us (33%)
  starting transfers between devices  48.5 us (31%)
  Pallas kernels  34.9 us (23%)
  matrix products  9.8 us (6%)
  other arithmetic  5.81 us (4%)
  local copies, waits for them, and re-layouts  3.81 us (2%)
    all_to_all x1, waiting for transfers between devices, clips_to_devices(): return lax.all_to_all(sent, TIME, 0, 0, tiled=True)  26.5 us
    ppermute x12, starting transfers between devices, from_peer(): return lax.ppermute(x, axes, [(i, i ^ k) for i in range(4)])  15.7 us
    ppermute x6, starting transfers between devices, swapped(): return lax.ppermute(x, 'core', [(0, 1), (1, 0)])  13.9 us
    all_to_all x1, starting transfers between devices, from_all(): lax.all_to_all(jnp.broadcast_to(x[None], (peers, *x.shape)), axes, 0, 0,...  9.4 us
    ppermute x12, waiting for transfers between devices, from_peer(): return lax.ppermute(x, axes, [(i, i ^ k) for i in range(4)])  9 us
    all_to_all x1, waiting for transfers between devices, from_all(): lax.all_to_all(jnp.broadcast_to(x[None], (peers, *x.shape)), axes, 0, 0,...  8.44 us
    pallas_call x1, Pallas kernels, per_device(): plan.call(in_grad_kernel, [plan.got(rows, True), plan.maps(True), plan.ma...  7.92 us
    pallas_call x1, Pallas kernels, per_device(): plan.call(out_grad_kernel, [plan.maps(), plan.maps()], plan.grad_of(), pl...  6.74 us
  transfers between devices with their start and end apart: 22, of which 13 were waited for; matrix products, arithmetic and copies ran while one was open for 0% of the time, Pallas kernels for 4%

profile of v1, /device:TPU:1, one launch (start us, length us, event | category | flops | bytes accessed | tf_op | source)
XLA Modules:
  0.0 154.5 jit_solution(16211875133252367315)
XLA Ops:
  1.5 1.7 %broadcast_select_fusion.1 = (bf16[4,4,16,16,128]{4,3,2,1,0:T(8,128)(2,1)S(1)}, bf16[4,4,16,16,128]{4,3,2,1,0:T(8,128)(2,1)S(1)}) fusion(bf16[4,4,16,16,128]{4,3,2,1,0:T(8,128)(2,1)} %param.9, bf16[4,4,16,16,128]{4,3,2,1,0:T(8,128)(2,1)} %param.10, pred[]{:T(512)S(6)} %eq.9), kind=kLoop, calls=%fused_computation.17 | loop fusion | flops 1048576 | bytes 4194305 | tf_op jit(solution)/shard_map/jit(_where)/select_n | solution.py:321
  3.2 1.5 pad_maximum_fusion
  4.7 5.9 %all-to-all-start = ((bf16[8,1040,128]{2,1,0:T(8,128)(2,1)}), bf16[8,1040,128]{2,1,0:T(8,128)(2,1)S(1)}, u32[]{:S(2)}, u32[]{:S(2)}) async-start(bf16[8,1040,128]{2,1,0:T(8,128)(2,1)} %bitcast.124), calls=%async_computation | async-start | bytes 4259840 | tf_op jit(solution)/shard_map/all_to_all | solution.py:328
  10.7 26.5 %all-to-all-done.got_ref = bf16[8,1040,128]{2,1,0:T(8,128)(2,1)S(1)} async-done(((bf16[8,1040,128]{2,1,0:T(8,128)(2,1)}), bf16[8,1040,128]{2,1,0:T(8,128)(2,1)S(1)}, u32[]{:S(2)}, u32[]{:S(2)}) %all-to-all-start) | async-done | bytes 2129952 | tf_op jit(solution)/shard_map/all_to_all | solution.py:328
  38.2 5.6 %shard_map.104 = (bf16[32,8,2,16,128]{4,3,2,1,0:T(8,128)(2,1)S(1)}, f32[8,4,128]{2,1,0:T(4,128)S(1)}, f32[8,2,16,128]{3,2,1,0:T(8,128)S(1)}) custom-call(s32[4]{0:T(128)S(1)} %pad_add_fusion.place_ref, bf16[8,1040,128]{2,1,0:T(8,128)(2,1)S(1)} %all-to-all-done.got_ref, bf16[2,1152,128]{2,1,0:T(8,128)(2,1)S(1)} %copy-done.3), custom_call_target="tpu_custom_call" | custom-call | flops 4831838208 | bytes 4194304 | tf_op jit(solution)/shard_map/pallas_call | solution.py:450
  43.8 2.5 %collective-permute-start = (f32[8,2,16,128]{3,2,1,0:T(8,128)S(1)}, f32[8,2,16,128]{3,2,1,0:T(8,128)S(1)}, u32[]{:S(2)}, u32[]{:S(2)}) collective-permute-start(f32[8,2,16,128]{3,2,1,0:T(8,128)S(1)} %get-tuple-element.13), channel_id=1, source_target_pairs={{0,96},{32,64},{64,32},{96,0},{1,97},{33,65},{65,33},{97,1},{2,98}... | collective-permute-start | bytes 393224 | tf_op jit(solution)/shard_map/ppermute | solution.py:379
  46.4 3.0 %collective-permute-done.income_ref = f32[8,2,16,128]{3,2,1,0:T(8,128)S(1)} collective-permute-done((f32[8,2,16,128]{3,2,1,0:T(8,128)S(1)}, f32[8,2,16,128]{3,2,1,0:T(8,128)S(1)}, u32[]{:S(2)}, u32[]{:S(2)}) %collective-permute-start) | collective-permute-done | bytes 131104 | tf_op jit(solution)/shard_map/ppermute | solution.py:379
  49.4 6.5 %shard_map.105 = (bf16[32,8,2,16,128]{4,3,2,1,0:T(8,128)(2,1)S(1)}, f32[32,8,2,16,128]{4,3,2,1,0:T(8,128)S(1)}, f32[1,128]{1,0:T(1,128)S(1)}) custom-call(s32[4]{0:T(128)S(1)} %pad_add_fusion.place_ref, bf16[32,8,2,16,128]{4,3,2,1,0:T(8,128)(2,1)S(1)} %get-tuple-element.11.inputs_ref, f32[8,4,128]{2,1,0:T(4,128)S(1)} %get-tuple-element.12.decays_ref, ...), custom_call_target="tpu_custom_call" | custom-call | flops 4831838208 | bytes 4194304 | tf_op jit(solution)/shard_map/pallas_call | solution.py:458
  55.9 1.9 %copy-done.7 = f32[32,8,2,16,128]{4,3,2,1,0:T(8,128)} copy-done((f32[32,8,2,16,128]{4,3,2,1,0:T(8,128)}, f32[32,8,2,16,128]{4,3,2,1,0:T(8,128)S(1)}, u32[]{:S(2)}) %copy-start.7) | copy-done | bytes 4194328
  57.9 1.6 %collective-permute-start.1 = (f32[128]{0:T(128)S(1)}, f32[128]{0:T(128)S(1)}, u32[]{:S(2)}, u32[]{:S(2)}) collective-permute-start(f32[128]{0:T(128)S(1)} %bitcast.119), channel_id=1, source_target_pairs={{0,1},{1,0},{2,3},{3,2},{4,5},{5,4},{6,7},{7,6},{8,9},{9,8},{10,11... | collective-permute-start | bytes 1544 | tf_op jit(solution)/shard_map/ppermute | solution.py:297
  61.0 9.4 %all-to-all-start.1 = ((f32[64,2,128]{2,1,0:T(2,128)}), f32[64,2,128]{2,1,0:T(2,128)S(1)}, u32[]{:S(2)}, u32[]{:S(2)}) async-start(f32[64,2,128]{2,1,0:T(2,128)} %broadcast_in_dim.6), calls=%async_computation.1 | async-start | bytes 131072 | tf_op jit(solution)/shard_map/all_to_all | solution.py:308
  70.4 8.4 %all-to-all-done.1 = f32[64,2,128]{2,1,0:T(2,128)S(1)} async-done(((f32[64,2,128]{2,1,0:T(2,128)}), f32[64,2,128]{2,1,0:T(2,128)S(1)}, u32[]{:S(2)}, u32[]{:S(2)}) %all-to-all-start.1) | async-done | bytes 65568 | tf_op jit(solution)/shard_map/all_to_all | solution.py:308
  80.0 5.1 %fusion.58 = (f32[2,2048]{1,0:T(2,128)S(1)}, f32[2,32,2048]{2,1,0:T(8,128)S(1)}) fusion(bf16[2048,2048]{1,0:T(8,128)(2,1)} %param.17, f32[2,32,2048]{2,1,0:T(8,128)S(1)} %get-tuple-element.29), kind=kOutput, calls=%fused_computation.116 | convolution fusion | flops 537260032 | bytes 9453568 | tf_op jit(solution)/shard_map/dot_general | solution.py:353
  86.0 2.6 %fusion.2 = f32[32,2048]{1,0:T(8,128)S(1)} fusion(bf16[2048,2048]{1,0:T(8,128)(2,1)S(1)} %bitcast.123, f32[2,32,2048]{2,1,0:T(8,128)S(1)} %get-tuple-element.29, f32[32,2048]{1,0:T(8,128)S(1)} %get-tuple-element.45, f32[2048]{0:T(1024)S(1)} %copy-done.11, f32[2048]{0:T(1024)S(1)} %bitcast.131, f32[2048]{0:T(1024)S(1)} %get-tuple-element.48, ...), kind=kOutput, calls=%fused_computation.3 | convolution fusion | flops 269090816 | bytes 9995264 | tf_op jit(solution)/shard_map/dot_general | solution.py:369
  89.6 6.0 %shard_map.106 = (bf16[32,8,2,16,128]{4,3,2,1,0:T(8,128)(2,1)S(1)}, f32[32,8,2,16,128]{4,3,2,1,0:T(8,128)S(1)}, f32[8,2,16,128]{3,2,1,0:T(8,128)S(1)}) custom-call(s32[4]{0:T(128)S(1)} %pad_add_fusion.place_ref, f32[32,8,2,16,128]{4,3,2,1,0:T(8,128)S(1)} %copy-done.8, f32[8,4,128]{2,1,0:T(4,128)S(1)} %get-tuple-element.12.decays_ref, ...), custom_call_target="tpu_custom_call" | custom-call | flops 4831838208 | bytes 4194304 | tf_op jit(solution)/shard_map/pallas_call | solution.py:475
  96.7 6.7 %shard_map.108 = f32[1152,128]{1,0:T(8,128)S(1)} custom-call(s32[4]{0:T(128)S(1)} %pad_add_fusion.place_ref, bf16[32,8,2,16,128]{4,3,2,1,0:T(8,128)(2,1)S(1)} %copy-done.10, bf16[32,8,2,16,128]{4,3,2,1,0:T(8,128)(2,1)S(1)} %get-tuple-element.19.dmix_ref), custom_call_target="tpu_custom_call" | custom-call | flops 4831838208 | bytes 4194304 | tf_op jit(solution)/shard_map/pallas_call | solution.py:483
  103.4 7.9 %shard_map.107 = f32[1152,128]{1,0:T(8,128)S(1)} custom-call(s32[4]{0:T(128)S(1)} %pad_add_fusion.place_ref, bf16[8,1040,128]{2,1,0:T(8,128)(2,1)S(1)} %copy-done.2, f32[32,8,2,16,128]{4,3,2,1,0:T(8,128)S(1)} %copy-done.8, f32[32,8,2,16,128]{4,3,2,1,0:T(8,128)S(1)} %get-tuple-element.16.source_ref, f32[8,4,128]{2,1,0:T(4,128)S(1)} %get-tuple-element.12.decays_ref, ...), custom_call_target="tpu_custom_call" | custom-call | flops 4831838208 | bytes 4194304 | tf_op jit(solution)/shard_map/pallas_call | solution.py:490
  112.2 2.0 %collective-permute-start.3 = (f32[2,4,144,128]{3,2,0,1:T(8,128)}, f32[2,4,144,128]{3,2,0,1:T(8,128)S(1)}, u32[]{:S(2)}, u32[]{:S(2)}) collective-permute-start(f32[2,4,144,128]{3,2,0,1:T(8,128)} %fusion.9), channel_id=1, source_target_pairs={{0,1},{1,0},{2,3},{3,2},{4,5},{5,4},{6,7},{7,6},{8,9},{9,8},{10,11... | collective-permute-start | bytes 1769480 | tf_op jit(solution)/shard_map/ppermute | solution.py:297
  114.2 1.8 %collective-permute-done.3 = f32[2,4,144,128]{3,2,0,1:T(8,128)S(1)} collective-permute-done((f32[2,4,144,128]{3,2,0,1:T(8,128)}, f32[2,4,144,128]{3,2,0,1:T(8,128)S(1)}, u32[]{:S(2)}, u32[]{:S(2)}) %collective-permute-start.3) | collective-permute-done | bytes 589856 | tf_op jit(solution)/shard_map/ppermute | solution.py:297
  116.5 1.9 %collective-permute-start.5 = (bf16[2,144,128]{2,1,0:T(8,128)(2,1)S(1)}, bf16[2,144,128]{2,1,0:T(8,128)(2,1)S(1)}, u32[]{:S(2)}, u32[]{:S(2)}) collective-permute-start(bf16[2,144,128]{2,1,0:T(8,128)(2,1)S(1)} %get-tuple-element.35), channel_id=1, source_target_pairs={{0,4},{2,6},{4,0},{6,2},{1,5},{3,7},{5,1},{7,3},{8,12},{10,14},{12... | collective-permute-start | bytes 221192 | tf_op jit(solution)/shard_map/ppermute | solution.py:383
  118.4 1.7 %collective-permute-start.6 = (bf16[2,144,128]{2,1,0:T(8,128)(2,1)S(1)}, bf16[2,144,128]{2,1,0:T(8,128)(2,1)S(1)}, u32[]{:S(2)}, u32[]{:S(2)}) collective-permute-start(bf16[2,144,128]{2,1,0:T(8,128)(2,1)S(1)} %get-tuple-element.34), channel_id=1, source_target_pairs={{0,6},{2,4},{4,2},{6,0},{1,7},{3,5},{5,3},{7,1},{8,14},{10,12},{12... | collective-permute-start | bytes 221192 | tf_op jit(solution)/shard_map/ppermute | solution.py:383
  120.1 2.2 %collective-permute-done.5 = bf16[2,144,128]{2,1,0:T(8,128)(2,1)S(1)} collective-permute-done((bf16[2,144,128]{2,1,0:T(8,128)(2,1)S(1)}, bf16[2,144,128]{2,1,0:T(8,128)(2,1)S(1)}, u32[]{:S(2)}, u32[]{:S(2)}) %collective-permute-start.5) | collective-permute-done | bytes 73760 | tf_op jit(solution)/shard_map/ppermute | solution.py:383
  123.8 1.8 %collective-permute-start.8 = (bf16[2,144,128]{2,1,0:T(8,128)(2,1)S(1)}, bf16[2,144,128]{2,1,0:T(8,128)(2,1)S(1)}, u32[]{:S(2)}, u32[]{:S(2)}) collective-permute-start(bf16[2,144,128]{2,1,0:T(8,128)(2,1)S(1)} %fusion.22), channel_id=1, source_target_pairs={{0,16},{8,24},{16,0},{24,8},{1,17},{9,25},{17,1},{25,9},{2,18},{10... | collective-permute-start | bytes 221192 | tf_op jit(solution)/shard_map/ppermute | solution.py:383
  125.6 1.7 %collective-permute-start.9 = (bf16[2,144,128]{2,1,0:T(8,128)(2,1)S(1)}, bf16[2,144,128]{2,1,0:T(8,128)(2,1)S(1)}, u32[]{:S(2)}, u32[]{:S(2)}) collective-permute-start(bf16[2,144,128]{2,1,0:T(8,128)(2,1)S(1)} %fusion.22), channel_id=1, source_target_pairs={{0,24},{8,16},{16,8},{24,0},{1,25},{9,17},{17,9},{25,1},{2,26},{10... | collective-permute-start | bytes 221192 | tf_op jit(solution)/shard_map/ppermute | solution.py:383
  130.1 2.3 %collective-permute-start.10 = (bf16[2,144,128]{2,1,0:T(8,128)(2,1)S(1)}, bf16[2,144,128]{2,1,0:T(8,128)(2,1)S(1)}, u32[]{:S(2)}, u32[]{:S(2)}) collective-permute-start(bf16[2,144,128]{2,1,0:T(8,128)(2,1)S(1)} %add_convert_fusion.2), channel_id=1, source_target_pairs={{0,96},{32,64},{64,32},{96,0},{1,97},{33,65},{65,33},{97,1},{2,98}... | collective-permute-start | bytes 221192 | tf_op jit(solution)/shard_map/ppermute | solution.py:383
  132.4 1.6 %collective-permute-start.12 = (bf16[2,144,128]{2,1,0:T(8,128)(2,1)S(1)}, bf16[2,144,128]{2,1,0:T(8,128)(2,1)S(1)}, u32[]{:S(2)}, u32[]{:S(2)}) collective-permute-start(bf16[2,144,128]{2,1,0:T(8,128)(2,1)S(1)} %add_convert_fusion.2), channel_id=1, source_target_pairs={{0,64},{32,96},{64,0},{96,32},{1,65},{33,97},{65,1},{97,33},{2,66}... | collective-permute-start | bytes 221192 | tf_op jit(solution)/shard_map/ppermute | solution.py:383
  135.6 1.5 collective-permute-done.12
  137.2 2.5 %collective-permute-start.14 = (bf16[2,2,144,128]{3,2,1,0:T(8,128)(2,1)S(1)}, bf16[2,2,144,128]{3,2,1,0:T(8,128)(2,1)S(1)}, u32[]{:S(2)}, u32[]{:S(2)}) collective-permute-start(bf16[2,2,144,128]{3,2,1,0:T(8,128)(2,1)S(1)} %pad_maximum_fusion.1.refs_0_), channel_id=1, source_target_pairs={{0,4},{2,6},{4,0},{6,2},{1,5},{3,7},{5,1},{7,3},{8,12},{10,14},{12... | collective-permute-start | bytes 442376 | tf_op jit(solution)/shard_map/ppermute | solution.py:383
  141.1 5.2 %collective-permute-start.16 = (bf16[2,2,144,128]{3,2,1,0:T(8,128)(2,1)S(1)}, bf16[2,2,144,128]{3,2,1,0:T(8,128)(2,1)S(1)}, u32[]{:S(2)}, u32[]{:S(2)}) collective-permute-start(bf16[2,2,144,128]{3,2,1,0:T(8,128)(2,1)S(1)} %pad_maximum_fusion.1.refs_0_), channel_id=1, source_target_pairs={{0,1},{1,0},{2,3},{3,2},{4,5},{5,4},{6,7},{7,6},{8,9},{9,8},{10,11... | collective-permute-start | bytes 442376 | tf_op jit(solution)/shard_map/ppermute | solution.py:297
  146.8 3.0 %collective-permute-start.18 = (bf16[2,2,144,128]{3,2,1,0:T(8,128)(2,1)S(1)}, bf16[2,2,144,128]{3,2,1,0:T(8,128)(2,1)S(1)}, u32[]{:S(2)}, u32[]{:S(2)}) collective-permute-start(bf16[2,2,144,128]{3,2,1,0:T(8,128)(2,1)S(1)} %collective-permute-done.14.refs_2_), channel_id=1, source_target_pairs={{0,1},{1,0},{2,3},{3,2},{4,5},{5,4},{6,7},{7,6},{8,9},{9,8},{10,11... | collective-permute-start | bytes 442376 | tf_op jit(solution)/shard_map/ppermute | solution.py:297
  149.7 1.7 %collective-permute-start.19 = (bf16[2,2,144,128]{3,2,1,0:T(8,128)(2,1)S(1)}, bf16[2,2,144,128]{3,2,1,0:T(8,128)(2,1)S(1)}, u32[]{:S(2)}, u32[]{:S(2)}) collective-permute-start(bf16[2,2,144,128]{3,2,1,0:T(8,128)(2,1)S(1)} %collective-permute-done.15.refs_3_), channel_id=1, source_target_pairs={{0,1},{1,0},{2,3},{3,2},{4,5},{5,4},{6,7},{7,6},{8,9},{9,8},{10,11... | collective-permute-start | bytes 442376 | tf_op jit(solution)/shard_map/ppermute | solution.py:297
  152.4 2.1 %shard_map.109 = (f32[2,1152,128]{2,1,0:T(8,128)}, f32[2,1152,128]{2,1,0:T(8,128)}) custom-call(s32[4]{0:T(128)S(1)} %pad_add_fusion.place_ref, bf16[2,2,144,128]{3,2,1,0:T(8,128)(2,1)S(1)} %pad_maximum_fusion.1.refs_0_, bf16[2,2,144,128]{3,2,1,0:T(8,128)(2,1)S(1)} %collective-permute-done.13.refs_1_, ...), custom_call_target="tpu_custom_call" | custom-call | tf_op jit(solution)/shard_map/pallas_call | solution.py:422
  (90 shorter events, 17.4 us)
Async XLA Ops:
  0.6 78.3 %copy-start = (f32[128,2048]{1,0:T(8,128)S(1)}, f32[128,2048]{1,0:T(8,128)}, u32[]{:S(2)}) copy-start(f32[128,2048]{1,0:T(8,128)} %param.15) | copy-start | bytes 3145732
  4.7 32.5 %all-to-all-start = ((bf16[8,1040,128]{2,1,0:T(8,128)(2,1)}), bf16[8,1040,128]{2,1,0:T(8,128)(2,1)S(1)}, u32[]{:S(2)}, u32[]{:S(2)}) async-start(bf16[8,1040,128]{2,1,0:T(8,128)(2,1)} %bitcast.124), calls=%async_computation | async-start | bytes 4259840 | tf_op jit(solution)/shard_map/all_to_all | solution.py:328
  38.2 5.6 %copy-start.1 = (bf16[8,1040,128]{2,1,0:T(8,128)(2,1)}, bf16[8,1040,128]{2,1,0:T(8,128)(2,1)S(1)}, u32[]{:S(2)}) copy-start(bf16[8,1040,128]{2,1,0:T(8,128)(2,1)S(1)} %all-to-all-done.got_ref) | copy-start | bytes 6389764
  38.2 11.2 %copy-start.4 = (bf16[2,1152,128]{2,1,0:T(8,128)(2,1)S(1)}, bf16[2,1152,128]{2,1,0:T(8,128)(2,1)}, u32[]{:S(2)}) copy-start(bf16[2,1152,128]{2,1,0:T(8,128)(2,1)} %weights_ref.5) | copy-start | bytes 1769476
  38.2 11.2 %copy-start.6 = (f32[2,128]{1,0:T(2,128)S(1)}, f32[2,128]{1,0:T(2,128)}, u32[]{:S(2)}) copy-start(f32[2,128]{1,0:T(2,128)} %param.14) | copy-start | bytes 3076
  43.8 5.6 %collective-permute-start = (f32[8,2,16,128]{3,2,1,0:T(8,128)S(1)}, f32[8,2,16,128]{3,2,1,0:T(8,128)S(1)}, u32[]{:S(2)}, u32[]{:S(2)}) collective-permute-start(f32[8,2,16,128]{3,2,1,0:T(8,128)S(1)} %get-tuple-element.13), channel_id=1, source_target_pairs={{0,96},{32,64},{64,32},{96,0},{1,97},{33,65},{65,33},{97,1},{2,98}... | collective-permute-start | bytes 393224 | tf_op jit(solution)/shard_map/ppermute | solution.py:379
  57.9 22.1 %copy-start.9 = (bf16[32,8,2,16,128]{4,3,2,1,0:T(8,128)(2,1)}, bf16[32,8,2,16,128]{4,3,2,1,0:T(8,128)(2,1)S(1)}, u32[]{:S(2)}) copy-start(bf16[32,8,2,16,128]{4,3,2,1,0:T(8,128)(2,1)S(1)} %get-tuple-element.18.states_ref) | copy-start | bytes 6291460
  57.9 21.9 %copy-start.11 = (f32[2048]{0:T(1024)S(1)}, f32[2048]{0:T(1024)}, u32[]{:S(2)}) copy-start(f32[2048]{0:T(1024)} %param.16) | copy-start | bytes 24580
  57.9 2.5 %collective-permute-start.1 = (f32[128]{0:T(128)S(1)}, f32[128]{0:T(128)S(1)}, u32[]{:S(2)}, u32[]{:S(2)}) collective-permute-start(f32[128]{0:T(128)S(1)} %bitcast.119), channel_id=1, source_target_pairs={{0,1},{1,0},{2,3},{3,2},{4,5},{5,4},{6,7},{7,6},{8,9},{9,8},{10,11... | collective-permute-start | bytes 1544 | tf_op jit(solution)/shard_map/ppermute | solution.py:297
  61.0 17.9 %all-to-all-start.1 = ((f32[64,2,128]{2,1,0:T(2,128)}), f32[64,2,128]{2,1,0:T(2,128)S(1)}, u32[]{:S(2)}, u32[]{:S(2)}) async-start(f32[64,2,128]{2,1,0:T(2,128)} %broadcast_in_dim.6), calls=%async_computation.1 | async-start | bytes 131072 | tf_op jit(solution)/shard_map/all_to_all | solution.py:308
  79.9 6.0 %slice-start = ((s8[8388608]{0:T(1024)(128)(4,1)}), s8[4194304]{0:T(1024)(128)(4,1)S(1)}, s32[]{:S(2)}) async-start(s8[8388608]{0:T(1024)(128)(4,1)} %bitcast.122), calls=%async_computation.2 | async-start | bytes 8388608
  79.9 6.0 %slice-start.1 = ((s8[8388608]{0:T(1024)(128)(4,1)}), s8[4194304]{0:T(1024)(128)(4,1)S(1)}, s32[]{:S(2)}) async-start(s8[8388608]{0:T(1024)(128)(4,1)} %bitcast.122), calls=%async_computation.3 | async-start | bytes 8388608
  89.6 7.0 %copy-start.10 = (bf16[32,8,2,16,128]{4,3,2,1,0:T(8,128)(2,1)S(1)}, bf16[32,8,2,16,128]{4,3,2,1,0:T(8,128)(2,1)}, u32[]{:S(2)}) copy-start(bf16[32,8,2,16,128]{4,3,2,1,0:T(8,128)(2,1)} %copy-done.9) | copy-start | bytes 6291460
  95.7 7.8 %collective-permute-start.2 = (f32[8,2,16,128]{3,2,1,0:T(8,128)S(1)}, f32[8,2,16,128]{3,2,1,0:T(8,128)S(1)}, u32[]{:S(2)}, u32[]{:S(2)}) collective-permute-start(f32[8,2,16,128]{3,2,1,0:T(8,128)S(1)} %get-tuple-element.17), channel_id=1, source_target_pairs={{0,96},{32,64},{64,32},{96,0},{1,97},{33,65},{65,33},{97,1},{2,98}... | collective-permute-start | bytes 393224 | tf_op jit(solution)/shard_map/ppermute | solution.py:379
  96.7 6.8 %copy-start.2 = (bf16[8,1040,128]{2,1,0:T(8,128)(2,1)S(1)}, bf16[8,1040,128]{2,1,0:T(8,128)(2,1)}, u32[]{:S(2)}) copy-start(bf16[8,1040,128]{2,1,0:T(8,128)(2,1)} %copy-done.1) | copy-start | bytes 6389764
  112.2 3.8 %collective-permute-start.3 = (f32[2,4,144,128]{3,2,0,1:T(8,128)}, f32[2,4,144,128]{3,2,0,1:T(8,128)S(1)}, u32[]{:S(2)}, u32[]{:S(2)}) collective-permute-start(f32[2,4,144,128]{3,2,0,1:T(8,128)} %fusion.9), channel_id=1, source_target_pairs={{0,1},{1,0},{2,3},{3,2},{4,5},{5,4},{6,7},{7,6},{8,9},{9,8},{10,11... | collective-permute-start | bytes 1769480 | tf_op jit(solution)/shard_map/ppermute | solution.py:297
  116.2 3.9 %collective-permute-start.4 = (bf16[2,144,128]{2,1,0:T(8,128)(2,1)S(1)}, bf16[2,144,128]{2,1,0:T(8,128)(2,1)S(1)}, u32[]{:S(2)}, u32[]{:S(2)}) collective-permute-start(bf16[2,144,128]{2,1,0:T(8,128)(2,1)S(1)} %get-tuple-element.33), channel_id=1, source_target_pairs={{0,2},{2,0},{4,6},{6,4},{1,3},{3,1},{5,7},{7,5},{8,10},{10,8},{12,... | collective-permute-start | bytes 221192 | tf_op jit(solution)/shard_map/ppermute | solution.py:383
  116.5 5.7 %collective-permute-start.5 = (bf16[2,144,128]{2,1,0:T(8,128)(2,1)S(1)}, bf16[2,144,128]{2,1,0:T(8,128)(2,1)S(1)}, u32[]{:S(2)}, u32[]{:S(2)}) collective-permute-start(bf16[2,144,128]{2,1,0:T(8,128)(2,1)S(1)} %get-tuple-element.35), channel_id=1, source_target_pairs={{0,4},{2,6},{4,0},{6,2},{1,5},{3,7},{5,1},{7,3},{8,12},{10,14},{12... | collective-permute-start | bytes 221192 | tf_op jit(solution)/shard_map/ppermute | solution.py:383
  118.4 4.9 %collective-permute-start.6 = (bf16[2,144,128]{2,1,0:T(8,128)(2,1)S(1)}, bf16[2,144,128]{2,1,0:T(8,128)(2,1)S(1)}, u32[]{:S(2)}, u32[]{:S(2)}) collective-permute-start(bf16[2,144,128]{2,1,0:T(8,128)(2,1)S(1)} %get-tuple-element.34), channel_id=1, source_target_pairs={{0,6},{2,4},{4,2},{6,0},{1,7},{3,5},{5,3},{7,1},{8,14},{10,12},{12... | collective-permute-start | bytes 221192 | tf_op jit(solution)/shard_map/ppermute | solution.py:383
  123.4 3.9 %collective-permute-start.7 = (bf16[2,144,128]{2,1,0:T(8,128)(2,1)S(1)}, bf16[2,144,128]{2,1,0:T(8,128)(2,1)S(1)}, u32[]{:S(2)}, u32[]{:S(2)}) collective-permute-start(bf16[2,144,128]{2,1,0:T(8,128)(2,1)S(1)} %fusion.22), channel_id=1, source_target_pairs={{0,8},{8,0},{16,24},{24,16},{1,9},{9,1},{17,25},{25,17},{2,10},{10... | collective-permute-start | bytes 221192 | tf_op jit(solution)/shard_map/ppermute | solution.py:383
  123.8 4.7 %collective-permute-start.8 = (bf16[2,144,128]{2,1,0:T(8,128)(2,1)S(1)}, bf16[2,144,128]{2,1,0:T(8,128)(2,1)S(1)}, u32[]{:S(2)}, u32[]{:S(2)}) collective-permute-start(bf16[2,144,128]{2,1,0:T(8,128)(2,1)S(1)} %fusion.22), channel_id=1, source_target_pairs={{0,16},{8,24},{16,0},{24,8},{1,17},{9,25},{17,1},{25,9},{2,18},{10... | collective-permute-start | bytes 221192 | tf_op jit(solution)/shard_map/ppermute | solution.py:383
  125.6 4.4 %collective-permute-start.9 = (bf16[2,144,128]{2,1,0:T(8,128)(2,1)S(1)}, bf16[2,144,128]{2,1,0:T(8,128)(2,1)S(1)}, u32[]{:S(2)}, u32[]{:S(2)}) collective-permute-start(bf16[2,144,128]{2,1,0:T(8,128)(2,1)S(1)} %fusion.22), channel_id=1, source_target_pairs={{0,24},{8,16},{16,8},{24,0},{1,25},{9,17},{17,9},{25,1},{2,26},{10... | collective-permute-start | bytes 221192 | tf_op jit(solution)/shard_map/ppermute | solution.py:383
  130.1 4.5 %collective-permute-start.10 = (bf16[2,144,128]{2,1,0:T(8,128)(2,1)S(1)}, bf16[2,144,128]{2,1,0:T(8,128)(2,1)S(1)}, u32[]{:S(2)}, u32[]{:S(2)}) collective-permute-start(bf16[2,144,128]{2,1,0:T(8,128)(2,1)S(1)} %add_convert_fusion.2), channel_id=1, source_target_pairs={{0,96},{32,64},{64,32},{96,0},{1,97},{33,65},{65,33},{97,1},{2,98}... | collective-permute-start | bytes 221192 | tf_op jit(solution)/shard_map/ppermute | solution.py:383
  132.4 3.2 %collective-permute-start.11 = (bf16[2,144,128]{2,1,0:T(8,128)(2,1)S(1)}, bf16[2,144,128]{2,1,0:T(8,128)(2,1)S(1)}, u32[]{:S(2)}, u32[]{:S(2)}) collective-permute-start(bf16[2,144,128]{2,1,0:T(8,128)(2,1)S(1)} %add_convert_fusion.2), channel_id=1, source_target_pairs={{0,32},{32,0},{64,96},{96,64},{1,33},{33,1},{65,97},{97,65},{2,34}... | collective-permute-start | bytes 221192 | tf_op jit(solution)/shard_map/ppermute | solution.py:383
  132.4 4.7 %collective-permute-start.12 = (bf16[2,144,128]{2,1,0:T(8,128)(2,1)S(1)}, bf16[2,144,128]{2,1,0:T(8,128)(2,1)S(1)}, u32[]{:S(2)}, u32[]{:S(2)}) collective-permute-start(bf16[2,144,128]{2,1,0:T(8,128)(2,1)S(1)} %add_convert_fusion.2), channel_id=1, source_target_pairs={{0,64},{32,96},{64,0},{96,32},{1,65},{33,97},{65,1},{97,33},{2,66}... | collective-permute-start | bytes 221192 | tf_op jit(solution)/shard_map/ppermute | solution.py:383
  137.1 9.2 %collective-permute-start.13 = (bf16[2,2,144,128]{3,2,1,0:T(8,128)(2,1)S(1)}, bf16[2,2,144,128]{3,2,1,0:T(8,128)(2,1)S(1)}, u32[]{:S(2)}, u32[]{:S(2)}) collective-permute-start(bf16[2,2,144,128]{3,2,1,0:T(8,128)(2,1)S(1)} %pad_maximum_fusion.1.refs_0_), channel_id=1, source_target_pairs={{0,2},{2,0},{4,6},{6,4},{1,3},{3,1},{5,7},{7,5},{8,10},{10,8},{12,... | collective-permute-start | bytes 442376 | tf_op jit(solution)/shard_map/ppermute | solution.py:383
  137.2 9.5 %collective-permute-start.14 = (bf16[2,2,144,128]{3,2,1,0:T(8,128)(2,1)S(1)}, bf16[2,2,144,128]{3,2,1,0:T(8,128)(2,1)S(1)}, u32[]{:S(2)}, u32[]{:S(2)}) collective-permute-start(bf16[2,2,144,128]{3,2,1,0:T(8,128)(2,1)S(1)} %pad_maximum_fusion.1.refs_0_), channel_id=1, source_target_pairs={{0,4},{2,6},{4,0},{6,2},{1,5},{3,7},{5,1},{7,3},{8,12},{10,14},{12... | collective-permute-start | bytes 442376 | tf_op jit(solution)/shard_map/ppermute | solution.py:383
  139.7 10.0 %collective-permute-start.15 = (bf16[2,2,144,128]{3,2,1,0:T(8,128)(2,1)S(1)}, bf16[2,2,144,128]{3,2,1,0:T(8,128)(2,1)S(1)}, u32[]{:S(2)}, u32[]{:S(2)}) collective-permute-start(bf16[2,2,144,128]{3,2,1,0:T(8,128)(2,1)S(1)} %pad_maximum_fusion.1.refs_0_), channel_id=1, source_target_pairs={{0,6},{2,4},{4,2},{6,0},{1,7},{3,5},{5,3},{7,1},{8,14},{10,12},{12... | collective-permute-start | bytes 442376 | tf_op jit(solution)/shard_map/ppermute | solution.py:383
  141.1 10.3 %collective-permute-start.16 = (bf16[2,2,144,128]{3,2,1,0:T(8,128)(2,1)S(1)}, bf16[2,2,144,128]{3,2,1,0:T(8,128)(2,1)S(1)}, u32[]{:S(2)}, u32[]{:S(2)}) collective-permute-start(bf16[2,2,144,128]{3,2,1,0:T(8,128)(2,1)S(1)} %pad_maximum_fusion.1.refs_0_), channel_id=1, source_target_pairs={{0,1},{1,0},{2,3},{3,2},{4,5},{5,4},{6,7},{7,6},{8,9},{9,8},{10,11... | collective-permute-start | bytes 442376 | tf_op jit(solution)/shard_map/ppermute | solution.py:297
  146.3 5.1 %collective-permute-start.17 = (bf16[2,2,144,128]{3,2,1,0:T(8,128)(2,1)S(1)}, bf16[2,2,144,128]{3,2,1,0:T(8,128)(2,1)S(1)}, u32[]{:S(2)}, u32[]{:S(2)}) collective-permute-start(bf16[2,2,144,128]{3,2,1,0:T(8,128)(2,1)S(1)} %collective-permute-done.13.refs_1_), channel_id=1, source_target_pairs={{0,1},{1,0},{2,3},{3,2},{4,5},{5,4},{6,7},{7,6},{8,9},{9,8},{10,11... | collective-permute-start | bytes 442376 | tf_op jit(solution)/shard_map/ppermute | solution.py:297
  146.8 4.6 %collective-permute-start.18 = (bf16[2,2,144,128]{3,2,1,0:T(8,128)(2,1)S(1)}, bf16[2,2,144,128]{3,2,1,0:T(8,128)(2,1)S(1)}, u32[]{:S(2)}, u32[]{:S(2)}) collective-permute-start(bf16[2,2,144,128]{3,2,1,0:T(8,128)(2,1)S(1)} %collective-permute-done.14.refs_2_), channel_id=1, source_target_pairs={{0,1},{1,0},{2,3},{3,2},{4,5},{5,4},{6,7},{7,6},{8,9},{9,8},{10,11... | collective-permute-start | bytes 442376 | tf_op jit(solution)/shard_map/ppermute | solution.py:297
  149.7 2.7 %collective-permute-start.19 = (bf16[2,2,144,128]{3,2,1,0:T(8,128)(2,1)S(1)}, bf16[2,2,144,128]{3,2,1,0:T(8,128)(2,1)S(1)}, u32[]{:S(2)}, u32[]{:S(2)}) collective-permute-start(bf16[2,2,144,128]{3,2,1,0:T(8,128)(2,1)S(1)} %collective-permute-done.15.refs_3_), channel_id=1, source_target_pairs={{0,1},{1,0},{2,3},{3,2},{4,5},{5,4},{6,7},{7,6},{8,9},{9,8},{10,11... | collective-permute-start | bytes 442376 | tf_op jit(solution)/shard_map/ppermute | solution.py:297
  (4 other events, 7.7 us)

commit v2 on v1

--- a/solution.py
+++ b/solution.py
@@ -1,3 +1,5 @@
+import functools
+
 import jax
 import jax.numpy as jnp
 from jax import lax
@@ -329,9 +331,8 @@
 
 
 def batch_norm(values):
-    center = jnp.mean(values, axis=1, keepdims=True)
-    centered = values - center
-    scale = lax.rsqrt(jnp.mean(centered * centered, axis=1, keepdims=True) + EPSILON)
+    centered = values - jnp.mean(values, axis=0, keepdims=True)
+    scale = lax.rsqrt(jnp.mean(centered * centered, axis=0, keepdims=True) + EPSILON)
     return centered * scale, scale
 
 
@@ -341,38 +342,56 @@
     return (grad - mean - normed * along) * scale
 
 
-def projector_back(pooled, proj_in, proj_gain, proj_out, view):
-    _, clips, channels = pooled.shape
+def across(a, b, **kinds):
+    return lax.dot_general(a, b, (((1,), (1,)), ((), ())), preferred_element_type=F32, **kinds)
+
+
+def projector_kernel(place_ref, seen_ref, in_ref, gain_ref, out_ref, dpool_ref, x_ref, n_ref, z_ref, zn_ref, *, cell_count):
+    view, row = place_ref[1], place_ref[4]
+    clips = seen_ref.shape[1]
+    gain = gain_ref[...]
+    pooled = jnp.concatenate([seen_ref[0] + seen_ref[3], seen_ref[1] + seen_ref[2]]) / cell_count
+    hidden = jnp.dot(pooled, in_ref[...], precision=HIGHEST, preferred_element_type=F32)
+    hidden_s, relus = [], []
+    for v in range(2):
+        x_ref[v], scale = batch_norm(hidden[v * clips : (v + 1) * clips])
+        n_ref[v] = x_ref[v] * gain
+        hidden_s.append(scale)
+        relus.append(jnp.maximum(n_ref[v], 0.0).astype(BF16))
+    z = jnp.dot(jnp.concatenate(relus), out_ref[...], preferred_element_type=F32)
+    z_s = []
+    for v in range(2):
+        z_ref[v], scale = batch_norm(z[v * clips : (v + 1) * clips])
+        zn_ref[v] = z_ref[v].astype(BF16)
+        z_s.append(scale)
+    first = view == 0
+    own, other = zn_ref[view].astype(F32), zn_ref[1 - view].astype(F32)
+    corr_diag = jnp.sum(own * other, axis=0, keepdims=True) / clips
+    extra = -2.0 * (1.0 - corr_diag) - 2.0 * LAMBDA_OFF * corr_diag
+    gram = across(zn_ref[1 - view], zn_ref[1 - view])
+    spread = jnp.dot(gram, own, precision=HIGHEST, preferred_element_type=F32)
+    dzn = spread * (2.0 * LAMBDA_OFF / (clips * clips)) + other * (extra / clips)
+    dz_b = norm_back(dzn, z_ref[view], jnp.where(first, z_s[0], z_s[1])).astype(BF16)
+    dxh = jnp.where(n_ref[view] > 0, across(dz_b, out_ref[...]), 0.0) * gain
+    dhidden = norm_back(dxh, x_ref[view], jnp.where(first, hidden_s[0], hidden_s[1]))
+    mine = lax.broadcasted_iota(jnp.int32, dhidden.shape, 0) == row
+    own_row = jnp.sum(jnp.where(mine, dhidden, 0.0), axis=0, keepdims=True)
+    rows = jnp.broadcast_to(own_row, (8, own_row.shape[1]))
+    dpool_ref[...] = across(rows, in_ref[...], precision=HIGHEST)[:1] / cell_count
+
+
+def projector_back(seen, proj_in, proj_gain, proj_out, place, cell_count):
+    _, clips, channels = seen.shape
     width = proj_in.shape[1]
-    hidden = jnp.dot(
-        pooled.reshape(2 * clips, channels), proj_in, precision=HIGHEST, preferred_element_type=jnp.float32
-    )
-    hidden_x, hidden_s = batch_norm(hidden.reshape(2, clips, width))
-    hidden_n = hidden_x * proj_gain
-    relu_b = jnp.maximum(hidden_n, 0.0).astype(jnp.bfloat16)
-    z = jnp.dot(relu_b.reshape(2 * clips, width), proj_out, preferred_element_type=jnp.float32)
-    z_x, z_s = batch_norm(z.reshape(2, clips, width))
-    zn = z_x.astype(jnp.bfloat16)
-    first = view == 0
-    own = jnp.where(first, zn[0], zn[1])
-    other = jnp.where(first, zn[1], zn[0])
-    own_wide = own.astype(jnp.float32)
-    other_wide = other.astype(jnp.float32)
-    corr_diag = jnp.sum(own_wide * other_wide, axis=0) / clips
-    extra = -2.0 * (1.0 - corr_diag) - 2.0 * LAMBDA_OFF * corr_diag
-    gram = lax.dot_general(other, other, (((1,), (1,)), ((), ())), preferred_element_type=jnp.float32)
-    spread = jnp.dot(gram, own_wide, precision=HIGHEST, preferred_element_type=jnp.float32)
-    dzn = spread * (2.0 * LAMBDA_OFF / (clips * clips)) + other_wide * (extra / clips)
-    dz_b = norm_back(
-        dzn, jnp.where(first, z_x[0], z_x[1]), jnp.where(first, z_s[0], z_s[1])
-    ).astype(jnp.bfloat16)
-    drelu = lax.dot_general(dz_b, proj_out, (((1,), (1,)), ((), ())), preferred_element_type=jnp.float32)
-    own_x = jnp.where(first, hidden_x[0], hidden_x[1])
-    own_s = jnp.where(first, hidden_s[0], hidden_s[1])
-    own_n = jnp.where(first, hidden_n[0], hidden_n[1])
-    dxh = jnp.where(own_n > 0, drelu, 0.0) * proj_gain
-    dhidden = norm_back(dxh, own_x, own_s)
-    return dhidden
+    wide = (2, clips, width)
+    return pl.pallas_call(
+        functools.partial(projector_kernel, cell_count=cell_count),
+        out_shape=jax.ShapeDtypeStruct((1, channels), F32),
+        in_specs=[pl.BlockSpec(memory_space=pltpu.SMEM)] + [pl.BlockSpec(memory_space=pltpu.VMEM)] * 4,
+        scratch_shapes=[pltpu.VMEM(wide, F32), pltpu.VMEM(wide, F32), pltpu.VMEM(wide, F32), pltpu.VMEM(wide, BF16)],
+        cost_estimate=pl.CostEstimate(flops=6 * clips * width * width, transcendentals=0, bytes_accessed=2 * width * width),
+        compiler_params=pltpu.CompilerParams(vmem_limit_bytes=26 << 20),
+    )(place, seen, proj_in, proj_gain.reshape(1, width), proj_out)
 
 
 def from_other_half(x):
@@ -433,9 +452,6 @@
 ):
     half = lax.axis_index("xh")
     view = lax.axis_index("xl") ^ half
-    clip = lax.axis_index("y")
-    batch = lax.axis_index(("z", "core"))
-    clips_here = rgb_maps.shape[0]
     _, frames_here, side, _, channels = rgb_maps.shape
     got = clips_to_devices(rgb_maps, flow_maps, decay, half)
     steps, rows, _ = got.shape
@@ -444,7 +460,8 @@
     taps = in_weights.shape[1]
     weights = plan.of_view(taps)
     skips = skip.reshape(2, 1, channels)
-    place = jnp.stack([half, view, lax.axis_index("core"), lax.axis_index("z")]).astype(jnp.int32)
+    place = jnp.stack([half, view, lax.axis_index("core"), lax.axis_index("z"), lax.axis_index(("y", "z", "core"))])
+    place = place.astype(jnp.int32)
     carry_spec = plan.whole(plan.map)
 
     inputs, decays, end = plan.call(
@@ -464,14 +481,8 @@
     )(place, inputs, decays, income, skips, out_weights)
 
     seen = from_all(from_cores(pooled_part[0]), ("xh", "xl", "y", "z"))
-    seen = seen.reshape(2, 2, clips_here, 4, 2, channels)
-    views = jnp.stack([seen[0, 0] + seen[1, 1], seen[0, 1] + seen[1, 0]]) / cell_count
-    pooled = views.transpose(0, 2, 3, 1, 4).reshape(2, -1, channels)
-    dhidden = projector_back(pooled, proj_in, proj_gain, proj_out, view)
-    own_row = lax.dynamic_slice_in_dim(dhidden, batch * clips_here + clip, 1, 0)
-    dpooled = lax.dot_general(own_row, proj_in, (((1,), (1,)), ((), ())), precision=HIGHEST)
-
-    dpool = dpooled / cell_count
+    dpool = projector_back(seen.reshape(4, -1, channels), proj_in, proj_gain, proj_out, place, cell_count)
+
     dmix_b, source, end = plan.call(
         from_out_kernel,
         [plan.maps(True), plan.decays(True), plan.row(), weights],

time: 155 us -> 153 us (0.987)
  matrix products: 9.8 us -> 0 us
  Pallas kernels: 34.9 us -> 41.4 us
  local copies, waits for them, and re-layouts: 3.81 us -> 7.52 us
    dot_general x6 -> x0, matrix products: 9.8 us -> none  [the longest x1 5.14 us: projector_back(): jnp.dot(relu_b.reshape(2 * clips, width), proj_out, preferred_element_typ...]
    pallas_call x0 -> x1, Pallas kernels: none -> 6.58 us  [projector_back(): pl.pallas_call(functools.partial(projector_kernel, cell_count=cell_count)...]
    unnamed x28 -> x22, local copies, waits for them, and re-layouts: 3.11 us -> 6.76 us
where the time goes in v2:
time: 153 us
  waiting for transfers between devices  50.4 us (33%)
  starting transfers between devices  48.6 us (32%)
  Pallas kernels  41.4 us (27%)
  local copies, waits for them, and re-layouts  7.52 us (5%)
  other arithmetic  4.26 us (3%)
    all_to_all x1, waiting for transfers between devices, clips_to_devices(): return lax.all_to_all(sent, TIME, 0, 0, tiled=True)  26.5 us
    ppermute x12, starting transfers between devices, from_peer(): return lax.ppermute(x, axes, [(i, i ^ k) for i in range(4)])  15.7 us
    ppermute x6, starting transfers between devices, swapped(): return lax.ppermute(x, 'core', [(0, 1), (1, 0)])  14 us
    all_to_all x1, starting transfers between devices, from_all(): lax.all_to_all(jnp.broadcast_to(x[None], (peers, *x.shape)), axes, 0, 0,...  9.41 us
    ppermute x12, waiting for transfers between devices, from_peer(): return lax.ppermute(x, axes, [(i, i ^ k) for i in range(4)])  9 us
    all_to_all x1, waiting for transfers between devices, from_all(): lax.all_to_all(jnp.broadcast_to(x[None], (peers, *x.shape)), axes, 0, 0,...  8.46 us
    pallas_call x1, Pallas kernels, per_device(): plan.call(in_grad_kernel, [plan.got(rows, True), plan.maps(True), plan.ma...  7.9 us
    unnamed x22, local copies, waits for them, and re-layouts  6.76 us
  transfers between devices with their start and end apart: 22, of which 13 were waited for; matrix products, arithmetic and copies ran while one was open for 0% of the time, Pallas kernels for 4%

profile of v2, /device:TPU:1, one launch (start us, length us, event | category | flops | bytes accessed | tf_op | source)
XLA Modules:
  0.0 153.0 jit_solution(13635000838802522889)
XLA Ops:
  1.4 1.7 %broadcast_select_fusion.1 = (bf16[4,4,16,16,128]{4,3,2,1,0:T(8,128)(2,1)S(1)}, bf16[4,4,16,16,128]{4,3,2,1,0:T(8,128)(2,1)S(1)}) fusion(bf16[4,4,16,16,128]{4,3,2,1,0:T(8,128)(2,1)} %param.9, bf16[4,4,16,16,128]{4,3,2,1,0:T(8,128)(2,1)} %param.10, pred[]{:T(512)S(6)} %eq.6), kind=kLoop, calls=%fused_computation.6 | loop fusion | flops 1048576 | bytes 4194305 | tf_op jit(solution)/shard_map/jit(_where)/select_n | solution.py:323
  3.1 1.5 pad_maximum_fusion
  4.6 6.1 %all-to-all-start = ((bf16[8,1040,128]{2,1,0:T(8,128)(2,1)}), bf16[8,1040,128]{2,1,0:T(8,128)(2,1)S(1)}, u32[]{:S(2)}, u32[]{:S(2)}) async-start(bf16[8,1040,128]{2,1,0:T(8,128)(2,1)} %bitcast.56), calls=%async_computation | async-start | bytes 4259840 | tf_op jit(solution)/shard_map/all_to_all | solution.py:330
  10.8 26.5 %all-to-all-done.got_ref = bf16[8,1040,128]{2,1,0:T(8,128)(2,1)S(1)} async-done(((bf16[8,1040,128]{2,1,0:T(8,128)(2,1)}), bf16[8,1040,128]{2,1,0:T(8,128)(2,1)S(1)}, u32[]{:S(2)}, u32[]{:S(2)}) %all-to-all-start) | async-done | bytes 2129952 | tf_op jit(solution)/shard_map/all_to_all | solution.py:330
  37.3 5.6 %shard_map.104 = (bf16[32,8,2,16,128]{4,3,2,1,0:T(8,128)(2,1)S(1)}, f32[8,4,128]{2,1,0:T(4,128)S(1)}, f32[8,2,16,128]{3,2,1,0:T(8,128)S(1)}) custom-call(s32[5]{0:T(128)S(1)} %stack.62.place_ref, bf16[8,1040,128]{2,1,0:T(8,128)(2,1)S(1)} %all-to-all-done.got_ref, bf16[2,1152,128]{2,1,0:T(8,128)(2,1)S(1)} %copy-done.3), custom_call_target="tpu_custom_call" | custom-call | flops 4831838208 | bytes 4194304 | tf_op jit(solution)/shard_map/pallas_call | solution.py:467
  42.9 2.5 %collective-permute-start = (f32[8,2,16,128]{3,2,1,0:T(8,128)S(1)}, f32[8,2,16,128]{3,2,1,0:T(8,128)S(1)}, u32[]{:S(2)}, u32[]{:S(2)}) collective-permute-start(f32[8,2,16,128]{3,2,1,0:T(8,128)S(1)} %get-tuple-element.13), channel_id=1, source_target_pairs={{0,96},{32,64},{64,32},{96,0},{1,97},{33,65},{65,33},{97,1},{2,98}... | collective-permute-start | bytes 393224 | tf_op jit(solution)/shard_map/ppermute | solution.py:398
  45.4 3.0 %collective-permute-done.income_ref = f32[8,2,16,128]{3,2,1,0:T(8,128)S(1)} collective-permute-done((f32[8,2,16,128]{3,2,1,0:T(8,128)S(1)}, f32[8,2,16,128]{3,2,1,0:T(8,128)S(1)}, u32[]{:S(2)}, u32[]{:S(2)}) %collective-permute-start) | collective-permute-done | bytes 131104 | tf_op jit(solution)/shard_map/ppermute | solution.py:398
  48.4 6.5 %shard_map.105 = (bf16[32,8,2,16,128]{4,3,2,1,0:T(8,128)(2,1)S(1)}, f32[32,8,2,16,128]{4,3,2,1,0:T(8,128)S(1)}, f32[1,128]{1,0:T(1,128)S(1)}) custom-call(s32[5]{0:T(128)S(1)} %stack.62.place_ref, bf16[32,8,2,16,128]{4,3,2,1,0:T(8,128)(2,1)S(1)} %get-tuple-element.11.inputs_ref, f32[8,4,128]{2,1,0:T(4,128)S(1)} %get-tuple-element.12.decays_ref, ...), custom_call_target="tpu_custom_call" | custom-call | flops 4831838208 | bytes 4194304 | tf_op jit(solution)/shard_map/pallas_call | solution.py:475
  54.9 2.0 %copy-done.7 = f32[32,8,2,16,128]{4,3,2,1,0:T(8,128)} copy-done((f32[32,8,2,16,128]{4,3,2,1,0:T(8,128)}, f32[32,8,2,16,128]{4,3,2,1,0:T(8,128)S(1)}, u32[]{:S(2)}) %copy-start.7) | copy-done | bytes 4194328
  58.3 1.7 %collective-permute-start.1 = (f32[128]{0:T(128)S(1)}, f32[128]{0:T(128)S(1)}, u32[]{:S(2)}, u32[]{:S(2)}) collective-permute-start(f32[128]{0:T(128)S(1)} %bitcast.53), channel_id=1, source_target_pairs={{0,1},{1,0},{2,3},{3,2},{4,5},{5,4},{6,7},{7,6},{8,9},{9,8},{10,11... | collective-permute-start | bytes 1544 | tf_op jit(solution)/shard_map/ppermute | solution.py:299
  61.4 9.4 %all-to-all-start.1 = ((f32[64,2,128]{2,1,0:T(2,128)}), f32[64,2,128]{2,1,0:T(2,128)S(1)}, u32[]{:S(2)}, u32[]{:S(2)}) async-start(f32[64,2,128]{2,1,0:T(2,128)} %broadcast_in_dim.5), calls=%async_computation.1 | async-start | bytes 131072 | tf_op jit(solution)/shard_map/all_to_all | solution.py:310
  70.8 8.5 %all-to-all-done.1 = f32[64,2,128]{2,1,0:T(2,128)S(1)} async-done(((f32[64,2,128]{2,1,0:T(2,128)}), f32[64,2,128]{2,1,0:T(2,128)S(1)}, u32[]{:S(2)}, u32[]{:S(2)}) %all-to-all-start.1) | async-done | bytes 65568 | tf_op jit(solution)/shard_map/all_to_all | solution.py:310
  79.3 3.4 %copy-done = bf16[2048,2048]{1,0:T(8,128)(2,1)S(1)} copy-done((bf16[2048,2048]{1,0:T(8,128)(2,1)S(1)}, bf16[2048,2048]{1,0:T(8,128)(2,1)}, u32[]{:S(2)}) %copy-start) | copy-done | bytes 8388632
  82.7 6.6 %shard_map.106.dpool_ref = f32[1,128]{1,0:T(1,128)S(1)} custom-call(s32[5]{0:T(128)S(1)} %stack.62.place_ref, f32[4,32,128]{2,1,0:T(8,128)S(1)} %bitcast.51, f32[128,2048]{1,0:T(8,128)S(1)} %copy-done.1, f32[1,2048]{1,0:T(1,128)S(1)} %bitcast.52, bf16[2048,2048]{1,0:T(8,128)(2,1)S(1)} %copy-done), custom_call_target="tpu_custom_call" | custom-call | flops 805306368 | bytes 8388608 | tf_op jit(solution)/shard_map/pallas_call | solution.py:387
  89.3 6.0 %shard_map.107 = (bf16[32,8,2,16,128]{4,3,2,1,0:T(8,128)(2,1)S(1)}, f32[32,8,2,16,128]{4,3,2,1,0:T(8,128)S(1)}, f32[8,2,16,128]{3,2,1,0:T(8,128)S(1)}) custom-call(s32[5]{0:T(128)S(1)} %stack.62.place_ref, f32[32,8,2,16,128]{4,3,2,1,0:T(8,128)S(1)} %copy-done.8, f32[8,4,128]{2,1,0:T(4,128)S(1)} %get-tuple-element.12.decays_ref, ...), custom_call_target="tpu_custom_call" | custom-call | flops 4831838208 | bytes 4194304 | tf_op jit(solution)/shard_map/pallas_call | solution.py:486
  96.2 6.7 %shard_map.109 = f32[1152,128]{1,0:T(8,128)S(1)} custom-call(s32[5]{0:T(128)S(1)} %stack.62.place_ref, bf16[32,8,2,16,128]{4,3,2,1,0:T(8,128)(2,1)S(1)} %copy-done.10, bf16[32,8,2,16,128]{4,3,2,1,0:T(8,128)(2,1)S(1)} %get-tuple-element.19.dmix_ref), custom_call_target="tpu_custom_call" | custom-call | flops 4831838208 | bytes 4194304 | tf_op jit(solution)/shard_map/pallas_call | solution.py:494
  102.9 7.9 %shard_map.108 = f32[1152,128]{1,0:T(8,128)S(1)} custom-call(s32[5]{0:T(128)S(1)} %stack.62.place_ref, bf16[8,1040,128]{2,1,0:T(8,128)(2,1)S(1)} %all-to-all-done.got_ref, f32[32,8,2,16,128]{4,3,2,1,0:T(8,128)S(1)} %copy-done.8, f32[32,8,2,16,128]{4,3,2,1,0:T(8,128)S(1)} %get-tuple-element.16.source_ref, f32[8,4,128]{2,1,0:T(4,128)S(1)} %get-tuple-element.12.decays_ref, ...), custom_call_target="tpu_custom_call" | custom-call | flops 4831838208 | bytes 4194304 | tf_op jit(solution)/shard_map/pallas_call | solution.py:501
  110.9 2.1 %collective-permute-start.3 = (f32[2,4,144,128]{3,2,0,1:T(8,128)S(1)}, f32[2,4,144,128]{3,2,0,1:T(8,128)S(1)}, u32[]{:S(2)}, u32[]{:S(2)}) collective-permute-start(f32[2,4,144,128]{3,2,0,1:T(8,128)S(1)} %fusion.1), channel_id=1, source_target_pairs={{0,1},{1,0},{2,3},{3,2},{4,5},{5,4},{6,7},{7,6},{8,9},{9,8},{10,11... | collective-permute-start | bytes 1769480 | tf_op jit(solution)/shard_map/ppermute | solution.py:299
  112.9 1.6 %collective-permute-done.3 = f32[2,4,144,128]{3,2,0,1:T(8,128)S(1)} collective-permute-done((f32[2,4,144,128]{3,2,0,1:T(8,128)S(1)}, f32[2,4,144,128]{3,2,0,1:T(8,128)S(1)}, u32[]{:S(2)}, u32[]{:S(2)}) %collective-permute-start.3) | collective-permute-done | bytes 589856 | tf_op jit(solution)/shard_map/ppermute | solution.py:299
  115.0 1.9 %collective-permute-start.5 = (bf16[2,144,128]{2,1,0:T(8,128)(2,1)S(1)}, bf16[2,144,128]{2,1,0:T(8,128)(2,1)S(1)}, u32[]{:S(2)}, u32[]{:S(2)}) collective-permute-start(bf16[2,144,128]{2,1,0:T(8,128)(2,1)S(1)} %get-tuple-element.24), channel_id=1, source_target_pairs={{0,4},{2,6},{4,0},{6,2},{1,5},{3,7},{5,1},{7,3},{8,12},{10,14},{12... | collective-permute-start | bytes 221192 | tf_op jit(solution)/shard_map/ppermute | solution.py:402
  116.9 1.7 %collective-permute-start.6 = (bf16[2,144,128]{2,1,0:T(8,128)(2,1)S(1)}, bf16[2,144,128]{2,1,0:T(8,128)(2,1)S(1)}, u32[]{:S(2)}, u32[]{:S(2)}) collective-permute-start(bf16[2,144,128]{2,1,0:T(8,128)(2,1)S(1)} %get-tuple-element.23), channel_id=1, source_target_pairs={{0,6},{2,4},{4,2},{6,0},{1,7},{3,5},{5,3},{7,1},{8,14},{10,12},{12... | collective-permute-start | bytes 221192 | tf_op jit(solution)/shard_map/ppermute | solution.py:402
  118.6 2.2 %collective-permute-done.5 = bf16[2,144,128]{2,1,0:T(8,128)(2,1)S(1)} collective-permute-done((bf16[2,144,128]{2,1,0:T(8,128)(2,1)S(1)}, bf16[2,144,128]{2,1,0:T(8,128)(2,1)S(1)}, u32[]{:S(2)}, u32[]{:S(2)}) %collective-permute-start.5) | collective-permute-done | bytes 73760 | tf_op jit(solution)/shard_map/ppermute | solution.py:402
  122.3 1.8 %collective-permute-start.8 = (bf16[2,144,128]{2,1,0:T(8,128)(2,1)S(1)}, bf16[2,144,128]{2,1,0:T(8,128)(2,1)S(1)}, u32[]{:S(2)}, u32[]{:S(2)}) collective-permute-start(bf16[2,144,128]{2,1,0:T(8,128)(2,1)S(1)} %fusion.8), channel_id=1, source_target_pairs={{0,16},{8,24},{16,0},{24,8},{1,17},{9,25},{17,1},{25,9},{2,18},{10... | collective-permute-start | bytes 221192 | tf_op jit(solution)/shard_map/ppermute | solution.py:402
  124.1 1.7 %collective-permute-start.9 = (bf16[2,144,128]{2,1,0:T(8,128)(2,1)S(1)}, bf16[2,144,128]{2,1,0:T(8,128)(2,1)S(1)}, u32[]{:S(2)}, u32[]{:S(2)}) collective-permute-start(bf16[2,144,128]{2,1,0:T(8,128)(2,1)S(1)} %fusion.8), channel_id=1, source_target_pairs={{0,24},{8,16},{16,8},{24,0},{1,25},{9,17},{17,9},{25,1},{2,26},{10... | collective-permute-start | bytes 221192 | tf_op jit(solution)/shard_map/ppermute | solution.py:402
  127.0 1.8 %collective-permute-done.9 = bf16[2,144,128]{2,1,0:T(8,128)(2,1)S(1)} collective-permute-done((bf16[2,144,128]{2,1,0:T(8,128)(2,1)S(1)}, bf16[2,144,128]{2,1,0:T(8,128)(2,1)S(1)}, u32[]{:S(2)}, u32[]{:S(2)}) %collective-permute-start.9) | collective-permute-done | bytes 73760 | tf_op jit(solution)/shard_map/ppermute | solution.py:402
  128.9 2.0 %collective-permute-start.10 = (bf16[2,144,128]{2,1,0:T(8,128)(2,1)S(1)}, bf16[2,144,128]{2,1,0:T(8,128)(2,1)S(1)}, u32[]{:S(2)}, u32[]{:S(2)}) collective-permute-start(bf16[2,144,128]{2,1,0:T(8,128)(2,1)S(1)} %add_convert_fusion.2), channel_id=1, source_target_pairs={{0,96},{32,64},{64,32},{96,0},{1,97},{33,65},{65,33},{97,1},{2,98}... | collective-permute-start | bytes 221192 | tf_op jit(solution)/shard_map/ppermute | solution.py:402
  130.9 1.9 %collective-permute-start.12 = (bf16[2,144,128]{2,1,0:T(8,128)(2,1)S(1)}, bf16[2,144,128]{2,1,0:T(8,128)(2,1)S(1)}, u32[]{:S(2)}, u32[]{:S(2)}) collective-permute-start(bf16[2,144,128]{2,1,0:T(8,128)(2,1)S(1)} %add_convert_fusion.2), channel_id=1, source_target_pairs={{0,64},{32,96},{64,0},{96,32},{1,65},{33,97},{65,1},{97,33},{2,66}... | collective-permute-start | bytes 221192 | tf_op jit(solution)/shard_map/ppermute | solution.py:402
  135.8 2.5 %collective-permute-start.14 = (bf16[2,2,144,128]{3,2,1,0:T(8,128)(2,1)S(1)}, bf16[2,2,144,128]{3,2,1,0:T(8,128)(2,1)S(1)}, u32[]{:S(2)}, u32[]{:S(2)}) collective-permute-start(bf16[2,2,144,128]{3,2,1,0:T(8,128)(2,1)S(1)} %pad_maximum_fusion.1.refs_0_), channel_id=1, source_target_pairs={{0,4},{2,6},{4,0},{6,2},{1,5},{3,7},{5,1},{7,3},{8,12},{10,14},{12... | collective-permute-start | bytes 442376 | tf_op jit(solution)/shard_map/ppermute | solution.py:402
  139.6 5.2 %collective-permute-start.16 = (bf16[2,2,144,128]{3,2,1,0:T(8,128)(2,1)S(1)}, bf16[2,2,144,128]{3,2,1,0:T(8,128)(2,1)S(1)}, u32[]{:S(2)}, u32[]{:S(2)}) collective-permute-start(bf16[2,2,144,128]{3,2,1,0:T(8,128)(2,1)S(1)} %pad_maximum_fusion.1.refs_0_), channel_id=1, source_target_pairs={{0,1},{1,0},{2,3},{3,2},{4,5},{5,4},{6,7},{7,6},{8,9},{9,8},{10,11... | collective-permute-start | bytes 442376 | tf_op jit(solution)/shard_map/ppermute | solution.py:299
  145.3 3.0 %collective-permute-start.18 = (bf16[2,2,144,128]{3,2,1,0:T(8,128)(2,1)S(1)}, bf16[2,2,144,128]{3,2,1,0:T(8,128)(2,1)S(1)}, u32[]{:S(2)}, u32[]{:S(2)}) collective-permute-start(bf16[2,2,144,128]{3,2,1,0:T(8,128)(2,1)S(1)} %collective-permute-done.14.refs_2_), channel_id=1, source_target_pairs={{0,1},{1,0},{2,3},{3,2},{4,5},{5,4},{6,7},{7,6},{8,9},{9,8},{10,11... | collective-permute-start | bytes 442376 | tf_op jit(solution)/shard_map/ppermute | solution.py:299
  148.3 1.7 %collective-permute-start.19 = (bf16[2,2,144,128]{3,2,1,0:T(8,128)(2,1)S(1)}, bf16[2,2,144,128]{3,2,1,0:T(8,128)(2,1)S(1)}, u32[]{:S(2)}, u32[]{:S(2)}) collective-permute-start(bf16[2,2,144,128]{3,2,1,0:T(8,128)(2,1)S(1)} %collective-permute-done.15.refs_3_), channel_id=1, source_target_pairs={{0,1},{1,0},{2,3},{3,2},{4,5},{5,4},{6,7},{7,6},{8,9},{9,8},{10,11... | collective-permute-start | bytes 442376 | tf_op jit(solution)/shard_map/ppermute | solution.py:299
  150.9 2.1 %shard_map.110 = (f32[2,1152,128]{2,1,0:T(8,128)}, f32[2,1152,128]{2,1,0:T(8,128)}) custom-call(s32[5]{0:T(128)S(1)} %stack.62.place_ref, bf16[2,2,144,128]{3,2,1,0:T(8,128)(2,1)S(1)} %pad_maximum_fusion.1.refs_0_, bf16[2,2,144,128]{3,2,1,0:T(8,128)(2,1)S(1)} %collective-permute-done.13.refs_1_, ...), custom_call_target="tpu_custom_call" | custom-call | tf_op jit(solution)/shard_map/pallas_call | solution.py:441
  (58 shorter events, 13.5 us)
Async XLA Ops:
  4.6 32.6 %copy-start.3 = (bf16[2,1152,128]{2,1,0:T(8,128)(2,1)S(1)}, bf16[2,1152,128]{2,1,0:T(8,128)(2,1)}, u32[]{:S(2)}) copy-start(bf16[2,1152,128]{2,1,0:T(8,128)(2,1)} %weights_ref.3) | copy-start | bytes 1769476
  4.6 32.6 %all-to-all-start = ((bf16[8,1040,128]{2,1,0:T(8,128)(2,1)}), bf16[8,1040,128]{2,1,0:T(8,128)(2,1)S(1)}, u32[]{:S(2)}, u32[]{:S(2)}) async-start(bf16[8,1040,128]{2,1,0:T(8,128)(2,1)} %bitcast.56), calls=%async_computation | async-start | bytes 4259840 | tf_op jit(solution)/shard_map/all_to_all | solution.py:330
  10.8 37.6 %copy-start.6 = (f32[2,128]{1,0:T(2,128)S(1)}, f32[2,128]{1,0:T(2,128)}, u32[]{:S(2)}) copy-start(f32[2,128]{1,0:T(2,128)} %param.14) | copy-start | bytes 3076
  37.3 11.2 %copy-start.4 = (bf16[2,1152,128]{2,1,0:T(8,128)(2,1)S(1)}, bf16[2,1152,128]{2,1,0:T(8,128)(2,1)}, u32[]{:S(2)}) copy-start(bf16[2,1152,128]{2,1,0:T(8,128)(2,1)} %weights_ref.5) | copy-start | bytes 1769476
  42.9 5.6 %collective-permute-start = (f32[8,2,16,128]{3,2,1,0:T(8,128)S(1)}, f32[8,2,16,128]{3,2,1,0:T(8,128)S(1)}, u32[]{:S(2)}, u32[]{:S(2)}) collective-permute-start(f32[8,2,16,128]{3,2,1,0:T(8,128)S(1)} %get-tuple-element.13), channel_id=1, source_target_pairs={{0,96},{32,64},{64,32},{96,0},{1,97},{33,65},{65,33},{97,1},{2,98}... | collective-permute-start | bytes 393224 | tf_op jit(solution)/shard_map/ppermute | solution.py:398
  48.4 30.9 %copy-start.1 = (f32[128,2048]{1,0:T(8,128)S(1)}, f32[128,2048]{1,0:T(8,128)}, u32[]{:S(2)}) copy-start(f32[128,2048]{1,0:T(8,128)} %in_ref.1) | copy-start | bytes 3145732
  48.4 30.9 %copy-start.2 = (f32[2048]{0:T(1024)S(1)}, f32[2048]{0:T(1024)}, u32[]{:S(2)}) copy-start(f32[2048]{0:T(1024)} %param.16) | copy-start | bytes 24580
  54.9 2.0 %copy-start.7 = (f32[32,8,2,16,128]{4,3,2,1,0:T(8,128)}, f32[32,8,2,16,128]{4,3,2,1,0:T(8,128)S(1)}, u32[]{:S(2)}) copy-start(f32[32,8,2,16,128]{4,3,2,1,0:T(8,128)S(1)} %get-tuple-element.14.slope_ref) | copy-start | bytes 12582916
  58.3 2.5 %collective-permute-start.1 = (f32[128]{0:T(128)S(1)}, f32[128]{0:T(128)S(1)}, u32[]{:S(2)}, u32[]{:S(2)}) collective-permute-start(f32[128]{0:T(128)S(1)} %bitcast.53), channel_id=1, source_target_pairs={{0,1},{1,0},{2,3},{3,2},{4,5},{5,4},{6,7},{7,6},{8,9},{9,8},{10,11... | collective-permute-start | bytes 1544 | tf_op jit(solution)/shard_map/ppermute | solution.py:299
  61.4 17.9 %all-to-all-start.1 = ((f32[64,2,128]{2,1,0:T(2,128)}), f32[64,2,128]{2,1,0:T(2,128)S(1)}, u32[]{:S(2)}, u32[]{:S(2)}) async-start(f32[64,2,128]{2,1,0:T(2,128)} %broadcast_in_dim.5), calls=%async_computation.1 | async-start | bytes 131072 | tf_op jit(solution)/shard_map/all_to_all | solution.py:310
  79.3 3.4 %copy-start = (bf16[2048,2048]{1,0:T(8,128)(2,1)S(1)}, bf16[2048,2048]{1,0:T(8,128)(2,1)}, u32[]{:S(2)}) copy-start(bf16[2048,2048]{1,0:T(8,128)(2,1)} %out_ref.1) | copy-start | bytes 25165828
  82.7 6.6 %copy-start.5 = (bf16[2,1152,128]{2,1,0:T(8,128)(2,1)S(1)}, bf16[2,1152,128]{2,1,0:T(8,128)(2,1)}, u32[]{:S(2)}) copy-start(bf16[2,1152,128]{2,1,0:T(8,128)(2,1)} %weights_ref.5) | copy-start | bytes 1769476
  82.7 6.6 %copy-start.8 = (f32[32,8,2,16,128]{4,3,2,1,0:T(8,128)S(1)}, f32[32,8,2,16,128]{4,3,2,1,0:T(8,128)}, u32[]{:S(2)}) copy-start(f32[32,8,2,16,128]{4,3,2,1,0:T(8,128)} %copy-done.7) | copy-start | bytes 12582916
  89.3 6.9 %copy-start.10 = (bf16[32,8,2,16,128]{4,3,2,1,0:T(8,128)(2,1)S(1)}, bf16[32,8,2,16,128]{4,3,2,1,0:T(8,128)(2,1)}, u32[]{:S(2)}) copy-start(bf16[32,8,2,16,128]{4,3,2,1,0:T(8,128)(2,1)} %copy-done.9) | copy-start | bytes 6291460
  95.3 7.5 %collective-permute-start.2 = (f32[8,2,16,128]{3,2,1,0:T(8,128)S(1)}, f32[8,2,16,128]{3,2,1,0:T(8,128)S(1)}, u32[]{:S(2)}, u32[]{:S(2)}) collective-permute-start(f32[8,2,16,128]{3,2,1,0:T(8,128)S(1)} %get-tuple-element.17), channel_id=1, source_target_pairs={{0,96},{32,64},{64,32},{96,0},{1,97},{33,65},{65,33},{97,1},{2,98}... | collective-permute-start | bytes 393224 | tf_op jit(solution)/shard_map/ppermute | solution.py:398
  110.9 3.7 %collective-permute-start.3 = (f32[2,4,144,128]{3,2,0,1:T(8,128)S(1)}, f32[2,4,144,128]{3,2,0,1:T(8,128)S(1)}, u32[]{:S(2)}, u32[]{:S(2)}) collective-permute-start(f32[2,4,144,128]{3,2,0,1:T(8,128)S(1)} %fusion.1), channel_id=1, source_target_pairs={{0,1},{1,0},{2,3},{3,2},{4,5},{5,4},{6,7},{7,6},{8,9},{9,8},{10,11... | collective-permute-start | bytes 1769480 | tf_op jit(solution)/shard_map/ppermute | solution.py:299
  114.7 3.9 %collective-permute-start.4 = (bf16[2,144,128]{2,1,0:T(8,128)(2,1)S(1)}, bf16[2,144,128]{2,1,0:T(8,128)(2,1)S(1)}, u32[]{:S(2)}, u32[]{:S(2)}) collective-permute-start(bf16[2,144,128]{2,1,0:T(8,128)(2,1)S(1)} %get-tuple-element.22), channel_id=1, source_target_pairs={{0,2},{2,0},{4,6},{6,4},{1,3},{3,1},{5,7},{7,5},{8,10},{10,8},{12,... | collective-permute-start | bytes 221192 | tf_op jit(solution)/shard_map/ppermute | solution.py:402
  115.0 5.8 %collective-permute-start.5 = (bf16[2,144,128]{2,1,0:T(8,128)(2,1)S(1)}, bf16[2,144,128]{2,1,0:T(8,128)(2,1)S(1)}, u32[]{:S(2)}, u32[]{:S(2)}) collective-permute-start(bf16[2,144,128]{2,1,0:T(8,128)(2,1)S(1)} %get-tuple-element.24), channel_id=1, source_target_pairs={{0,4},{2,6},{4,0},{6,2},{1,5},{3,7},{5,1},{7,3},{8,12},{10,14},{12... | collective-permute-start | bytes 221192 | tf_op jit(solution)/shard_map/ppermute | solution.py:402
  116.9 4.9 %collective-permute-start.6 = (bf16[2,144,128]{2,1,0:T(8,128)(2,1)S(1)}, bf16[2,144,128]{2,1,0:T(8,128)(2,1)S(1)}, u32[]{:S(2)}, u32[]{:S(2)}) collective-permute-start(bf16[2,144,128]{2,1,0:T(8,128)(2,1)S(1)} %get-tuple-element.23), channel_id=1, source_target_pairs={{0,6},{2,4},{4,2},{6,0},{1,7},{3,5},{5,3},{7,1},{8,14},{10,12},{12... | collective-permute-start | bytes 221192 | tf_op jit(solution)/shard_map/ppermute | solution.py:402
  121.9 3.9 %collective-permute-start.7 = (bf16[2,144,128]{2,1,0:T(8,128)(2,1)S(1)}, bf16[2,144,128]{2,1,0:T(8,128)(2,1)S(1)}, u32[]{:S(2)}, u32[]{:S(2)}) collective-permute-start(bf16[2,144,128]{2,1,0:T(8,128)(2,1)S(1)} %fusion.8), channel_id=1, source_target_pairs={{0,8},{8,0},{16,24},{24,16},{1,9},{9,1},{17,25},{25,17},{2,10},{10... | collective-permute-start | bytes 221192 | tf_op jit(solution)/shard_map/ppermute | solution.py:402
  122.3 4.7 %collective-permute-start.8 = (bf16[2,144,128]{2,1,0:T(8,128)(2,1)S(1)}, bf16[2,144,128]{2,1,0:T(8,128)(2,1)S(1)}, u32[]{:S(2)}, u32[]{:S(2)}) collective-permute-start(bf16[2,144,128]{2,1,0:T(8,128)(2,1)S(1)} %fusion.8), channel_id=1, source_target_pairs={{0,16},{8,24},{16,0},{24,8},{1,17},{9,25},{17,1},{25,9},{2,18},{10... | collective-permute-start | bytes 221192 | tf_op jit(solution)/shard_map/ppermute | solution.py:402
  124.1 4.7 %collective-permute-start.9 = (bf16[2,144,128]{2,1,0:T(8,128)(2,1)S(1)}, bf16[2,144,128]{2,1,0:T(8,128)(2,1)S(1)}, u32[]{:S(2)}, u32[]{:S(2)}) collective-permute-start(bf16[2,144,128]{2,1,0:T(8,128)(2,1)S(1)} %fusion.8), channel_id=1, source_target_pairs={{0,24},{8,16},{16,8},{24,0},{1,25},{9,17},{17,9},{25,1},{2,26},{10... | collective-permute-start | bytes 221192 | tf_op jit(solution)/shard_map/ppermute | solution.py:402
  128.9 4.5 %collective-permute-start.10 = (bf16[2,144,128]{2,1,0:T(8,128)(2,1)S(1)}, bf16[2,144,128]{2,1,0:T(8,128)(2,1)S(1)}, u32[]{:S(2)}, u32[]{:S(2)}) collective-permute-start(bf16[2,144,128]{2,1,0:T(8,128)(2,1)S(1)} %add_convert_fusion.2), channel_id=1, source_target_pairs={{0,96},{32,64},{64,32},{96,0},{1,97},{33,65},{65,33},{97,1},{2,98}... | collective-permute-start | bytes 221192 | tf_op jit(solution)/shard_map/ppermute | solution.py:402
  130.9 3.2 %collective-permute-start.11 = (bf16[2,144,128]{2,1,0:T(8,128)(2,1)S(1)}, bf16[2,144,128]{2,1,0:T(8,128)(2,1)S(1)}, u32[]{:S(2)}, u32[]{:S(2)}) collective-permute-start(bf16[2,144,128]{2,1,0:T(8,128)(2,1)S(1)} %add_convert_fusion.2), channel_id=1, source_target_pairs={{0,32},{32,0},{64,96},{96,64},{1,33},{33,1},{65,97},{97,65},{2,34}... | collective-permute-start | bytes 221192 | tf_op jit(solution)/shard_map/ppermute | solution.py:402
  130.9 4.7 %collective-permute-start.12 = (bf16[2,144,128]{2,1,0:T(8,128)(2,1)S(1)}, bf16[2,144,128]{2,1,0:T(8,128)(2,1)S(1)}, u32[]{:S(2)}, u32[]{:S(2)}) collective-permute-start(bf16[2,144,128]{2,1,0:T(8,128)(2,1)S(1)} %add_convert_fusion.2), channel_id=1, source_target_pairs={{0,64},{32,96},{64,0},{96,32},{1,65},{33,97},{65,1},{97,33},{2,66}... | collective-permute-start | bytes 221192 | tf_op jit(solution)/shard_map/ppermute | solution.py:402
  135.7 9.2 %collective-permute-start.13 = (bf16[2,2,144,128]{3,2,1,0:T(8,128)(2,1)S(1)}, bf16[2,2,144,128]{3,2,1,0:T(8,128)(2,1)S(1)}, u32[]{:S(2)}, u32[]{:S(2)}) collective-permute-start(bf16[2,2,144,128]{3,2,1,0:T(8,128)(2,1)S(1)} %pad_maximum_fusion.1.refs_0_), channel_id=1, source_target_pairs={{0,2},{2,0},{4,6},{6,4},{1,3},{3,1},{5,7},{7,5},{8,10},{10,8},{12,... | collective-permute-start | bytes 442376 | tf_op jit(solution)/shard_map/ppermute | solution.py:402
  135.8 9.5 %collective-permute-start.14 = (bf16[2,2,144,128]{3,2,1,0:T(8,128)(2,1)S(1)}, bf16[2,2,144,128]{3,2,1,0:T(8,128)(2,1)S(1)}, u32[]{:S(2)}, u32[]{:S(2)}) collective-permute-start(bf16[2,2,144,128]{3,2,1,0:T(8,128)(2,1)S(1)} %pad_maximum_fusion.1.refs_0_), channel_id=1, source_target_pairs={{0,4},{2,6},{4,0},{6,2},{1,5},{3,7},{5,1},{7,3},{8,12},{10,14},{12... | collective-permute-start | bytes 442376 | tf_op jit(solution)/shard_map/ppermute | solution.py:402
  138.3 10.0 %collective-permute-start.15 = (bf16[2,2,144,128]{3,2,1,0:T(8,128)(2,1)S(1)}, bf16[2,2,144,128]{3,2,1,0:T(8,128)(2,1)S(1)}, u32[]{:S(2)}, u32[]{:S(2)}) collective-permute-start(bf16[2,2,144,128]{3,2,1,0:T(8,128)(2,1)S(1)} %pad_maximum_fusion.1.refs_0_), channel_id=1, source_target_pairs={{0,6},{2,4},{4,2},{6,0},{1,7},{3,5},{5,3},{7,1},{8,14},{10,12},{12... | collective-permute-start | bytes 442376 | tf_op jit(solution)/shard_map/ppermute | solution.py:402
  139.6 10.3 %collective-permute-start.16 = (bf16[2,2,144,128]{3,2,1,0:T(8,128)(2,1)S(1)}, bf16[2,2,144,128]{3,2,1,0:T(8,128)(2,1)S(1)}, u32[]{:S(2)}, u32[]{:S(2)}) collective-permute-start(bf16[2,2,144,128]{3,2,1,0:T(8,128)(2,1)S(1)} %pad_maximum_fusion.1.refs_0_), channel_id=1, source_target_pairs={{0,1},{1,0},{2,3},{3,2},{4,5},{5,4},{6,7},{7,6},{8,9},{9,8},{10,11... | collective-permute-start | bytes 442376 | tf_op jit(solution)/shard_map/ppermute | solution.py:299
  144.8 5.1 %collective-permute-start.17 = (bf16[2,2,144,128]{3,2,1,0:T(8,128)(2,1)S(1)}, bf16[2,2,144,128]{3,2,1,0:T(8,128)(2,1)S(1)}, u32[]{:S(2)}, u32[]{:S(2)}) collective-permute-start(bf16[2,2,144,128]{3,2,1,0:T(8,128)(2,1)S(1)} %collective-permute-done.13.refs_1_), channel_id=1, source_target_pairs={{0,1},{1,0},{2,3},{3,2},{4,5},{5,4},{6,7},{7,6},{8,9},{9,8},{10,11... | collective-permute-start | bytes 442376 | tf_op jit(solution)/shard_map/ppermute | solution.py:299
  145.3 4.6 %collective-permute-start.18 = (bf16[2,2,144,128]{3,2,1,0:T(8,128)(2,1)S(1)}, bf16[2,2,144,128]{3,2,1,0:T(8,128)(2,1)S(1)}, u32[]{:S(2)}, u32[]{:S(2)}) collective-permute-start(bf16[2,2,144,128]{3,2,1,0:T(8,128)(2,1)S(1)} %collective-permute-done.14.refs_2_), channel_id=1, source_target_pairs={{0,1},{1,0},{2,3},{3,2},{4,5},{5,4},{6,7},{7,6},{8,9},{9,8},{10,11... | collective-permute-start | bytes 442376 | tf_op jit(solution)/shard_map/ppermute | solution.py:299
  148.3 2.7 %collective-permute-start.19 = (bf16[2,2,144,128]{3,2,1,0:T(8,128)(2,1)S(1)}, bf16[2,2,144,128]{3,2,1,0:T(8,128)(2,1)S(1)}, u32[]{:S(2)}, u32[]{:S(2)}) collective-permute-start(bf16[2,2,144,128]{3,2,1,0:T(8,128)(2,1)S(1)} %collective-permute-done.15.refs_3_), channel_id=1, source_target_pairs={{0,1},{1,0},{2,3},{3,2},{4,5},{5,4},{6,7},{7,6},{8,9},{9,8},{10,11... | collective-permute-start | bytes 442376 | tf_op jit(solution)/shard_map/ppermute | solution.py:299
  (1 other events, 1.4 us)

commit v3 on v2

--- a/solution.py
+++ b/solution.py
@@ -18,6 +18,7 @@
 
 
 BF16, F32 = jnp.bfloat16, jnp.float32
+CHUNKS = 4
 
 
 def pair_weights(weights_ref, both_ref):
@@ -84,13 +85,13 @@
     return both[:, :channels].reshape(shape), both[:, channels:].reshape(shape)
 
 
-def add_weight_product(cols_ref, grads, acc_ref):
+def add_weight_product(cols, grads, acc_ref):
     frames, pairs, _, side, channels = grads.shape
     rows = frames * pairs * side
     both = [grads[:, :, k].reshape(rows, channels) for k in range(2)]
     acc_ref[...] += lax.dot_general(
         jnp.concatenate(both, axis=1),
-        pair_patches(cols_ref),
+        jnp.concatenate([pair_patches(cols_ref) for cols_ref in cols]),
         (((0,), (0,)), ((), ())),
         preferred_element_type=F32,
     )
@@ -103,26 +104,49 @@
     return total.T
 
 
-def inputs_kernel(place_ref, got_ref, weights_ref, inputs_ref, decays_ref, end_ref, cols_ref, both_ref, carry_ref):
+def spread_groups(groups, cols):
+    for maps, cols_ref in zip(groups, cols):
+        spread_columns(maps, cols_ref)
+
+
+def halves(ref):
+    group = ref.shape[0] // 2
+    return [ref[:group], ref[group:]]
+
+
+def got_maps(got_ref, shape):
+    cells = shape[0] * shape[1] * shape[2] * shape[3] // 2
+    return [got_ref[h, :cells].reshape(shape[0] // 2, *shape[1:]) for h in range(2)]
+
+
+def decay_of(decays_ref, t):
+    group = decays_ref.shape[1]
+    return decays_ref[t // group, t % group : t % group + 1]
+
+
+def inputs_kernel(place_ref, got_ref, weights_ref, inputs_ref, decays_ref, end_ref, cols_a, cols_b, both_ref, carry_ref):
     step = pl.program_id(0)
-    frames, pairs, _, side, channels = inputs_ref.shape
-    cells = frames * side * side
+    cols = (cols_a, cols_b)
+    frames, _, _, side, _ = inputs_ref.shape
+    group = frames // 2
+    cells = group * side * side
 
     @pl.when(step == 0)
     def _():
-        clear_edges(cols_ref)
+        clear_edges(cols_a)
+        clear_edges(cols_b)
         pair_weights(weights_ref, both_ref)
         carry_ref[...] = jnp.zeros_like(carry_ref)
 
-    spread_columns(got_ref[0, :cells].reshape(inputs_ref.shape), cols_ref)
-    parts = got_ref[0, cells:].astype(F32)
-    decays = parts[:frames] + parts[frames : 2 * frames] + parts[2 * frames : 3 * frames]
-    decays_ref[0] = decays
-    for k, rows in enumerate(pair_convolve(cols_ref, both_ref)):
-        inputs_ref[:, :, k] = rows.astype(BF16)
+    spread_groups(got_maps(got_ref, inputs_ref.shape), cols)
+    for h in range(2):
+        parts = got_ref[h, cells:].astype(F32)
+        decays_ref[h] = parts[:group] + parts[group : 2 * group] + parts[2 * group : 3 * group]
+        for k, rows in enumerate(pair_convolve(cols[h], both_ref)):
+            inputs_ref[h * group : (h + 1) * group, :, k] = rows.astype(BF16)
     carried = carry_ref[...]
     for t in range(frames):
-        carried = decays[t : t + 1] * carried + inputs_ref[t].astype(F32)
+        carried = decay_of(decays_ref, t) * carried + inputs_ref[t].astype(F32)
     carry_ref[...] = carried
 
     @pl.when(step == pl.num_programs(0) - 1)
@@ -130,29 +154,34 @@
         end_ref[...] = carried
 
 
-def mixed_kernel(place_ref, inputs_ref, decays_ref, income_ref, skip_ref, weights_ref, states_ref, slope_ref, pooled_ref, cols_ref, both_ref, carry_ref, sum_ref):
+def mixed_kernel(place_ref, inputs_ref, decays_ref, income_ref, skip_ref, weights_ref, states_ref, slope_ref, pooled_ref, cols_a, cols_b, both_ref, carry_ref, sum_ref):
     step = pl.program_id(0)
+    cols = (cols_a, cols_b)
     frames = inputs_ref.shape[0]
+    group = frames // 2
 
     @pl.when(step == 0)
     def _():
-        clear_edges(cols_ref)
+        clear_edges(cols_a)
+        clear_edges(cols_b)
         pair_weights(weights_ref, both_ref)
         take_carry(carry_ref, income_ref, place_ref[0] == 1)
         sum_ref[...] = jnp.zeros_like(sum_ref)
 
     carried = carry_ref[...]
     for t in range(frames):
-        carried = decays_ref[0, t : t + 1] * carried + inputs_ref[t].astype(F32)
+        carried = decay_of(decays_ref, t) * carried + inputs_ref[t].astype(F32)
         states_ref[t] = carried.astype(BF16)
     carry_ref[...] = carried
-    spread_columns(states_ref[...], cols_ref)
+    spread_groups(halves(states_ref), cols)
     total = sum_ref[...]
-    for k, rows in enumerate(pair_convolve(cols_ref, both_ref)):
-        mixed = rows + skip_ref[0] * inputs_ref[:, :, k].astype(F32)
-        sigma = jax.nn.sigmoid(mixed)
-        slope_ref[:, :, k] = sigma * (1.0 + mixed * (1.0 - sigma))
-        total = total + jnp.sum(mixed * sigma, axis=(0, 1))
+    for h in range(2):
+        here = slice(h * group, (h + 1) * group)
+        for k, rows in enumerate(pair_convolve(cols[h], both_ref)):
+            mixed = rows + skip_ref[0] * inputs_ref[here, :, k].astype(F32)
+            sigma = jax.nn.sigmoid(mixed)
+            slope_ref[here, :, k] = sigma * (1.0 + mixed * (1.0 - sigma))
+            total = total + jnp.sum(mixed * sigma, axis=(0, 1))
     sum_ref[...] = total
 
     @pl.when(step == pl.num_programs(0) - 1)
@@ -160,65 +189,71 @@
         pooled_ref[...] = jnp.sum(total, axis=0, keepdims=True)
 
 
-def from_out_kernel(place_ref, slope_ref, decays_ref, dpool_ref, weights_ref, dmix_ref, source_ref, end_ref, cols_ref, both_ref, carry_ref):
+def from_out_kernel(place_ref, slope_ref, decays_ref, dpool_ref, weights_ref, dmix_ref, source_ref, end_ref, cols_a, cols_b, both_ref, carry_ref):
+    step = pl.program_id(0)
+    cols = (cols_a, cols_b)
+    frames = slope_ref.shape[0]
+    group = frames // 2
+
+    @pl.when(step == 0)
+    def _():
+        clear_edges(cols_a)
+        clear_edges(cols_b)
+        flipped_pair_weights(weights_ref, both_ref)
+        carry_ref[...] = jnp.zeros_like(carry_ref)
+
+    dmix_ref[...] = (dpool_ref[...] * slope_ref[...]).astype(BF16)
+    spread_groups(halves(dmix_ref), cols)
+    for h in range(2):
+        for k, rows in enumerate(pair_convolve(cols[h], both_ref)):
+            source_ref[h * group : (h + 1) * group, :, k] = rows
+    carried = carry_ref[...]
+    for t in reversed(range(frames)):
+        carried = decay_of(decays_ref, t) * (source_ref[t] + carried)
+    carry_ref[...] = carried
+
+    @pl.when(step == pl.num_programs(0) - 1)
+    def _():
+        end_ref[...] = carried
+
+
+def out_grad_kernel(place_ref, states_ref, dmix_ref, grad_ref, cols_a, cols_b, acc_ref):
+    step = pl.program_id(0)
+
+    @pl.when(step == 0)
+    def _():
+        clear_edges(cols_a)
+        clear_edges(cols_b)
+        acc_ref[...] = jnp.zeros_like(acc_ref)
+
+    spread_groups(halves(states_ref), (cols_a, cols_b))
+    add_weight_product((cols_a, cols_b), dmix_ref[...], acc_ref)
+
+    @pl.when(step == pl.num_programs(0) - 1)
+    def _():
+        grad_ref[...] = folded(acc_ref)
+
+
+def in_grad_kernel(place_ref, got_ref, slope_ref, source_ref, decays_ref, income_ref, dpool_ref, skip_ref, grad_ref, cols_a, cols_b, carry_ref, dinput_ref, acc_ref):
     step = pl.program_id(0)
     frames = slope_ref.shape[0]
 
     @pl.when(step == 0)
     def _():
-        clear_edges(cols_ref)
-        flipped_pair_weights(weights_ref, both_ref)
-        carry_ref[...] = jnp.zeros_like(carry_ref)
-
-    dmix_ref[...] = (dpool_ref[...] * slope_ref[...]).astype(BF16)
-    spread_columns(dmix_ref[...], cols_ref)
-    for k, rows in enumerate(pair_convolve(cols_ref, both_ref)):
-        source_ref[:, :, k] = rows
-    carried = carry_ref[...]
-    for t in reversed(range(frames)):
-        carried = decays_ref[0, t : t + 1] * (source_ref[t] + carried)
-    carry_ref[...] = carried
-
-    @pl.when(step == pl.num_programs(0) - 1)
-    def _():
-        end_ref[...] = carried
-
-
-def out_grad_kernel(place_ref, states_ref, dmix_ref, grad_ref, cols_ref, acc_ref):
-    step = pl.program_id(0)
-
-    @pl.when(step == 0)
-    def _():
-        clear_edges(cols_ref)
-        acc_ref[...] = jnp.zeros_like(acc_ref)
-
-    spread_columns(states_ref[...], cols_ref)
-    add_weight_product(cols_ref, dmix_ref[...], acc_ref)
-
-    @pl.when(step == pl.num_programs(0) - 1)
-    def _():
-        grad_ref[...] = folded(acc_ref)
-
-
-def in_grad_kernel(place_ref, got_ref, slope_ref, source_ref, decays_ref, income_ref, dpool_ref, skip_ref, grad_ref, cols_ref, carry_ref, dinput_ref, acc_ref):
-    step = pl.program_id(0)
-    frames, _, _, side, _ = slope_ref.shape
-
-    @pl.when(step == 0)
-    def _():
-        clear_edges(cols_ref)
+        clear_edges(cols_a)
+        clear_edges(cols_b)
         take_carry(carry_ref, income_ref, place_ref[0] == 0)
         acc_ref[...] = jnp.zeros_like(acc_ref)
 
-    spread_columns(got_ref[0, : frames * side * side].reshape(slope_ref.shape), cols_ref)
+    spread_groups(got_maps(got_ref, slope_ref.shape), (cols_a, cols_b))
     carried = carry_ref[...]
     for t in reversed(range(frames)):
         carried = source_ref[t] + carried
         dmix = dpool_ref[...] * slope_ref[t]
         dinput_ref[t] = (carried + skip_ref[0] * dmix).astype(BF16)
-        carried = decays_ref[0, t : t + 1] * carried
+        carried = decay_of(decays_ref, t) * carried
     carry_ref[...] = carried
-    add_weight_product(cols_ref, dinput_ref[...], acc_ref)
+    add_weight_product((cols_a, cols_b), dinput_ref[...], acc_ref)
 
     @pl.when(step == pl.num_programs(0) - 1)
     def _():
@@ -226,8 +261,8 @@
 
 
 class Plan:
-    def __init__(self, steps, frames, side, channels):
-        self.steps, self.frames, self.side, self.channels = steps, frames, side, channels
+    def __init__(self, senders, group, side, channels):
+        self.steps, self.frames, self.group, self.side, self.channels = senders // 2, 2 * group, group, side, channels
         self.map = (side // 2, 2, side, channels)
 
     def whole(self, shape):
@@ -242,10 +277,10 @@
 
     def got(self, rows, back=False):
         at = self.order(back)
-        return pl.BlockSpec((1, rows, self.channels), lambda i, place: (at(i), 0, 0))
+        return pl.BlockSpec((2, rows, self.channels), lambda i, place: (at(i), 0, 0))
 
     def decays(self, back=False):
-        return self.got(self.frames, back)
+        return self.got(self.group, back)
 
     def of_view(self, rows):
         return pl.BlockSpec((1, rows, self.channels), lambda i, place: (place[1], 0, 0))
@@ -257,13 +292,13 @@
         return jax.ShapeDtypeStruct(self.map, F32)
 
     def decays_of(self):
-        return jax.ShapeDtypeStruct((self.steps, self.frames, self.channels), F32)
+        return jax.ShapeDtypeStruct((2 * self.steps, self.group, self.channels), F32)
 
     def grad_of(self):
         return jax.ShapeDtypeStruct((9 * self.channels, self.channels), F32)
 
     def cols(self):
-        return pltpu.VMEM((self.frames, self.side // 2 + 1, 2, self.side, 3 * self.channels), BF16)
+        return [pltpu.VMEM((self.group, self.side // 2 + 1, 2, self.side, 3 * self.channels), BF16)] * 2
 
     def carry(self):
         return pltpu.VMEM(self.map, F32)
@@ -291,7 +326,7 @@
                 scratch_shapes=scratch,
             ),
             cost_estimate=pl.CostEstimate(flops=2 * work, transcendentals=0, bytes_accessed=4 * cells * self.channels),
-            compiler_params=pltpu.CompilerParams(dimension_semantics=("arbitrary",), vmem_limit_bytes=16 << 20),
+            compiler_params=pltpu.CompilerParams(dimension_semantics=("arbitrary",), vmem_limit_bytes=24 << 20),
         )
 
 
@@ -310,23 +345,51 @@
     return lax.all_to_all(jnp.broadcast_to(x[None], (peers, *x.shape)), axes, 0, 0, tiled=True)
 
 
-def in_parts(x):
-    high = lax.reduce_precision(x, 8, 7)
-    middle = lax.reduce_precision(x - high, 8, 7)
-    low = x - high - middle
-    return jnp.concatenate([high, middle, low], axis=-2).astype(jnp.bfloat16)
-
-
-def clips_to_devices(rgb_maps, flow_maps, decay, half):
+def in_hbm(x):
+    return pltpu.with_memory_space_constraint(x, pltpu.HBM)
+
+
+def pack_kernel(place_ref, rgb_ref, flow_ref, decay_ref, sent_ref):
+    view = pl.program_id(0)
+    frames, channels = decay_ref.shape[1:]
+    cells = rgb_ref.shape[1] * rgb_ref.shape[2] * rgb_ref.shape[3]
+
+    @pl.when(view == 0)
+    def _():
+        sent_ref[0, :cells] = rgb_ref[...].reshape(cells, channels)
+
+    @pl.when(view == 1)
+    def _():
+        sent_ref[0, :cells] = flow_ref[...].reshape(cells, channels)
+
+    decays = decay_ref[view]
+    high = decays.astype(BF16).astype(F32)
+    middle = (decays - high).astype(BF16).astype(F32)
+    low = decays - high - middle
+    rows = sent_ref.shape[1] - cells
+    parts = [high, middle, low, jnp.zeros((rows - 3 * frames, channels), F32)]
+    sent_ref[0, cells:] = jnp.concatenate(parts).astype(BF16)
+
+
+def clips_to_devices(rgb_maps, flow_maps, decay, place):
     clips, frames, side, _, channels = rgb_maps.shape
-    straight = half == 0
-    first = jnp.where(straight, rgb_maps, flow_maps)
-    second = jnp.where(straight, flow_maps, rgb_maps)
-    pieces = jnp.stack([first, second]).reshape(2, clips, frames * side * side, channels)
-    parts = in_parts(jnp.where(straight, decay, decay[::-1]))
-    parts = jnp.pad(parts, ((0, 0), (0, 16 - 3 * frames), (0, 0)))
-    parts = jnp.broadcast_to(parts[:, None], (2, clips, 16, channels))
-    sent = jnp.concatenate([pieces, parts], axis=2).reshape(2 * clips, -1, channels)
+    rows = frames * side * side + 16
+    block = (1, *rgb_maps.shape[1:])
+    sent = pl.pallas_call(
+        pack_kernel,
+        out_shape=pltpu.HBM((2 * clips, rows, channels), BF16),
+        grid_spec=pltpu.PrefetchScalarGridSpec(
+            num_scalar_prefetch=1,
+            grid=(2, clips),
+            in_specs=[
+                pl.BlockSpec(block, lambda v, c, place: (jnp.where(v == 0, c, clips - 1), 0, 0, 0, 0)),
+                pl.BlockSpec(block, lambda v, c, place: (jnp.where(v == 0, 0, c), 0, 0, 0, 0)),
+                pl.BlockSpec(decay.shape, lambda v, c, place: (0, 0, 0)),
+            ],
+            out_specs=pl.BlockSpec((1, rows, channels), lambda v, c, place: ((v ^ place[0]) * clips + c, 0, 0)),
+        ),
+        compiler_params=pltpu.CompilerParams(vmem_limit_bytes=16 << 20),
+    )(place, in_hbm(rgb_maps), in_hbm(flow_maps), decay)
     return lax.all_to_all(sent, TIME, 0, 0, tiled=True)
 
 
@@ -346,9 +409,14 @@
     return lax.dot_general(a, b, (((1,), (1,)), ((), ())), preferred_element_type=F32, **kinds)
 
 
-def projector_kernel(place_ref, seen_ref, in_ref, gain_ref, out_ref, dpool_ref, x_ref, n_ref, z_ref, zn_ref, *, cell_count):
+def projector_kernel(place_ref, seen_ref, in_ref, gain_ref, far_ref, dpool_ref, x_ref, n_ref, z_ref, zn_ref, out_ref, sems, *, cell_count):
     view, row = place_ref[1], place_ref[4]
     clips = seen_ref.shape[1]
+    chunk = out_ref.shape[1] // CHUNKS
+    columns = [slice(j * chunk, (j + 1) * chunk) for j in range(CHUNKS)]
+    copies = [pltpu.make_async_copy(far_ref.at[:, c], out_ref.at[:, c], sems.at[j]) for j, c in enumerate(columns)]
+    for copy in copies:
+        copy.start()
     gain = gain_ref[...]
     pooled = jnp.concatenate([seen_ref[0] + seen_ref[3], seen_ref[1] + seen_ref[2]]) / cell_count
     hidden = jnp.dot(pooled, in_ref[...], precision=HIGHEST, preferred_element_type=F32)
@@ -358,12 +426,16 @@
         n_ref[v] = x_ref[v] * gain
         hidden_s.append(scale)
         relus.append(jnp.maximum(n_ref[v], 0.0).astype(BF16))
-    z = jnp.dot(jnp.concatenate(relus), out_ref[...], preferred_element_type=F32)
-    z_s = []
-    for v in range(2):
-        z_ref[v], scale = batch_norm(z[v * clips : (v + 1) * clips])
-        zn_ref[v] = z_ref[v].astype(BF16)
-        z_s.append(scale)
+    relu_b = jnp.concatenate(relus)
+    scales = []
+    for copy, c in zip(copies, columns):
+        copy.wait()
+        z = jnp.dot(relu_b, out_ref[:, c], preferred_element_type=F32)
+        for v in range(2):
+            z_ref[v, :, c], scale = batch_norm(z[v * clips : (v + 1) * clips])
+            zn_ref[v, :, c] = z_ref[v, :, c].astype(BF16)
+            scales.append(scale)
+    z_s = [jnp.concatenate(scales[v::2], axis=1) for v in range(2)]
     first = view == 0
     own, other = zn_ref[view].astype(F32), zn_ref[1 - view].astype(F32)
     corr_diag = jnp.sum(own * other, axis=0, keepdims=True) / clips
@@ -387,11 +459,20 @@
     return pl.pallas_call(
         functools.partial(projector_kernel, cell_count=cell_count),
         out_shape=jax.ShapeDtypeStruct((1, channels), F32),
-        in_specs=[pl.BlockSpec(memory_space=pltpu.SMEM)] + [pl.BlockSpec(memory_space=pltpu.VMEM)] * 4,
-        scratch_shapes=[pltpu.VMEM(wide, F32), pltpu.VMEM(wide, F32), pltpu.VMEM(wide, F32), pltpu.VMEM(wide, BF16)],
+        in_specs=[pl.BlockSpec(memory_space=pltpu.SMEM)]
+        + [pl.BlockSpec(memory_space=pltpu.VMEM)] * 3
+        + [pl.BlockSpec(memory_space=pltpu.HBM)],
+        scratch_shapes=[
+            pltpu.VMEM(wide, F32),
+            pltpu.VMEM(wide, F32),
+            pltpu.VMEM(wide, F32),
+            pltpu.VMEM(wide, BF16),
+            pltpu.VMEM(proj_out.shape, BF16),
+            pltpu.SemaphoreType.DMA((CHUNKS,)),
+        ],
         cost_estimate=pl.CostEstimate(flops=6 * clips * width * width, transcendentals=0, bytes_accessed=2 * width * width),
         compiler_params=pltpu.CompilerParams(vmem_limit_bytes=26 << 20),
-    )(place, seen, proj_in, proj_gain.reshape(1, width), proj_out)
+    )(place, seen, proj_in, proj_gain.reshape(1, width), in_hbm(proj_out))
 
 
 def from_other_half(x):
@@ -453,15 +534,15 @@
     half = lax.axis_index("xh")
     view = lax.axis_index("xl") ^ half
     _, frames_here, side, _, channels = rgb_maps.shape
-    got = clips_to_devices(rgb_maps, flow_maps, decay, half)
-    steps, rows, _ = got.shape
-    cell_count = 2 * steps * frames_here * side * side
-    plan = Plan(steps, frames_here, side, channels)
+    place = jnp.stack([half, view, lax.axis_index("core"), lax.axis_index("z"), lax.axis_index(("y", "z", "core"))])
+    place = place.astype(jnp.int32)
+    got = clips_to_devices(rgb_maps, flow_maps, decay, place)
+    senders, rows, _ = got.shape
+    cell_count = 2 * senders * frames_here * side * side
+    plan = Plan(senders, frames_here, side, channels)
     taps = in_weights.shape[1]
     weights = plan.of_view(taps)
     skips = skip.reshape(2, 1, channels)
-    place = jnp.stack([half, view, lax.axis_index("core"), lax.axis_index("z"), lax.axis_index(("y", "z", "core"))])
-    place = place.astype(jnp.int32)
     carry_spec = plan.whole(plan.map)
 
     inputs, decays, end = plan.call(
@@ -469,15 +550,15 @@
         [plan.got(rows), weights],
         [plan.maps_of(BF16), plan.decays_of(), plan.carry_of()],
         [plan.maps(), plan.decays(), carry_spec],
-        [plan.cols(), plan.both(), plan.carry()],
+        [*plan.cols(), plan.both(), plan.carry()],
     )(place, got, in_weights)
     income = from_other_half(end)
     states_b, slope, pooled_part = plan.call(
         mixed_kernel,
         [plan.maps(), plan.decays(), carry_spec, plan.of_view(1), weights],
-        [plan.maps_of(BF16), plan.maps_of(F32), jax.ShapeDtypeStruct((1, channels), F32)],
+        [pltpu.HBM(a.shape, a.dtype) for a in (plan.maps_of(BF16), plan.maps_of(F32))] + [jax.ShapeDtypeStruct((1, channels), F32)],
         [plan.maps(), plan.maps(), plan.row()],
-        [plan.cols(), plan.both(), plan.carry(), pltpu.VMEM((side, channels), F32)],
+        [*plan.cols(), plan.both(), plan.carry(), pltpu.VMEM((side, channels), F32)],
     )(place, inputs, decays, income, skips, out_weights)
 
     seen = from_all(from_cores(pooled_part[0]), ("xh", "xl", "y", "z"))
@@ -488,7 +569,7 @@
         [plan.maps(True), plan.decays(True), plan.row(), weights],
         [plan.maps_of(BF16), plan.maps_of(F32), plan.carry_of()],
         [plan.maps(True), plan.maps(True), carry_spec],
-        [plan.cols(), plan.both(), plan.carry()],
+        [*plan.cols(), plan.both(), plan.carry()],
     )(place, slope, decays, dpool, out_weights)
     income = from_other_half(end)
     out_grad = plan.call(
@@ -496,14 +577,14 @@
         [plan.maps(), plan.maps()],
         plan.grad_of(),
         plan.whole((9 * channels, channels)),
-        [plan.cols(), plan.acc()],
+        [*plan.cols(), plan.acc()],
     )(place, states_b, dmix_b)
     in_grad = plan.call(
         in_grad_kernel,
         [plan.got(rows, True), plan.maps(True), plan.maps(True), plan.decays(True), carry_spec, plan.row(), plan.of_view(1)],
         plan.grad_of(),
         plan.whole((9 * channels, channels)),
-        [plan.cols(), plan.carry(), pltpu.VMEM((frames_here, *plan.map), BF16), plan.acc()],
+        [*plan.cols(), plan.carry(), pltpu.VMEM((plan.frames, *plan.map), BF16), plan.acc()],
     )(place, got, slope, source, decays, income, dpool, skips)
     return summed([in_grad, out_grad], place)
 

time: 153 us -> 151 us (0.987)
  blocking collectives: 0 us -> 32.6 us
  waiting for transfers between devices: 50.4 us -> 24.3 us
  Pallas kernels: 41.4 us -> 48.9 us
  starting transfers between devices: 48.6 us -> 42.1 us
  local copies, waits for them, and re-layouts: 7.52 us -> 1.48 us
  other arithmetic: 4.26 us -> 0.29 us
    all_to_all x0 -> x1, blocking collectives: none -> 32.6 us  [clips_to_devices(): return lax.all_to_all(sent, TIME, 0, 0, tiled=True)]
    all_to_all x1 -> x0, waiting for transfers between devices: 26.5 us -> none  [clips_to_devices(): return lax.all_to_all(sent, TIME, 0, 0, tiled=True)]
    pallas_call x0 -> x1, Pallas kernels: none -> 6.4 us  [clips_to_devices(): pl.pallas_call(pack_kernel, out_shape=pltpu.HBM((2 * clips, rows, channel...]
    all_to_all x1 -> x0, starting transfers between devices: 6.07 us -> none  [clips_to_devices(): return lax.all_to_all(sent, TIME, 0, 0, tiled=True)]
    unnamed x22 -> x18, local copies, waits for them, and re-layouts: 6.76 us -> 0.72 us
    pallas_call x1, Pallas kernels: 6.58 us -> 8.71 us  [projector_back(): pl.pallas_call(functools.partial(projector_kernel, cell_count=cell_count)...]
    select_n x1 -> x0, other arithmetic: 1.68 us -> none  [clips_to_devices(): first = jnp.where(straight, rgb_maps, flow_maps)]
    ppermute x6, starting transfers between devices: 14 us -> 15.7 us  [swapped(): return lax.ppermute(x, 'core', [(0, 1), (1, 0)])]
  transfers between devices with their start and end apart: 22 -> 21, of which waited for: 13 -> 12; matrix products, arithmetic and copies ran while one was open for 0% -> 0% of each run, Pallas kernels for 4% -> 4%
where the time goes in v3:
time: 151 us; the launch traced here: 150 us
  Pallas kernels  48.9 us (32%)
  starting transfers between devices  42.1 us (28%)
  blocking collectives  32.6 us (22%)
  waiting for transfers between devices  24.3 us (16%)
    all_to_all x1, blocking collectives, clips_to_devices(): return lax.all_to_all(sent, TIME, 0, 0, tiled=True)  32.6 us
    ppermute x12, starting transfers between devices, from_peer(): return lax.ppermute(x, axes, [(i, i ^ k) for i in range(4)])  15.7 us
    ppermute x6, starting transfers between devices, swapped(): return lax.ppermute(x, 'core', [(0, 1), (1, 0)])  15.7 us
    ppermute x12, waiting for transfers between devices, from_peer(): return lax.ppermute(x, axes, [(i, i ^ k) for i in range(4)])  8.99 us
    pallas_call x1, Pallas kernels, projector_back(): pl.pallas_call(functools.partial(projector_kernel, cell_count=cell_count)...  8.71 us
    all_to_all x1, waiting for transfers between devices, from_all(): lax.all_to_all(jnp.broadcast_to(x[None], (peers, *x.shape)), axes, 0, 0,...  8.46 us
    all_to_all x1, starting transfers between devices, from_all(): lax.all_to_all(jnp.broadcast_to(x[None], (peers, *x.shape)), axes, 0, 0,...  7.95 us
    pallas_call x1, Pallas kernels, per_device(): plan.call(mixed_kernel, [plan.maps(), plan.decays(), carry_spec, plan.of_...  7.94 us
  transfers between devices with their start and end apart: 21, of which 12 were waited for; matrix products, arithmetic and copies ran while one was open for 0% of the time, Pallas kernels for 4%

profile of v3, /device:TPU:1, one launch (start us, length us, event | category | flops | bytes accessed | tf_op | source)
XLA Modules:
  0.0 150.5 jit_solution(8825205975680539977)
XLA Ops:
  1.4 6.4 %shard_map.104 = bf16[8,1040,128]{2,1,0:T(8,128)(2,1)} custom-call(s32[5]{0:T(128)S(1)} %stack.53.place_ref, bf16[4,4,16,16,128]{4,3,2,1,0:T(8,128)(2,1)} %rgb_ref.1, bf16[4,4,16,16,128]{4,3,2,1,0:T(8,128)(2,1)} %flow_ref.1, f32[2,4,128]{2,1,0:T(4,128)S(1)} %copy-done.2), custom_call_target="tpu_custom_call" | custom-call | tf_op jit(solution)/shard_map/pallas_call | solution.py:378
  7.8 32.6 %all_to_all.10.got_ref = bf16[8,1040,128]{2,1,0:T(8,128)(2,1)S(1)} all-to-all(bf16[8,1040,128]{2,1,0:T(8,128)(2,1)} %shard_map.104), channel_id=1, replica_groups=mesh['xh'=2,'xl'=2,'y'=4,'z'=4,'core'=2] {'xl','y'}, dimensions={0} | all-to-all | bytes 4259840 | tf_op jit(solution)/shard_map/all_to_all | solution.py:393
  40.5 5.2 %shard_map.105 = (bf16[32,8,2,16,128]{4,3,2,1,0:T(8,128)(2,1)S(1)}, f32[8,4,128]{2,1,0:T(4,128)S(1)}, f32[8,2,16,128]{3,2,1,0:T(8,128)S(1)}) custom-call(s32[5]{0:T(128)S(1)} %stack.53.place_ref, bf16[8,1040,128]{2,1,0:T(8,128)(2,1)S(1)} %all_to_all.10.got_ref, bf16[2,1152,128]{2,1,0:T(8,128)(2,1)S(1)} %copy-done.3), custom_call_target="tpu_custom_call" | custom-call | flops 4831838208 | bytes 4194304 | tf_op jit(solution)/shard_map/pallas_call | solution.py:548
  45.7 1.7 %collective-permute-start = (f32[8,2,16,128]{3,2,1,0:T(8,128)S(1)}, f32[8,2,16,128]{3,2,1,0:T(8,128)S(1)}, u32[]{:S(2)}, u32[]{:S(2)}) collective-permute-start(f32[8,2,16,128]{3,2,1,0:T(8,128)S(1)} %get-tuple-element.13), channel_id=1, source_target_pairs={{0,96},{32,64},{64,32},{96,0},{1,97},{33,65},{65,33},{97,1},{2,98}... | collective-permute-start | bytes 393224 | tf_op jit(solution)/shard_map/ppermute | solution.py:479
  47.4 3.4 %collective-permute-done.income_ref = f32[8,2,16,128]{3,2,1,0:T(8,128)S(1)} collective-permute-done((f32[8,2,16,128]{3,2,1,0:T(8,128)S(1)}, f32[8,2,16,128]{3,2,1,0:T(8,128)S(1)}, u32[]{:S(2)}, u32[]{:S(2)}) %collective-permute-start) | collective-permute-done | bytes 131104 | tf_op jit(solution)/shard_map/ppermute | solution.py:479
  50.8 7.9 %shard_map.106 = (bf16[32,8,2,16,128]{4,3,2,1,0:T(8,128)(2,1)}, f32[32,8,2,16,128]{4,3,2,1,0:T(8,128)}, f32[1,128]{1,0:T(1,128)S(1)}) custom-call(s32[5]{0:T(128)S(1)} %stack.53.place_ref, bf16[32,8,2,16,128]{4,3,2,1,0:T(8,128)(2,1)S(1)} %get-tuple-element.11.inputs_ref, f32[8,4,128]{2,1,0:T(4,128)S(1)} %get-tuple-element.12.decays_ref, ...), custom_call_target="tpu_custom_call" | custom-call | flops 4831838208 | bytes 4194304 | tf_op jit(solution)/shard_map/pallas_call | solution.py:556
  58.8 3.3 %collective-permute-start.1 = (f32[128]{0:T(128)S(1)}, f32[128]{0:T(128)S(1)}, u32[]{:S(2)}, u32[]{:S(2)}) collective-permute-start(f32[128]{0:T(128)S(1)} %bitcast.50), channel_id=1, source_target_pairs={{0,1},{1,0},{2,3},{3,2},{4,5},{5,4},{6,7},{7,6},{8,9},{9,8},{10,11... | collective-permute-start | bytes 1544 | tf_op jit(solution)/shard_map/ppermute | solution.py:334
  63.6 7.9 %all-to-all-start.1 = ((f32[64,2,128]{2,1,0:T(2,128)}), f32[64,2,128]{2,1,0:T(2,128)S(1)}, u32[]{:S(2)}, u32[]{:S(2)}) async-start(f32[64,2,128]{2,1,0:T(2,128)} %broadcast_in_dim.2), calls=%async_computation.1 | async-start | bytes 131072 | tf_op jit(solution)/shard_map/all_to_all | solution.py:345
  71.5 8.5 %all-to-all-done.1 = f32[64,2,128]{2,1,0:T(2,128)S(1)} async-done(((f32[64,2,128]{2,1,0:T(2,128)}), f32[64,2,128]{2,1,0:T(2,128)S(1)}, u32[]{:S(2)}, u32[]{:S(2)}) %all-to-all-start.1) | async-done | bytes 65568 | tf_op jit(solution)/shard_map/all_to_all | solution.py:345
  80.0 8.7 %shard_map.107.dpool_ref = f32[1,128]{1,0:T(1,128)S(1)} custom-call(s32[5]{0:T(128)S(1)} %stack.53.place_ref, f32[4,32,128]{2,1,0:T(8,128)S(1)} %bitcast.48, f32[128,2048]{1,0:T(8,128)S(1)} %copy-done, f32[1,2048]{1,0:T(1,128)S(1)} %bitcast.49, bf16[2048,2048]{1,0:T(8,128)(2,1)} %far_ref.1), custom_call_target="tpu_custom_call" | custom-call | flops 805306368 | bytes 8388608 | tf_op jit(solution)/shard_map/pallas_call | solution.py:459
  88.8 5.8 %shard_map.108 = (bf16[32,8,2,16,128]{4,3,2,1,0:T(8,128)(2,1)S(1)}, f32[32,8,2,16,128]{4,3,2,1,0:T(8,128)S(1)}, f32[8,2,16,128]{3,2,1,0:T(8,128)S(1)}) custom-call(s32[5]{0:T(128)S(1)} %stack.53.place_ref, f32[32,8,2,16,128]{4,3,2,1,0:T(8,128)S(1)} %copy-done.7, f32[8,4,128]{2,1,0:T(4,128)S(1)} %get-tuple-element.12.decays_ref, ...), custom_call_target="tpu_custom_call" | custom-call | flops 4831838208 | bytes 4194304 | tf_op jit(solution)/shard_map/pallas_call | solution.py:567
  95.6 5.7 %shard_map.110 = f32[1152,128]{1,0:T(8,128)S(1)} custom-call(s32[5]{0:T(128)S(1)} %stack.53.place_ref, bf16[32,8,2,16,128]{4,3,2,1,0:T(8,128)(2,1)S(1)} %copy-done.8, bf16[32,8,2,16,128]{4,3,2,1,0:T(8,128)(2,1)S(1)} %get-tuple-element.19.dmix_ref), custom_call_target="tpu_custom_call" | custom-call | flops 4831838208 | bytes 4194304 | tf_op jit(solution)/shard_map/pallas_call | solution.py:575
  101.3 7.0 %shard_map.109 = f32[1152,128]{1,0:T(8,128)S(1)} custom-call(s32[5]{0:T(128)S(1)} %stack.53.place_ref, bf16[8,1040,128]{2,1,0:T(8,128)(2,1)S(1)} %all_to_all.10.got_ref, f32[32,8,2,16,128]{4,3,2,1,0:T(8,128)S(1)} %copy-done.7, f32[32,8,2,16,128]{4,3,2,1,0:T(8,128)S(1)} %get-tuple-element.16.source_ref, f32[8,4,128]{2,1,0:T(4,128)S(1)} %get-tuple-element.12.decays_ref, ...), custom_call_target="tpu_custom_call" | custom-call | flops 4831838208 | bytes 4194304 | tf_op jit(solution)/shard_map/pallas_call | solution.py:582
  108.4 2.1 %collective-permute-start.3 = (f32[2,4,144,128]{3,2,0,1:T(8,128)S(1)}, f32[2,4,144,128]{3,2,0,1:T(8,128)S(1)}, u32[]{:S(2)}, u32[]{:S(2)}) collective-permute-start(f32[2,4,144,128]{3,2,0,1:T(8,128)S(1)} %fusion.1), channel_id=1, source_target_pairs={{0,1},{1,0},{2,3},{3,2},{4,5},{5,4},{6,7},{7,6},{8,9},{9,8},{10,11... | collective-permute-start | bytes 1769480 | tf_op jit(solution)/shard_map/ppermute | solution.py:334
  110.4 1.6 %collective-permute-done.3 = f32[2,4,144,128]{3,2,0,1:T(8,128)S(1)} collective-permute-done((f32[2,4,144,128]{3,2,0,1:T(8,128)S(1)}, f32[2,4,144,128]{3,2,0,1:T(8,128)S(1)}, u32[]{:S(2)}, u32[]{:S(2)}) %collective-permute-start.3) | collective-permute-done | bytes 589856 | tf_op jit(solution)/shard_map/ppermute | solution.py:334
  112.5 1.9 %collective-permute-start.5 = (bf16[2,144,128]{2,1,0:T(8,128)(2,1)S(1)}, bf16[2,144,128]{2,1,0:T(8,128)(2,1)S(1)}, u32[]{:S(2)}, u32[]{:S(2)}) collective-permute-start(bf16[2,144,128]{2,1,0:T(8,128)(2,1)S(1)} %get-tuple-element.22), channel_id=1, source_target_pairs={{0,4},{2,6},{4,0},{6,2},{1,5},{3,7},{5,1},{7,3},{8,12},{10,14},{12... | collective-permute-start | bytes 221192 | tf_op jit(solution)/shard_map/ppermute | solution.py:483
  114.4 1.7 %collective-permute-start.6 = (bf16[2,144,128]{2,1,0:T(8,128)(2,1)S(1)}, bf16[2,144,128]{2,1,0:T(8,128)(2,1)S(1)}, u32[]{:S(2)}, u32[]{:S(2)}) collective-permute-start(bf16[2,144,128]{2,1,0:T(8,128)(2,1)S(1)} %get-tuple-element.21), channel_id=1, source_target_pairs={{0,6},{2,4},{4,2},{6,0},{1,7},{3,5},{5,3},{7,1},{8,14},{10,12},{12... | collective-permute-start | bytes 221192 | tf_op jit(solution)/shard_map/ppermute | solution.py:483
  116.1 2.2 %collective-permute-done.5 = bf16[2,144,128]{2,1,0:T(8,128)(2,1)S(1)} collective-permute-done((bf16[2,144,128]{2,1,0:T(8,128)(2,1)S(1)}, bf16[2,144,128]{2,1,0:T(8,128)(2,1)S(1)}, u32[]{:S(2)}, u32[]{:S(2)}) %collective-permute-start.5) | collective-permute-done | bytes 73760 | tf_op jit(solution)/shard_map/ppermute | solution.py:483
  118.3 1.1 collective-permute-done.6
  119.8 1.8 %collective-permute-start.8 = (bf16[2,144,128]{2,1,0:T(8,128)(2,1)S(1)}, bf16[2,144,128]{2,1,0:T(8,128)(2,1)S(1)}, u32[]{:S(2)}, u32[]{:S(2)}) collective-permute-start(bf16[2,144,128]{2,1,0:T(8,128)(2,1)S(1)} %fusion.8), channel_id=1, source_target_pairs={{0,16},{8,24},{16,0},{24,8},{1,17},{9,25},{17,1},{25,9},{2,18},{10... | collective-permute-start | bytes 221192 | tf_op jit(solution)/shard_map/ppermute | solution.py:483
  121.6 1.7 %collective-permute-start.9 = (bf16[2,144,128]{2,1,0:T(8,128)(2,1)S(1)}, bf16[2,144,128]{2,1,0:T(8,128)(2,1)S(1)}, u32[]{:S(2)}, u32[]{:S(2)}) collective-permute-start(bf16[2,144,128]{2,1,0:T(8,128)(2,1)S(1)} %fusion.8), channel_id=1, source_target_pairs={{0,24},{8,16},{16,8},{24,0},{1,25},{9,17},{17,9},{25,1},{2,26},{10... | collective-permute-start | bytes 221192 | tf_op jit(solution)/shard_map/ppermute | solution.py:483
  123.4 1.2 collective-permute-done.8
  124.6 1.5 collective-permute-done.9
  126.1 2.3 %collective-permute-start.10 = (bf16[2,144,128]{2,1,0:T(8,128)(2,1)S(1)}, bf16[2,144,128]{2,1,0:T(8,128)(2,1)S(1)}, u32[]{:S(2)}, u32[]{:S(2)}) collective-permute-start(bf16[2,144,128]{2,1,0:T(8,128)(2,1)S(1)} %add_convert_fusion.2), channel_id=1, source_target_pairs={{0,96},{32,64},{64,32},{96,0},{1,97},{33,65},{65,33},{97,1},{2,98}... | collective-permute-start | bytes 221192 | tf_op jit(solution)/shard_map/ppermute | solution.py:483
  128.4 1.6 %collective-permute-start.12 = (bf16[2,144,128]{2,1,0:T(8,128)(2,1)S(1)}, bf16[2,144,128]{2,1,0:T(8,128)(2,1)S(1)}, u32[]{:S(2)}, u32[]{:S(2)}) collective-permute-start(bf16[2,144,128]{2,1,0:T(8,128)(2,1)S(1)} %add_convert_fusion.2), channel_id=1, source_target_pairs={{0,64},{32,96},{64,0},{96,32},{1,65},{33,97},{65,1},{97,33},{2,66}... | collective-permute-start | bytes 221192 | tf_op jit(solution)/shard_map/ppermute | solution.py:483
  131.6 1.5 %collective-permute-done.12 = bf16[2,144,128]{2,1,0:T(8,128)(2,1)S(1)} collective-permute-done((bf16[2,144,128]{2,1,0:T(8,128)(2,1)S(1)}, bf16[2,144,128]{2,1,0:T(8,128)(2,1)S(1)}, u32[]{:S(2)}, u32[]{:S(2)}) %collective-permute-start.12) | collective-permute-done | bytes 73760 | tf_op jit(solution)/shard_map/ppermute | solution.py:483
  133.2 2.5 %collective-permute-start.14 = (bf16[2,2,144,128]{3,2,1,0:T(8,128)(2,1)S(1)}, bf16[2,2,144,128]{3,2,1,0:T(8,128)(2,1)S(1)}, u32[]{:S(2)}, u32[]{:S(2)}) collective-permute-start(bf16[2,2,144,128]{3,2,1,0:T(8,128)(2,1)S(1)} %pad_maximum_fusion.refs_0_), channel_id=1, source_target_pairs={{0,4},{2,6},{4,0},{6,2},{1,5},{3,7},{5,1},{7,3},{8,12},{10,14},{12... | collective-permute-start | bytes 442376 | tf_op jit(solution)/shard_map/ppermute | solution.py:483
  135.7 1.4 collective-permute-start.15
  137.1 5.2 %collective-permute-start.16 = (bf16[2,2,144,128]{3,2,1,0:T(8,128)(2,1)S(1)}, bf16[2,2,144,128]{3,2,1,0:T(8,128)(2,1)S(1)}, u32[]{:S(2)}, u32[]{:S(2)}) collective-permute-start(bf16[2,2,144,128]{3,2,1,0:T(8,128)(2,1)S(1)} %pad_maximum_fusion.refs_0_), channel_id=1, source_target_pairs={{0,1},{1,0},{2,3},{3,2},{4,5},{5,4},{6,7},{7,6},{8,9},{9,8},{10,11... | collective-permute-start | bytes 442376 | tf_op jit(solution)/shard_map/ppermute | solution.py:334
  142.8 3.0 %collective-permute-start.18 = (bf16[2,2,144,128]{3,2,1,0:T(8,128)(2,1)S(1)}, bf16[2,2,144,128]{3,2,1,0:T(8,128)(2,1)S(1)}, u32[]{:S(2)}, u32[]{:S(2)}) collective-permute-start(bf16[2,2,144,128]{3,2,1,0:T(8,128)(2,1)S(1)} %collective-permute-done.14.refs_2_), channel_id=1, source_target_pairs={{0,1},{1,0},{2,3},{3,2},{4,5},{5,4},{6,7},{7,6},{8,9},{9,8},{10,11... | collective-permute-start | bytes 442376 | tf_op jit(solution)/shard_map/ppermute | solution.py:334
  145.7 1.7 %collective-permute-start.19 = (bf16[2,2,144,128]{3,2,1,0:T(8,128)(2,1)S(1)}, bf16[2,2,144,128]{3,2,1,0:T(8,128)(2,1)S(1)}, u32[]{:S(2)}, u32[]{:S(2)}) collective-permute-start(bf16[2,2,144,128]{3,2,1,0:T(8,128)(2,1)S(1)} %collective-permute-done.15.refs_3_), channel_id=1, source_target_pairs={{0,1},{1,0},{2,3},{3,2},{4,5},{5,4},{6,7},{7,6},{8,9},{9,8},{10,11... | collective-permute-start | bytes 442376 | tf_op jit(solution)/shard_map/ppermute | solution.py:334
  148.4 2.1 %shard_map.111 = (f32[2,1152,128]{2,1,0:T(8,128)}, f32[2,1152,128]{2,1,0:T(8,128)}) custom-call(s32[5]{0:T(128)S(1)} %stack.53.place_ref, bf16[2,2,144,128]{3,2,1,0:T(8,128)(2,1)S(1)} %pad_maximum_fusion.refs_0_, bf16[2,2,144,128]{3,2,1,0:T(8,128)(2,1)S(1)} %collective-permute-done.13.refs_1_, bf16[2,2,144,128]{3,2,1,0:T(8,128)(2,1)S(1)} %collective-permute-done.14.refs_2_, ...), custom_call_target="tpu_custom_call" | custom-call | tf_op jit(solution)/shard_map/pallas_call | solution.py:522
  (49 shorter events, 7.5 us)
Async XLA Ops:
  0.7 0.7 copy-start.2
  7.8 32.6 %copy-start.3 = (bf16[2,1152,128]{2,1,0:T(8,128)(2,1)S(1)}, bf16[2,1152,128]{2,1,0:T(8,128)(2,1)}, u32[]{:S(2)}) copy-start(bf16[2,1152,128]{2,1,0:T(8,128)(2,1)} %weights_ref.3) | copy-start | bytes 1769476
  40.5 10.3 %copy-start.4 = (bf16[2,1152,128]{2,1,0:T(8,128)(2,1)S(1)}, bf16[2,1152,128]{2,1,0:T(8,128)(2,1)}, u32[]{:S(2)}) copy-start(bf16[2,1152,128]{2,1,0:T(8,128)(2,1)} %weights_ref.5) | copy-start | bytes 1769476
  40.5 10.3 %copy-start.6 = (f32[2,128]{1,0:T(2,128)S(1)}, f32[2,128]{1,0:T(2,128)}, u32[]{:S(2)}) copy-start(f32[2,128]{1,0:T(2,128)} %param.14) | copy-start | bytes 3076
  45.7 5.1 %collective-permute-start = (f32[8,2,16,128]{3,2,1,0:T(8,128)S(1)}, f32[8,2,16,128]{3,2,1,0:T(8,128)S(1)}, u32[]{:S(2)}, u32[]{:S(2)}) collective-permute-start(f32[8,2,16,128]{3,2,1,0:T(8,128)S(1)} %get-tuple-element.13), channel_id=1, source_target_pairs={{0,96},{32,64},{64,32},{96,0},{1,97},{33,65},{65,33},{97,1},{2,98}... | collective-permute-start | bytes 393224 | tf_op jit(solution)/shard_map/ppermute | solution.py:479
  50.8 29.2 %copy-start = (f32[128,2048]{1,0:T(8,128)S(1)}, f32[128,2048]{1,0:T(8,128)}, u32[]{:S(2)}) copy-start(f32[128,2048]{1,0:T(8,128)} %in_ref.1) | copy-start | bytes 3145732
  50.8 29.2 %copy-start.1 = (f32[2048]{0:T(1024)S(1)}, f32[2048]{0:T(1024)}, u32[]{:S(2)}) copy-start(f32[2048]{0:T(1024)} %param.16) | copy-start | bytes 24580
  58.8 4.2 %collective-permute-start.1 = (f32[128]{0:T(128)S(1)}, f32[128]{0:T(128)S(1)}, u32[]{:S(2)}, u32[]{:S(2)}) collective-permute-start(f32[128]{0:T(128)S(1)} %bitcast.50), channel_id=1, source_target_pairs={{0,1},{1,0},{2,3},{3,2},{4,5},{5,4},{6,7},{7,6},{8,9},{9,8},{10,11... | collective-permute-start | bytes 1544 | tf_op jit(solution)/shard_map/ppermute | solution.py:334
  63.6 16.4 %all-to-all-start.1 = ((f32[64,2,128]{2,1,0:T(2,128)}), f32[64,2,128]{2,1,0:T(2,128)S(1)}, u32[]{:S(2)}, u32[]{:S(2)}) async-start(f32[64,2,128]{2,1,0:T(2,128)} %broadcast_in_dim.2), calls=%async_computation.1 | async-start | bytes 131072 | tf_op jit(solution)/shard_map/all_to_all | solution.py:345
  80.0 8.7 %copy-start.5 = (bf16[2,1152,128]{2,1,0:T(8,128)(2,1)S(1)}, bf16[2,1152,128]{2,1,0:T(8,128)(2,1)}, u32[]{:S(2)}) copy-start(bf16[2,1152,128]{2,1,0:T(8,128)(2,1)} %weights_ref.5) | copy-start | bytes 1769476
  80.0 8.7 %copy-start.7 = (f32[32,8,2,16,128]{4,3,2,1,0:T(8,128)S(1)}, f32[32,8,2,16,128]{4,3,2,1,0:T(8,128)}, u32[]{:S(2)}) copy-start(f32[32,8,2,16,128]{4,3,2,1,0:T(8,128)} %get-tuple-element.14.slope_ref) | copy-start | bytes 12582916
  88.7 6.8 %copy-start.8 = (bf16[32,8,2,16,128]{4,3,2,1,0:T(8,128)(2,1)S(1)}, bf16[32,8,2,16,128]{4,3,2,1,0:T(8,128)(2,1)}, u32[]{:S(2)}) copy-start(bf16[32,8,2,16,128]{4,3,2,1,0:T(8,128)(2,1)} %get-tuple-element.18.states_ref) | copy-start | bytes 6291460
  94.6 6.7 %collective-permute-start.2 = (f32[8,2,16,128]{3,2,1,0:T(8,128)S(1)}, f32[8,2,16,128]{3,2,1,0:T(8,128)S(1)}, u32[]{:S(2)}, u32[]{:S(2)}) collective-permute-start(f32[8,2,16,128]{3,2,1,0:T(8,128)S(1)} %get-tuple-element.17), channel_id=1, source_target_pairs={{0,96},{32,64},{64,32},{96,0},{1,97},{33,65},{65,33},{97,1},{2,98}... | collective-permute-start | bytes 393224 | tf_op jit(solution)/shard_map/ppermute | solution.py:479
  108.4 3.7 %collective-permute-start.3 = (f32[2,4,144,128]{3,2,0,1:T(8,128)S(1)}, f32[2,4,144,128]{3,2,0,1:T(8,128)S(1)}, u32[]{:S(2)}, u32[]{:S(2)}) collective-permute-start(f32[2,4,144,128]{3,2,0,1:T(8,128)S(1)} %fusion.1), channel_id=1, source_target_pairs={{0,1},{1,0},{2,3},{3,2},{4,5},{5,4},{6,7},{7,6},{8,9},{9,8},{10,11... | collective-permute-start | bytes 1769480 | tf_op jit(solution)/shard_map/ppermute | solution.py:334
  112.2 3.9 %collective-permute-start.4 = (bf16[2,144,128]{2,1,0:T(8,128)(2,1)S(1)}, bf16[2,144,128]{2,1,0:T(8,128)(2,1)S(1)}, u32[]{:S(2)}, u32[]{:S(2)}) collective-permute-start(bf16[2,144,128]{2,1,0:T(8,128)(2,1)S(1)} %get-tuple-element.20), channel_id=1, source_target_pairs={{0,2},{2,0},{4,6},{6,4},{1,3},{3,1},{5,7},{7,5},{8,10},{10,8},{12,... | collective-permute-start | bytes 221192 | tf_op jit(solution)/shard_map/ppermute | solution.py:483
  112.5 5.7 %collective-permute-start.5 = (bf16[2,144,128]{2,1,0:T(8,128)(2,1)S(1)}, bf16[2,144,128]{2,1,0:T(8,128)(2,1)S(1)}, u32[]{:S(2)}, u32[]{:S(2)}) collective-permute-start(bf16[2,144,128]{2,1,0:T(8,128)(2,1)S(1)} %get-tuple-element.22), channel_id=1, source_target_pairs={{0,4},{2,6},{4,0},{6,2},{1,5},{3,7},{5,1},{7,3},{8,12},{10,14},{12... | collective-permute-start | bytes 221192 | tf_op jit(solution)/shard_map/ppermute | solution.py:483
  114.4 4.9 %collective-permute-start.6 = (bf16[2,144,128]{2,1,0:T(8,128)(2,1)S(1)}, bf16[2,144,128]{2,1,0:T(8,128)(2,1)S(1)}, u32[]{:S(2)}, u32[]{:S(2)}) collective-permute-start(bf16[2,144,128]{2,1,0:T(8,128)(2,1)S(1)} %get-tuple-element.21), channel_id=1, source_target_pairs={{0,6},{2,4},{4,2},{6,0},{1,7},{3,5},{5,3},{7,1},{8,14},{10,12},{12... | collective-permute-start | bytes 221192 | tf_op jit(solution)/shard_map/ppermute | solution.py:483
  119.4 3.9 %collective-permute-start.7 = (bf16[2,144,128]{2,1,0:T(8,128)(2,1)S(1)}, bf16[2,144,128]{2,1,0:T(8,128)(2,1)S(1)}, u32[]{:S(2)}, u32[]{:S(2)}) collective-permute-start(bf16[2,144,128]{2,1,0:T(8,128)(2,1)S(1)} %fusion.8), channel_id=1, source_target_pairs={{0,8},{8,0},{16,24},{24,16},{1,9},{9,1},{17,25},{25,17},{2,10},{10... | collective-permute-start | bytes 221192 | tf_op jit(solution)/shard_map/ppermute | solution.py:483
  119.8 4.7 %collective-permute-start.8 = (bf16[2,144,128]{2,1,0:T(8,128)(2,1)S(1)}, bf16[2,144,128]{2,1,0:T(8,128)(2,1)S(1)}, u32[]{:S(2)}, u32[]{:S(2)}) collective-permute-start(bf16[2,144,128]{2,1,0:T(8,128)(2,1)S(1)} %fusion.8), channel_id=1, source_target_pairs={{0,16},{8,24},{16,0},{24,8},{1,17},{9,25},{17,1},{25,9},{2,18},{10... | collective-permute-start | bytes 221192 | tf_op jit(solution)/shard_map/ppermute | solution.py:483
  121.6 4.4 %collective-permute-start.9 = (bf16[2,144,128]{2,1,0:T(8,128)(2,1)S(1)}, bf16[2,144,128]{2,1,0:T(8,128)(2,1)S(1)}, u32[]{:S(2)}, u32[]{:S(2)}) collective-permute-start(bf16[2,144,128]{2,1,0:T(8,128)(2,1)S(1)} %fusion.8), channel_id=1, source_target_pairs={{0,24},{8,16},{16,8},{24,0},{1,25},{9,17},{17,9},{25,1},{2,26},{10... | collective-permute-start | bytes 221192 | tf_op jit(solution)/shard_map/ppermute | solution.py:483
  126.1 4.5 %collective-permute-start.10 = (bf16[2,144,128]{2,1,0:T(8,128)(2,1)S(1)}, bf16[2,144,128]{2,1,0:T(8,128)(2,1)S(1)}, u32[]{:S(2)}, u32[]{:S(2)}) collective-permute-start(bf16[2,144,128]{2,1,0:T(8,128)(2,1)S(1)} %add_convert_fusion.2), channel_id=1, source_target_pairs={{0,96},{32,64},{64,32},{96,0},{1,97},{33,65},{65,33},{97,1},{2,98}... | collective-permute-start | bytes 221192 | tf_op jit(solution)/shard_map/ppermute | solution.py:483
  128.4 3.2 %collective-permute-start.11 = (bf16[2,144,128]{2,1,0:T(8,128)(2,1)S(1)}, bf16[2,144,128]{2,1,0:T(8,128)(2,1)S(1)}, u32[]{:S(2)}, u32[]{:S(2)}) collective-permute-start(bf16[2,144,128]{2,1,0:T(8,128)(2,1)S(1)} %add_convert_fusion.2), channel_id=1, source_target_pairs={{0,32},{32,0},{64,96},{96,64},{1,33},{33,1},{65,97},{97,65},{2,34}... | collective-permute-start | bytes 221192 | tf_op jit(solution)/shard_map/ppermute | solution.py:483
  128.4 4.7 %collective-permute-start.12 = (bf16[2,144,128]{2,1,0:T(8,128)(2,1)S(1)}, bf16[2,144,128]{2,1,0:T(8,128)(2,1)S(1)}, u32[]{:S(2)}, u32[]{:S(2)}) collective-permute-start(bf16[2,144,128]{2,1,0:T(8,128)(2,1)S(1)} %add_convert_fusion.2), channel_id=1, source_target_pairs={{0,64},{32,96},{64,0},{96,32},{1,65},{33,97},{65,1},{97,33},{2,66}... | collective-permute-start | bytes 221192 | tf_op jit(solution)/shard_map/ppermute | solution.py:483
  133.2 9.2 %collective-permute-start.13 = (bf16[2,2,144,128]{3,2,1,0:T(8,128)(2,1)S(1)}, bf16[2,2,144,128]{3,2,1,0:T(8,128)(2,1)S(1)}, u32[]{:S(2)}, u32[]{:S(2)}) collective-permute-start(bf16[2,2,144,128]{3,2,1,0:T(8,128)(2,1)S(1)} %pad_maximum_fusion.refs_0_), channel_id=1, source_target_pairs={{0,2},{2,0},{4,6},{6,4},{1,3},{3,1},{5,7},{7,5},{8,10},{10,8},{12,... | collective-permute-start | bytes 442376 | tf_op jit(solution)/shard_map/ppermute | solution.py:483
  133.2 9.5 %collective-permute-start.14 = (bf16[2,2,144,128]{3,2,1,0:T(8,128)(2,1)S(1)}, bf16[2,2,144,128]{3,2,1,0:T(8,128)(2,1)S(1)}, u32[]{:S(2)}, u32[]{:S(2)}) collective-permute-start(bf16[2,2,144,128]{3,2,1,0:T(8,128)(2,1)S(1)} %pad_maximum_fusion.refs_0_), channel_id=1, source_target_pairs={{0,4},{2,6},{4,0},{6,2},{1,5},{3,7},{5,1},{7,3},{8,12},{10,14},{12... | collective-permute-start | bytes 442376 | tf_op jit(solution)/shard_map/ppermute | solution.py:483
  135.7 10.0 %collective-permute-start.15 = (bf16[2,2,144,128]{3,2,1,0:T(8,128)(2,1)S(1)}, bf16[2,2,144,128]{3,2,1,0:T(8,128)(2,1)S(1)}, u32[]{:S(2)}, u32[]{:S(2)}) collective-permute-start(bf16[2,2,144,128]{3,2,1,0:T(8,128)(2,1)S(1)} %pad_maximum_fusion.refs_0_), channel_id=1, source_target_pairs={{0,6},{2,4},{4,2},{6,0},{1,7},{3,5},{5,3},{7,1},{8,14},{10,12},{12... | collective-permute-start | bytes 442376 | tf_op jit(solution)/shard_map/ppermute | solution.py:483
  137.1 10.3 %collective-permute-start.16 = (bf16[2,2,144,128]{3,2,1,0:T(8,128)(2,1)S(1)}, bf16[2,2,144,128]{3,2,1,0:T(8,128)(2,1)S(1)}, u32[]{:S(2)}, u32[]{:S(2)}) collective-permute-start(bf16[2,2,144,128]{3,2,1,0:T(8,128)(2,1)S(1)} %pad_maximum_fusion.refs_0_), channel_id=1, source_target_pairs={{0,1},{1,0},{2,3},{3,2},{4,5},{5,4},{6,7},{7,6},{8,9},{9,8},{10,11... | collective-permute-start | bytes 442376 | tf_op jit(solution)/shard_map/ppermute | solution.py:334
  142.3 5.1 %collective-permute-start.17 = (bf16[2,2,144,128]{3,2,1,0:T(8,128)(2,1)S(1)}, bf16[2,2,144,128]{3,2,1,0:T(8,128)(2,1)S(1)}, u32[]{:S(2)}, u32[]{:S(2)}) collective-permute-start(bf16[2,2,144,128]{3,2,1,0:T(8,128)(2,1)S(1)} %collective-permute-done.13.refs_1_), channel_id=1, source_target_pairs={{0,1},{1,0},{2,3},{3,2},{4,5},{5,4},{6,7},{7,6},{8,9},{9,8},{10,11... | collective-permute-start | bytes 442376 | tf_op jit(solution)/shard_map/ppermute | solution.py:334
  142.8 4.6 %collective-permute-start.18 = (bf16[2,2,144,128]{3,2,1,0:T(8,128)(2,1)S(1)}, bf16[2,2,144,128]{3,2,1,0:T(8,128)(2,1)S(1)}, u32[]{:S(2)}, u32[]{:S(2)}) collective-permute-start(bf16[2,2,144,128]{3,2,1,0:T(8,128)(2,1)S(1)} %collective-permute-done.14.refs_2_), channel_id=1, source_target_pairs={{0,1},{1,0},{2,3},{3,2},{4,5},{5,4},{6,7},{7,6},{8,9},{9,8},{10,11... | collective-permute-start | bytes 442376 | tf_op jit(solution)/shard_map/ppermute | solution.py:334
  145.7 2.7 %collective-permute-start.19 = (bf16[2,2,144,128]{3,2,1,0:T(8,128)(2,1)S(1)}, bf16[2,2,144,128]{3,2,1,0:T(8,128)(2,1)S(1)}, u32[]{:S(2)}, u32[]{:S(2)}) collective-permute-start(bf16[2,2,144,128]{3,2,1,0:T(8,128)(2,1)S(1)} %collective-permute-done.15.refs_3_), channel_id=1, source_target_pairs={{0,1},{1,0},{2,3},{3,2},{4,5},{5,4},{6,7},{7,6},{8,9},{9,8},{10,11... | collective-permute-start | bytes 442376 | tf_op jit(solution)/shard_map/ppermute | solution.py:334

commit v4 on v3

--- a/solution.py
+++ b/solution.py
@@ -124,8 +124,7 @@
     return decays_ref[t // group, t % group : t % group + 1]
 
 
-def inputs_kernel(place_ref, got_ref, weights_ref, inputs_ref, decays_ref, end_ref, cols_a, cols_b, both_ref, carry_ref):
-    step = pl.program_id(0)
+def inputs_step(step, last, place_ref, got_ref, weights_ref, inputs_ref, decays_ref, end_ref, cols_a, cols_b, both_ref, carry_ref):
     cols = (cols_a, cols_b)
     frames, _, _, side, _ = inputs_ref.shape
     group = frames // 2
@@ -149,13 +148,12 @@
         carried = decay_of(decays_ref, t) * carried + inputs_ref[t].astype(F32)
     carry_ref[...] = carried
 
-    @pl.when(step == pl.num_programs(0) - 1)
+    @pl.when(step == last)
     def _():
         end_ref[...] = carried
 
 
-def mixed_kernel(place_ref, inputs_ref, decays_ref, income_ref, skip_ref, weights_ref, states_ref, slope_ref, pooled_ref, cols_a, cols_b, both_ref, carry_ref, sum_ref):
-    step = pl.program_id(0)
+def mixed_step(step, last, place_ref, inputs_ref, decays_ref, income_ref, skip_ref, weights_ref, states_ref, slope_ref, pooled_ref, cols_a, cols_b, both_ref, carry_ref, sum_ref):
     cols = (cols_a, cols_b)
     frames = inputs_ref.shape[0]
     group = frames // 2
@@ -184,13 +182,12 @@
             total = total + jnp.sum(mixed * sigma, axis=(0, 1))
     sum_ref[...] = total
 
-    @pl.when(step == pl.num_programs(0) - 1)
+    @pl.when(step == last)
     def _():
         pooled_ref[...] = jnp.sum(total, axis=0, keepdims=True)
 
 
-def from_out_kernel(place_ref, slope_ref, decays_ref, dpool_ref, weights_ref, dmix_ref, source_ref, end_ref, cols_a, cols_b, both_ref, carry_ref):
-    step = pl.program_id(0)
+def from_out_step(step, last, place_ref, slope_ref, decays_ref, dpool_ref, weights_ref, dmix_ref, source_ref, end_ref, cols_a, cols_b, both_ref, carry_ref):
     cols = (cols_a, cols_b)
     frames = slope_ref.shape[0]
     group = frames // 2
@@ -212,13 +209,12 @@
         carried = decay_of(decays_ref, t) * (source_ref[t] + carried)
     carry_ref[...] = carried
 
-    @pl.when(step == pl.num_programs(0) - 1)
+    @pl.when(step == last)
     def _():
         end_ref[...] = carried
 
 
-def out_grad_kernel(place_ref, states_ref, dmix_ref, grad_ref, cols_a, cols_b, acc_ref):
-    step = pl.program_id(0)
+def out_grad_step(step, last, place_ref, states_ref, dmix_ref, grad_ref, cols_a, cols_b, acc_ref):
 
     @pl.when(step == 0)
     def _():
@@ -229,13 +225,12 @@
     spread_groups(halves(states_ref), (cols_a, cols_b))
     add_weight_product((cols_a, cols_b), dmix_ref[...], acc_ref)
 
-    @pl.when(step == pl.num_programs(0) - 1)
+    @pl.when(step == last)
     def _():
         grad_ref[...] = folded(acc_ref)
 
 
-def in_grad_kernel(place_ref, got_ref, slope_ref, source_ref, decays_ref, income_ref, dpool_ref, skip_ref, grad_ref, cols_a, cols_b, carry_ref, dinput_ref, acc_ref):
-    step = pl.program_id(0)
+def in_grad_step(step, last, place_ref, got_ref, slope_ref, source_ref, decays_ref, income_ref, dpool_ref, skip_ref, grad_ref, cols_a, cols_b, carry_ref, dinput_ref, acc_ref):
     frames = slope_ref.shape[0]
 
     @pl.when(step == 0)
@@ -255,7 +250,7 @@
     carry_ref[...] = carried
     add_weight_product((cols_a, cols_b), dinput_ref[...], acc_ref)
 
-    @pl.when(step == pl.num_programs(0) - 1)
+    @pl.when(step == last)
     def _():
         grad_ref[...] = folded(acc_ref)
 
@@ -265,26 +260,6 @@
         self.steps, self.frames, self.group, self.side, self.channels = senders // 2, 2 * group, group, side, channels
         self.map = (side // 2, 2, side, channels)
 
-    def whole(self, shape):
-        return pl.BlockSpec(shape, lambda i, place: (0,) * len(shape))
-
-    def order(self, back):
-        return (lambda i: self.steps - 1 - i) if back else (lambda i: i)
-
-    def maps(self, back=False):
-        at = self.order(back)
-        return pl.BlockSpec((self.frames, *self.map), lambda i, place: (at(i), 0, 0, 0, 0))
-
-    def got(self, rows, back=False):
-        at = self.order(back)
-        return pl.BlockSpec((2, rows, self.channels), lambda i, place: (at(i), 0, 0))
-
-    def decays(self, back=False):
-        return self.got(self.group, back)
-
-    def of_view(self, rows):
-        return pl.BlockSpec((1, rows, self.channels), lambda i, place: (place[1], 0, 0))
-
     def maps_of(self, dtype):
         return jax.ShapeDtypeStruct((self.steps * self.frames, *self.map), dtype)
 
@@ -306,27 +281,58 @@
     def acc(self):
         return pltpu.VMEM((2 * self.channels, 12 * self.channels), F32)
 
-    def row(self):
-        return self.whole((1, self.channels))
-
     def both(self):
         return pltpu.VMEM((12 * self.channels, 2 * self.channels), BF16)
 
-    def call(self, kernel, in_specs, out_shape, out_specs, scratch):
+    def call(self, run, back, takes, out_shape, gives, scratch, kept=()):
         cells = self.steps * self.frames * self.side * self.side
         work = 2 * 9 * cells * self.channels * self.channels
+        blocks = [*takes, *gives]
+        buffers = [pltpu.VMEM(out_shape[n].shape, out_shape[n].dtype) for n in kept]
+        sems = [pltpu.SemaphoreType.DMA((len(kept), self.steps))] if kept else []
+        first_out = len(takes)
+
+        def kernel(place_ref, *refs):
+            arrays, rest = list(refs[: len(blocks)]), refs[len(blocks) :]
+            far = {}
+            for k, n in enumerate(kept):
+                far[k] = arrays[first_out + n]
+                arrays[first_out + n] = rest[k]
+            rest = rest[len(kept) :]
+            if kept:
+                sems_ref, rest = rest[-1], rest[:-1]
+
+            def copy_of(k, i):
+                rows = pl.ds(i * gives[kept[k]], gives[kept[k]])
+                return pltpu.make_async_copy(arrays[first_out + kept[k]].at[rows], far[k].at[rows], sems_ref.at[k, i])
+
+            def step(i, _):
+                at = self.steps - 1 - i if back else i
+                views = []
+                for ref, block in zip(arrays, blocks):
+                    if block == "view":
+                        views.append(ref.at[pl.ds(place_ref[1], 1)])
+                    else:
+                        views.append(ref if block is None else ref.at[pl.ds(at * block, block)])
+                run(i, self.steps - 1, place_ref, *views, *rest)
+                for k in range(len(kept)):
+                    copy_of(k, at).start()
+                return 0
+
+            lax.fori_loop(0, self.steps, step, 0)
+            for k in range(len(kept)):
+                for i in range(self.steps):
+                    copy_of(k, i).wait()
+
+        vmem, hbm = pl.BlockSpec(memory_space=pltpu.VMEM), pl.BlockSpec(memory_space=pltpu.HBM)
         return pl.pallas_call(
             kernel,
-            out_shape=out_shape,
-            grid_spec=pltpu.PrefetchScalarGridSpec(
-                num_scalar_prefetch=1,
-                grid=(self.steps,),
-                in_specs=in_specs,
-                out_specs=out_specs,
-                scratch_shapes=scratch,
-            ),
+            out_shape=[pltpu.HBM(o.shape, o.dtype) if n in kept else o for n, o in enumerate(out_shape)],
+            in_specs=[pl.BlockSpec(memory_space=pltpu.SMEM)] + [vmem] * len(takes),
+            out_specs=[hbm if n in kept else vmem for n in range(len(out_shape))],
+            scratch_shapes=[*buffers, *scratch, *sems],
             cost_estimate=pl.CostEstimate(flops=2 * work, transcendentals=0, bytes_accessed=4 * cells * self.channels),
-            compiler_params=pltpu.CompilerParams(dimension_semantics=("arbitrary",), vmem_limit_bytes=24 << 20),
+            compiler_params=pltpu.CompilerParams(vmem_limit_bytes=24 << 20),
         )
 
 
@@ -349,47 +355,51 @@
     return pltpu.with_memory_space_constraint(x, pltpu.HBM)
 
 
-def pack_kernel(place_ref, rgb_ref, flow_ref, decay_ref, sent_ref):
-    view = pl.program_id(0)
-    frames, channels = decay_ref.shape[1:]
-    cells = rgb_ref.shape[1] * rgb_ref.shape[2] * rgb_ref.shape[3]
-
-    @pl.when(view == 0)
-    def _():
-        sent_ref[0, :cells] = rgb_ref[...].reshape(cells, channels)
-
-    @pl.when(view == 1)
-    def _():
-        sent_ref[0, :cells] = flow_ref[...].reshape(cells, channels)
-
-    decays = decay_ref[view]
-    high = decays.astype(BF16).astype(F32)
-    middle = (decays - high).astype(BF16).astype(F32)
-    low = decays - high - middle
-    rows = sent_ref.shape[1] - cells
-    parts = [high, middle, low, jnp.zeros((rows - 3 * frames, channels), F32)]
-    sent_ref[0, cells:] = jnp.concatenate(parts).astype(BF16)
+def pack_kernel(place_ref, rgb_ref, flow_ref, decay_ref, sent_ref, parts_ref, map_sems, part_sems):
+    half = place_ref[0]
+    clips, cells, channels = rgb_ref.shape
+    frames = decay_ref.shape[1]
+    copies = []
+    for v, maps_ref in enumerate((rgb_ref, flow_ref)):
+        for c in range(clips):
+            to = sent_ref.at[(v ^ half) * clips + c, :cells]
+            copies.append(pltpu.make_async_copy(maps_ref.at[c], to, map_sems.at[v, c]))
+    for copy in copies:
+        copy.start()
+    for v in range(2):
+        decays = decay_ref[v]
+        high = decays.astype(BF16).astype(F32)
+        middle = (decays - high).astype(BF16).astype(F32)
+        low = decays - high - middle
+        parts = [high, middle, low, jnp.zeros((parts_ref.shape[1] - 3 * frames, channels), F32)]
+        parts_ref[v] = jnp.concatenate(parts).astype(BF16)
+    late = []
+    for v in range(2):
+        for c in range(clips):
+            to = sent_ref.at[(v ^ half) * clips + c, cells:]
+            late.append(pltpu.make_async_copy(parts_ref.at[v], to, part_sems.at[v, c]))
+    for copy in late:
+        copy.start()
+    for copy in copies + late:
+        copy.wait()
 
 
 def clips_to_devices(rgb_maps, flow_maps, decay, place):
     clips, frames, side, _, channels = rgb_maps.shape
-    rows = frames * side * side + 16
-    block = (1, *rgb_maps.shape[1:])
+    cells = frames * side * side
+    hbm = pl.BlockSpec(memory_space=pltpu.HBM)
     sent = pl.pallas_call(
         pack_kernel,
-        out_shape=pltpu.HBM((2 * clips, rows, channels), BF16),
-        grid_spec=pltpu.PrefetchScalarGridSpec(
-            num_scalar_prefetch=1,
-            grid=(2, clips),
-            in_specs=[
-                pl.BlockSpec(block, lambda v, c, place: (jnp.where(v == 0, c, clips - 1), 0, 0, 0, 0)),
-                pl.BlockSpec(block, lambda v, c, place: (jnp.where(v == 0, 0, c), 0, 0, 0, 0)),
-                pl.BlockSpec(decay.shape, lambda v, c, place: (0, 0, 0)),
-            ],
-            out_specs=pl.BlockSpec((1, rows, channels), lambda v, c, place: ((v ^ place[0]) * clips + c, 0, 0)),
-        ),
+        out_shape=pltpu.HBM((2 * clips, cells + 16, channels), BF16),
+        in_specs=[pl.BlockSpec(memory_space=pltpu.SMEM), hbm, hbm, pl.BlockSpec(memory_space=pltpu.VMEM)],
+        out_specs=hbm,
+        scratch_shapes=[
+            pltpu.VMEM((2, 16, channels), BF16),
+            pltpu.SemaphoreType.DMA((2, clips)),
+            pltpu.SemaphoreType.DMA((2, clips)),
+        ],
         compiler_params=pltpu.CompilerParams(vmem_limit_bytes=16 << 20),
-    )(place, in_hbm(rgb_maps), in_hbm(flow_maps), decay)
+    )(place, *(in_hbm(maps.reshape(clips, cells, channels)) for maps in (rgb_maps, flow_maps)), decay)
     return lax.all_to_all(sent, TIME, 0, 0, tiled=True)
 
 
@@ -540,51 +550,54 @@
     senders, rows, _ = got.shape
     cell_count = 2 * senders * frames_here * side * side
     plan = Plan(senders, frames_here, side, channels)
-    taps = in_weights.shape[1]
-    weights = plan.of_view(taps)
     skips = skip.reshape(2, 1, channels)
-    carry_spec = plan.whole(plan.map)
-
+    here = plan.frames
     inputs, decays, end = plan.call(
-        inputs_kernel,
-        [plan.got(rows), weights],
+        inputs_step,
+        False,
+        [2, "view"],
         [plan.maps_of(BF16), plan.decays_of(), plan.carry_of()],
-        [plan.maps(), plan.decays(), carry_spec],
+        [here, 2, None],
         [*plan.cols(), plan.both(), plan.carry()],
     )(place, got, in_weights)
     income = from_other_half(end)
     states_b, slope, pooled_part = plan.call(
-        mixed_kernel,
-        [plan.maps(), plan.decays(), carry_spec, plan.of_view(1), weights],
-        [pltpu.HBM(a.shape, a.dtype) for a in (plan.maps_of(BF16), plan.maps_of(F32))] + [jax.ShapeDtypeStruct((1, channels), F32)],
-        [plan.maps(), plan.maps(), plan.row()],
+        mixed_step,
+        False,
+        [here, 2, None, "view", "view"],
+        [plan.maps_of(BF16), plan.maps_of(F32), jax.ShapeDtypeStruct((1, channels), F32)],
+        [here, here, None],
         [*plan.cols(), plan.both(), plan.carry(), pltpu.VMEM((side, channels), F32)],
+        kept=(0, 1),
     )(place, inputs, decays, income, skips, out_weights)
 
     seen = from_all(from_cores(pooled_part[0]), ("xh", "xl", "y", "z"))
     dpool = projector_back(seen.reshape(4, -1, channels), proj_in, proj_gain, proj_out, place, cell_count)
 
     dmix_b, source, end = plan.call(
-        from_out_kernel,
-        [plan.maps(True), plan.decays(True), plan.row(), weights],
+        from_out_step,
+        True,
+        [here, 2, None, "view"],
         [plan.maps_of(BF16), plan.maps_of(F32), plan.carry_of()],
-        [plan.maps(True), plan.maps(True), carry_spec],
+        [here, here, None],
         [*plan.cols(), plan.both(), plan.carry()],
     )(place, slope, decays, dpool, out_weights)
     income = from_other_half(end)
-    out_grad = plan.call(
-        out_grad_kernel,
-        [plan.maps(), plan.maps()],
-        plan.grad_of(),
-        plan.whole((9 * channels, channels)),
+    (out_grad,) = plan.call(
+        out_grad_step,
+        False,
+        [here, here],
+        [plan.grad_of()],
+        [None],
         [*plan.cols(), plan.acc()],
     )(place, states_b, dmix_b)
-    in_grad = plan.call(
-        in_grad_kernel,
-        [plan.got(rows, True), plan.maps(True), plan.maps(True), plan.decays(True), carry_spec, plan.row(), plan.of_view(1)],
-        plan.grad_of(),
-        plan.whole((9 * channels, channels)),
-        [*plan.cols(), plan.carry(), pltpu.VMEM((plan.frames, *plan.map), BF16), plan.acc()],
+    (in_grad,) = plan.call(
+        in_grad_step,
+        True,
+        [2, here, here, 2, None, None, "view"],
+        [plan.grad_of()],
+        [None],
+        [*plan.cols(), plan.carry(), pltpu.VMEM((here, *plan.map), BF16), plan.acc()],
     )(place, got, slope, source, decays, income, dpool, skips)
     return summed([in_grad, out_grad], place)
 

time: 151 us -> 210 us (1.39)
  Pallas kernels: 48.9 us -> 108 us
    pallas_call x6, Pallas kernels: 38.1 us -> 97.2 us  [the longest x1 65.3 us: clips_to_devices(): pl.pallas_call(pack_kernel, out_shape=pltpu.HBM((2 * clips, cells + 16, c...]
  transfers between devices with their start and end apart: 21 -> 21, of which waited for: 12 -> 12; matrix products, arithmetic and copies ran while one was open for 0% -> 0% of each run, Pallas kernels for 4% -> 3%
where the time goes in v4:
time: 210 us
  Pallas kernels  108 us (51%)
  starting transfers between devices  42.2 us (20%)
  blocking collectives  32.6 us (16%)
  waiting for transfers between devices  24.3 us (12%)
    pallas_call x1, Pallas kernels, clips_to_devices(): pl.pallas_call(pack_kernel, out_shape=pltpu.HBM((2 * clips, cells + 16, c...  65.3 us
    all_to_all x1, blocking collectives, clips_to_devices(): return lax.all_to_all(sent, TIME, 0, 0, tiled=True)  32.6 us
    ppermute x6, starting transfers between devices, swapped(): return lax.ppermute(x, 'core', [(0, 1), (1, 0)])  15.8 us
    ppermute x12, starting transfers between devices, from_peer(): return lax.ppermute(x, axes, [(i, i ^ k) for i in range(4)])  15.7 us
    ppermute x12, waiting for transfers between devices, from_peer(): return lax.ppermute(x, axes, [(i, i ^ k) for i in range(4)])  8.98 us
    pallas_call x1, Pallas kernels, projector_back(): pl.pallas_call(functools.partial(projector_kernel, cell_count=cell_count)...  8.73 us
    all_to_all x1, waiting for transfers between devices, from_all(): lax.all_to_all(jnp.broadcast_to(x[None], (peers, *x.shape)), axes, 0, 0,...  8.46 us
    pallas_call x1, Pallas kernels, per_device(): plan.call(mixed_step, False, [here, 2, None, 'view', 'view'], [plan.maps_...  8.03 us
  transfers between devices with their start and end apart: 21, of which 12 were waited for; matrix products, arithmetic and copies ran while one was open for 0% of the time, Pallas kernels for 3%

profile of v4, /device:TPU:1, one launch (start us, length us, event | category | flops | bytes accessed | tf_op | source)
XLA Modules:
  0.0 209.7 jit_solution(1381789985625537292)
XLA Ops:
  1.4 65.3 %shard_map.104 = bf16[8,1040,128]{2,1,0:T(8,128)(2,1)} custom-call(s32[5]{0:T(128)S(1)} %stack.53.place_ref, bf16[4,1024,128]{2,1,0:T(8,128)(2,1)} %bitcast.55, bf16[4,1024,128]{2,1,0:T(8,128)(2,1)} %bitcast.56, f32[2,4,128]{2,1,0:T(4,128)S(1)} %copy-done.2), custom_call_target="tpu_custom_call" | custom-call | tf_op jit(solution)/shard_map/pallas_call | solution.py:391
  66.8 32.6 %all_to_all.10.refs_0_ = bf16[8,1040,128]{2,1,0:T(8,128)(2,1)S(1)} all-to-all(bf16[8,1040,128]{2,1,0:T(8,128)(2,1)} %shard_map.104), channel_id=1, replica_groups=mesh['xh'=2,'xl'=2,'y'=4,'z'=4,'core'=2] {'xl','y'}, dimensions={0} | all-to-all | bytes 4259840 | tf_op jit(solution)/shard_map/all_to_all | solution.py:403
  99.4 5.2 %shard_map.105 = (bf16[32,8,2,16,128]{4,3,2,1,0:T(8,128)(2,1)S(1)}, f32[8,4,128]{2,1,0:T(4,128)S(1)}, f32[8,2,16,128]{3,2,1,0:T(8,128)S(1)}) custom-call(s32[5]{0:T(128)S(1)} %stack.53.place_ref, bf16[8,1040,128]{2,1,0:T(8,128)(2,1)S(1)} %all_to_all.10.refs_0_, bf16[2,1152,128]{2,1,0:T(8,128)(2,1)S(1)} %copy-done.3), custom_call_target="tpu_custom_call" | custom-call | flops 4831838208 | bytes 4194304 | tf_op jit(solution)/shard_map/pallas_call | solution.py:555
  104.6 1.7 collective-permute-start
  106.3 3.4 %collective-permute-done.refs_2_ = f32[8,2,16,128]{3,2,1,0:T(8,128)S(1)} collective-permute-done((f32[8,2,16,128]{3,2,1,0:T(8,128)S(1)}, f32[8,2,16,128]{3,2,1,0:T(8,128)S(1)}, u32[]{:S(2)}, u32[]{:S(2)}) %collective-permute-start) | collective-permute-done | bytes 131104 | tf_op jit(solution)/shard_map/ppermute | solution.py:489
  109.7 8.0 %shard_map.106 = (bf16[32,8,2,16,128]{4,3,2,1,0:T(8,128)(2,1)}, f32[32,8,2,16,128]{4,3,2,1,0:T(8,128)}, f32[1,128]{1,0:T(1,128)S(1)}) custom-call(s32[5]{0:T(128)S(1)} %stack.53.place_ref, bf16[32,8,2,16,128]{4,3,2,1,0:T(8,128)(2,1)S(1)} %get-tuple-element.11.refs_0_, f32[8,4,128]{2,1,0:T(4,128)S(1)} %get-tuple-element.12.refs_1_.refs_3_, ...), custom_call_target="tpu_custom_call" | custom-call | flops 4831838208 | bytes 4194304 | tf_op jit(solution)/shard_map/pallas_call | solution.py:564
  117.8 3.4 %collective-permute-start.1 = (f32[128]{0:T(128)S(1)}, f32[128]{0:T(128)S(1)}, u32[]{:S(2)}, u32[]{:S(2)}) collective-permute-start(f32[128]{0:T(128)S(1)} %bitcast.52), channel_id=1, source_target_pairs={{0,1},{1,0},{2,3},{3,2},{4,5},{5,4},{6,7},{7,6},{8,9},{9,8},{10,11... | collective-permute-start | bytes 1544 | tf_op jit(solution)/shard_map/ppermute | solution.py:340
  122.7 7.9 %all-to-all-start.1 = ((f32[64,2,128]{2,1,0:T(2,128)}), f32[64,2,128]{2,1,0:T(2,128)S(1)}, u32[]{:S(2)}, u32[]{:S(2)}) async-start(f32[64,2,128]{2,1,0:T(2,128)} %broadcast_in_dim.2), calls=%async_computation.1 | async-start | bytes 131072 | tf_op jit(solution)/shard_map/all_to_all | solution.py:351
  130.6 8.5 %all-to-all-done.1 = f32[64,2,128]{2,1,0:T(2,128)S(1)} async-done(((f32[64,2,128]{2,1,0:T(2,128)}), f32[64,2,128]{2,1,0:T(2,128)S(1)}, u32[]{:S(2)}, u32[]{:S(2)}) %all-to-all-start.1) | async-done | bytes 65568 | tf_op jit(solution)/shard_map/all_to_all | solution.py:351
  139.1 8.7 %shard_map.107.refs_2_.refs_5_ = f32[1,128]{1,0:T(1,128)S(1)} custom-call(s32[5]{0:T(128)S(1)} %stack.53.place_ref, f32[4,32,128]{2,1,0:T(8,128)S(1)} %bitcast.50, f32[128,2048]{1,0:T(8,128)S(1)} %copy-done, f32[1,2048]{1,0:T(1,128)S(1)} %bitcast.51, bf16[2048,2048]{1,0:T(8,128)(2,1)} %far_ref.1), custom_call_target="tpu_custom_call" | custom-call | flops 805306368 | bytes 8388608 | tf_op jit(solution)/shard_map/pallas_call | solution.py:469
  147.8 5.9 %shard_map.108 = (bf16[32,8,2,16,128]{4,3,2,1,0:T(8,128)(2,1)S(1)}, f32[32,8,2,16,128]{4,3,2,1,0:T(8,128)S(1)}, f32[8,2,16,128]{3,2,1,0:T(8,128)S(1)}) custom-call(s32[5]{0:T(128)S(1)} %stack.53.place_ref, f32[32,8,2,16,128]{4,3,2,1,0:T(8,128)S(1)} %copy-done.7, f32[8,4,128]{2,1,0:T(4,128)S(1)} %get-tuple-element.12.refs_1_.refs_3_, ...), custom_call_target="tpu_custom_call" | custom-call | flops 4831838208 | bytes 4194304 | tf_op jit(solution)/shard_map/pallas_call | solution.py:577
  154.8 5.7 %shard_map.110 = f32[1152,128]{1,0:T(8,128)S(1)} custom-call(s32[5]{0:T(128)S(1)} %stack.53.place_ref, bf16[32,8,2,16,128]{4,3,2,1,0:T(8,128)(2,1)S(1)} %copy-done.8, bf16[32,8,2,16,128]{4,3,2,1,0:T(8,128)(2,1)S(1)} %get-tuple-element.19.refs_1_), custom_call_target="tpu_custom_call" | custom-call | flops 4831838208 | bytes 4194304 | tf_op jit(solution)/shard_map/pallas_call | solution.py:586
  160.5 7.0 %shard_map.109 = f32[1152,128]{1,0:T(8,128)S(1)} custom-call(s32[5]{0:T(128)S(1)} %stack.53.place_ref, bf16[8,1040,128]{2,1,0:T(8,128)(2,1)S(1)} %all_to_all.10.refs_0_, f32[32,8,2,16,128]{4,3,2,1,0:T(8,128)S(1)} %copy-done.7, f32[32,8,2,16,128]{4,3,2,1,0:T(8,128)S(1)} %get-tuple-element.16.refs_2_, f32[8,4,128]{2,1,0:T(4,128)S(1)} %get-tuple-element.12.refs_1_.refs_3_, ...), custom_call_target="tpu_custom_call" | custom-call | flops 4831838208 | bytes 4194304 | tf_op jit(solution)/shard_map/pallas_call | solution.py:594
  167.6 2.1 collective-permute-start.3
  169.6 1.6 collective-permute-done.3
  171.7 1.9 collective-permute-start.5
  173.6 1.7 collective-permute-start.6
  175.3 2.2 %collective-permute-done.5 = bf16[2,144,128]{2,1,0:T(8,128)(2,1)S(1)} collective-permute-done((bf16[2,144,128]{2,1,0:T(8,128)(2,1)S(1)}, bf16[2,144,128]{2,1,0:T(8,128)(2,1)S(1)}, u32[]{:S(2)}, u32[]{:S(2)}) %collective-permute-start.5) | collective-permute-done | bytes 73760 | tf_op jit(solution)/shard_map/ppermute | solution.py:493
  177.5 1.1 collective-permute-done.6
  179.0 1.8 collective-permute-start.8
  180.8 1.7 collective-permute-start.9
  182.6 1.2 collective-permute-done.8
  183.7 1.5 collective-permute-done.9
  185.3 2.3 %collective-permute-start.10 = (bf16[2,144,128]{2,1,0:T(8,128)(2,1)S(1)}, bf16[2,144,128]{2,1,0:T(8,128)(2,1)S(1)}, u32[]{:S(2)}, u32[]{:S(2)}) collective-permute-start(bf16[2,144,128]{2,1,0:T(8,128)(2,1)S(1)} %add_convert_fusion.2), channel_id=1, source_target_pairs={{0,96},{32,64},{64,32},{96,0},{1,97},{33,65},{65,33},{97,1},{2,98}... | collective-permute-start | bytes 221192 | tf_op jit(solution)/shard_map/ppermute | solution.py:493
  187.6 1.7 collective-permute-start.12
  190.8 1.5 collective-permute-done.12
  192.4 2.5 %collective-permute-start.14 = (bf16[2,2,144,128]{3,2,1,0:T(8,128)(2,1)S(1)}, bf16[2,2,144,128]{3,2,1,0:T(8,128)(2,1)S(1)}, u32[]{:S(2)}, u32[]{:S(2)}) collective-permute-start(bf16[2,2,144,128]{3,2,1,0:T(8,128)(2,1)S(1)} %pad_maximum_fusion.refs_0_), channel_id=1, source_target_pairs={{0,4},{2,6},{4,0},{6,2},{1,5},{3,7},{5,1},{7,3},{8,12},{10,14},{12... | collective-permute-start | bytes 442376 | tf_op jit(solution)/shard_map/ppermute | solution.py:493
  194.9 1.3 collective-permute-start.15
  196.3 5.2 %collective-permute-start.16 = (bf16[2,2,144,128]{3,2,1,0:T(8,128)(2,1)S(1)}, bf16[2,2,144,128]{3,2,1,0:T(8,128)(2,1)S(1)}, u32[]{:S(2)}, u32[]{:S(2)}) collective-permute-start(bf16[2,2,144,128]{3,2,1,0:T(8,128)(2,1)S(1)} %pad_maximum_fusion.refs_0_), channel_id=1, source_target_pairs={{0,1},{1,0},{2,3},{3,2},{4,5},{5,4},{6,7},{7,6},{8,9},{9,8},{10,11... | collective-permute-start | bytes 442376 | tf_op jit(solution)/shard_map/ppermute | solution.py:340
  202.0 3.0 %collective-permute-start.18 = (bf16[2,2,144,128]{3,2,1,0:T(8,128)(2,1)S(1)}, bf16[2,2,144,128]{3,2,1,0:T(8,128)(2,1)S(1)}, u32[]{:S(2)}, u32[]{:S(2)}) collective-permute-start(bf16[2,2,144,128]{3,2,1,0:T(8,128)(2,1)S(1)} %collective-permute-done.14.refs_2_), channel_id=1, source_target_pairs={{0,1},{1,0},{2,3},{3,2},{4,5},{5,4},{6,7},{7,6},{8,9},{9,8},{10,11... | collective-permute-start | bytes 442376 | tf_op jit(solution)/shard_map/ppermute | solution.py:340
  204.9 1.7 collective-permute-start.19
  207.6 2.1 shard_map.111
  (49 shorter events, 7.4 us)
Async XLA Ops:
  0.7 0.7 copy-start.2
  66.8 32.7 %copy-start.3 = (bf16[2,1152,128]{2,1,0:T(8,128)(2,1)S(1)}, bf16[2,1152,128]{2,1,0:T(8,128)(2,1)}, u32[]{:S(2)}) copy-start(bf16[2,1152,128]{2,1,0:T(8,128)(2,1)} %refs_1_.1) | copy-start | bytes 1769476
  99.4 10.3 %copy-start.4 = (bf16[2,1152,128]{2,1,0:T(8,128)(2,1)S(1)}, bf16[2,1152,128]{2,1,0:T(8,128)(2,1)}, u32[]{:S(2)}) copy-start(bf16[2,1152,128]{2,1,0:T(8,128)(2,1)} %refs_3_.1) | copy-start | bytes 1769476
  99.4 10.3 %copy-start.6 = (f32[2,128]{1,0:T(2,128)S(1)}, f32[2,128]{1,0:T(2,128)}, u32[]{:S(2)}) copy-start(f32[2,128]{1,0:T(2,128)} %param.14) | copy-start | bytes 3076
  104.6 5.1 %collective-permute-start = (f32[8,2,16,128]{3,2,1,0:T(8,128)S(1)}, f32[8,2,16,128]{3,2,1,0:T(8,128)S(1)}, u32[]{:S(2)}, u32[]{:S(2)}) collective-permute-start(f32[8,2,16,128]{3,2,1,0:T(8,128)S(1)} %get-tuple-element.13), channel_id=1, source_target_pairs={{0,96},{32,64},{64,32},{96,0},{1,97},{33,65},{65,33},{97,1},{2,98}... | collective-permute-start | bytes 393224 | tf_op jit(solution)/shard_map/ppermute | solution.py:489
  109.7 29.3 %copy-start = (f32[128,2048]{1,0:T(8,128)S(1)}, f32[128,2048]{1,0:T(8,128)}, u32[]{:S(2)}) copy-start(f32[128,2048]{1,0:T(8,128)} %in_ref.1) | copy-start | bytes 3145732
  109.7 29.3 %copy-start.1 = (f32[2048]{0:T(1024)S(1)}, f32[2048]{0:T(1024)}, u32[]{:S(2)}) copy-start(f32[2048]{0:T(1024)} %param.16) | copy-start | bytes 24580
  117.8 4.2 %collective-permute-start.1 = (f32[128]{0:T(128)S(1)}, f32[128]{0:T(128)S(1)}, u32[]{:S(2)}, u32[]{:S(2)}) collective-permute-start(f32[128]{0:T(128)S(1)} %bitcast.52), channel_id=1, source_target_pairs={{0,1},{1,0},{2,3},{3,2},{4,5},{5,4},{6,7},{7,6},{8,9},{9,8},{10,11... | collective-permute-start | bytes 1544 | tf_op jit(solution)/shard_map/ppermute | solution.py:340
  122.7 16.4 %all-to-all-start.1 = ((f32[64,2,128]{2,1,0:T(2,128)}), f32[64,2,128]{2,1,0:T(2,128)S(1)}, u32[]{:S(2)}, u32[]{:S(2)}) async-start(f32[64,2,128]{2,1,0:T(2,128)} %broadcast_in_dim.2), calls=%async_computation.1 | async-start | bytes 131072 | tf_op jit(solution)/shard_map/all_to_all | solution.py:351
  139.0 8.7 %copy-start.5 = (bf16[2,1152,128]{2,1,0:T(8,128)(2,1)S(1)}, bf16[2,1152,128]{2,1,0:T(8,128)(2,1)}, u32[]{:S(2)}) copy-start(bf16[2,1152,128]{2,1,0:T(8,128)(2,1)} %refs_3_.1) | copy-start | bytes 1769476
  139.1 8.8 %copy-start.7 = (f32[32,8,2,16,128]{4,3,2,1,0:T(8,128)S(1)}, f32[32,8,2,16,128]{4,3,2,1,0:T(8,128)}, u32[]{:S(2)}) copy-start(f32[32,8,2,16,128]{4,3,2,1,0:T(8,128)} %get-tuple-element.14.refs_0_.refs_1_) | copy-start | bytes 12582916
  147.8 6.9 %copy-start.8 = (bf16[32,8,2,16,128]{4,3,2,1,0:T(8,128)(2,1)S(1)}, bf16[32,8,2,16,128]{4,3,2,1,0:T(8,128)(2,1)}, u32[]{:S(2)}) copy-start(bf16[32,8,2,16,128]{4,3,2,1,0:T(8,128)(2,1)} %get-tuple-element.18.refs_0_) | copy-start | bytes 6291460
  153.7 6.7 %collective-permute-start.2 = (f32[8,2,16,128]{3,2,1,0:T(8,128)S(1)}, f32[8,2,16,128]{3,2,1,0:T(8,128)S(1)}, u32[]{:S(2)}, u32[]{:S(2)}) collective-permute-start(f32[8,2,16,128]{3,2,1,0:T(8,128)S(1)} %get-tuple-element.17), channel_id=1, source_target_pairs={{0,96},{32,64},{64,32},{96,0},{1,97},{33,65},{65,33},{97,1},{2,98}... | collective-permute-start | bytes 393224 | tf_op jit(solution)/shard_map/ppermute | solution.py:489
  167.6 3.7 %collective-permute-start.3 = (f32[2,4,144,128]{3,2,0,1:T(8,128)S(1)}, f32[2,4,144,128]{3,2,0,1:T(8,128)S(1)}, u32[]{:S(2)}, u32[]{:S(2)}) collective-permute-start(f32[2,4,144,128]{3,2,0,1:T(8,128)S(1)} %fusion.1), channel_id=1, source_target_pairs={{0,1},{1,0},{2,3},{3,2},{4,5},{5,4},{6,7},{7,6},{8,9},{9,8},{10,11... | collective-permute-start | bytes 1769480 | tf_op jit(solution)/shard_map/ppermute | solution.py:340
  171.4 3.9 %collective-permute-start.4 = (bf16[2,144,128]{2,1,0:T(8,128)(2,1)S(1)}, bf16[2,144,128]{2,1,0:T(8,128)(2,1)S(1)}, u32[]{:S(2)}, u32[]{:S(2)}) collective-permute-start(bf16[2,144,128]{2,1,0:T(8,128)(2,1)S(1)} %get-tuple-element.20), channel_id=1, source_target_pairs={{0,2},{2,0},{4,6},{6,4},{1,3},{3,1},{5,7},{7,5},{8,10},{10,8},{12,... | collective-permute-start | bytes 221192 | tf_op jit(solution)/shard_map/ppermute | solution.py:493
  171.7 5.8 %collective-permute-start.5 = (bf16[2,144,128]{2,1,0:T(8,128)(2,1)S(1)}, bf16[2,144,128]{2,1,0:T(8,128)(2,1)S(1)}, u32[]{:S(2)}, u32[]{:S(2)}) collective-permute-start(bf16[2,144,128]{2,1,0:T(8,128)(2,1)S(1)} %get-tuple-element.22), channel_id=1, source_target_pairs={{0,4},{2,6},{4,0},{6,2},{1,5},{3,7},{5,1},{7,3},{8,12},{10,14},{12... | collective-permute-start | bytes 221192 | tf_op jit(solution)/shard_map/ppermute | solution.py:493
  173.6 4.9 %collective-permute-start.6 = (bf16[2,144,128]{2,1,0:T(8,128)(2,1)S(1)}, bf16[2,144,128]{2,1,0:T(8,128)(2,1)S(1)}, u32[]{:S(2)}, u32[]{:S(2)}) collective-permute-start(bf16[2,144,128]{2,1,0:T(8,128)(2,1)S(1)} %get-tuple-element.21), channel_id=1, source_target_pairs={{0,6},{2,4},{4,2},{6,0},{1,7},{3,5},{5,3},{7,1},{8,14},{10,12},{12... | collective-permute-start | bytes 221192 | tf_op jit(solution)/shard_map/ppermute | solution.py:493
  178.6 3.9 %collective-permute-start.7 = (bf16[2,144,128]{2,1,0:T(8,128)(2,1)S(1)}, bf16[2,144,128]{2,1,0:T(8,128)(2,1)S(1)}, u32[]{:S(2)}, u32[]{:S(2)}) collective-permute-start(bf16[2,144,128]{2,1,0:T(8,128)(2,1)S(1)} %fusion.8), channel_id=1, source_target_pairs={{0,8},{8,0},{16,24},{24,16},{1,9},{9,1},{17,25},{25,17},{2,10},{10... | collective-permute-start | bytes 221192 | tf_op jit(solution)/shard_map/ppermute | solution.py:493
  179.0 4.7 %collective-permute-start.8 = (bf16[2,144,128]{2,1,0:T(8,128)(2,1)S(1)}, bf16[2,144,128]{2,1,0:T(8,128)(2,1)S(1)}, u32[]{:S(2)}, u32[]{:S(2)}) collective-permute-start(bf16[2,144,128]{2,1,0:T(8,128)(2,1)S(1)} %fusion.8), channel_id=1, source_target_pairs={{0,16},{8,24},{16,0},{24,8},{1,17},{9,25},{17,1},{25,9},{2,18},{10... | collective-permute-start | bytes 221192 | tf_op jit(solution)/shard_map/ppermute | solution.py:493
  180.8 4.4 %collective-permute-start.9 = (bf16[2,144,128]{2,1,0:T(8,128)(2,1)S(1)}, bf16[2,144,128]{2,1,0:T(8,128)(2,1)S(1)}, u32[]{:S(2)}, u32[]{:S(2)}) collective-permute-start(bf16[2,144,128]{2,1,0:T(8,128)(2,1)S(1)} %fusion.8), channel_id=1, source_target_pairs={{0,24},{8,16},{16,8},{24,0},{1,25},{9,17},{17,9},{25,1},{2,26},{10... | collective-permute-start | bytes 221192 | tf_op jit(solution)/shard_map/ppermute | solution.py:493
  185.3 4.5 %collective-permute-start.10 = (bf16[2,144,128]{2,1,0:T(8,128)(2,1)S(1)}, bf16[2,144,128]{2,1,0:T(8,128)(2,1)S(1)}, u32[]{:S(2)}, u32[]{:S(2)}) collective-permute-start(bf16[2,144,128]{2,1,0:T(8,128)(2,1)S(1)} %add_convert_fusion.2), channel_id=1, source_target_pairs={{0,96},{32,64},{64,32},{96,0},{1,97},{33,65},{65,33},{97,1},{2,98}... | collective-permute-start | bytes 221192 | tf_op jit(solution)/shard_map/ppermute | solution.py:493
  187.6 3.2 %collective-permute-start.11 = (bf16[2,144,128]{2,1,0:T(8,128)(2,1)S(1)}, bf16[2,144,128]{2,1,0:T(8,128)(2,1)S(1)}, u32[]{:S(2)}, u32[]{:S(2)}) collective-permute-start(bf16[2,144,128]{2,1,0:T(8,128)(2,1)S(1)} %add_convert_fusion.2), channel_id=1, source_target_pairs={{0,32},{32,0},{64,96},{96,64},{1,33},{33,1},{65,97},{97,65},{2,34}... | collective-permute-start | bytes 221192 | tf_op jit(solution)/shard_map/ppermute | solution.py:493
  187.6 4.7 %collective-permute-start.12 = (bf16[2,144,128]{2,1,0:T(8,128)(2,1)S(1)}, bf16[2,144,128]{2,1,0:T(8,128)(2,1)S(1)}, u32[]{:S(2)}, u32[]{:S(2)}) collective-permute-start(bf16[2,144,128]{2,1,0:T(8,128)(2,1)S(1)} %add_convert_fusion.2), channel_id=1, source_target_pairs={{0,64},{32,96},{64,0},{96,32},{1,65},{33,97},{65,1},{97,33},{2,66}... | collective-permute-start | bytes 221192 | tf_op jit(solution)/shard_map/ppermute | solution.py:493
  192.3 9.2 %collective-permute-start.13 = (bf16[2,2,144,128]{3,2,1,0:T(8,128)(2,1)S(1)}, bf16[2,2,144,128]{3,2,1,0:T(8,128)(2,1)S(1)}, u32[]{:S(2)}, u32[]{:S(2)}) collective-permute-start(bf16[2,2,144,128]{3,2,1,0:T(8,128)(2,1)S(1)} %pad_maximum_fusion.refs_0_), channel_id=1, source_target_pairs={{0,2},{2,0},{4,6},{6,4},{1,3},{3,1},{5,7},{7,5},{8,10},{10,8},{12,... | collective-permute-start | bytes 442376 | tf_op jit(solution)/shard_map/ppermute | solution.py:493
  192.4 9.5 %collective-permute-start.14 = (bf16[2,2,144,128]{3,2,1,0:T(8,128)(2,1)S(1)}, bf16[2,2,144,128]{3,2,1,0:T(8,128)(2,1)S(1)}, u32[]{:S(2)}, u32[]{:S(2)}) collective-permute-start(bf16[2,2,144,128]{3,2,1,0:T(8,128)(2,1)S(1)} %pad_maximum_fusion.refs_0_), channel_id=1, source_target_pairs={{0,4},{2,6},{4,0},{6,2},{1,5},{3,7},{5,1},{7,3},{8,12},{10,14},{12... | collective-permute-start | bytes 442376 | tf_op jit(solution)/shard_map/ppermute | solution.py:493
  194.9 10.0 %collective-permute-start.15 = (bf16[2,2,144,128]{3,2,1,0:T(8,128)(2,1)S(1)}, bf16[2,2,144,128]{3,2,1,0:T(8,128)(2,1)S(1)}, u32[]{:S(2)}, u32[]{:S(2)}) collective-permute-start(bf16[2,2,144,128]{3,2,1,0:T(8,128)(2,1)S(1)} %pad_maximum_fusion.refs_0_), channel_id=1, source_target_pairs={{0,6},{2,4},{4,2},{6,0},{1,7},{3,5},{5,3},{7,1},{8,14},{10,12},{12... | collective-permute-start | bytes 442376 | tf_op jit(solution)/shard_map/ppermute | solution.py:493
  196.3 10.3 %collective-permute-start.16 = (bf16[2,2,144,128]{3,2,1,0:T(8,128)(2,1)S(1)}, bf16[2,2,144,128]{3,2,1,0:T(8,128)(2,1)S(1)}, u32[]{:S(2)}, u32[]{:S(2)}) collective-permute-start(bf16[2,2,144,128]{3,2,1,0:T(8,128)(2,1)S(1)} %pad_maximum_fusion.refs_0_), channel_id=1, source_target_pairs={{0,1},{1,0},{2,3},{3,2},{4,5},{5,4},{6,7},{7,6},{8,9},{9,8},{10,11... | collective-permute-start | bytes 442376 | tf_op jit(solution)/shard_map/ppermute | solution.py:340
  201.5 5.1 %collective-permute-start.17 = (bf16[2,2,144,128]{3,2,1,0:T(8,128)(2,1)S(1)}, bf16[2,2,144,128]{3,2,1,0:T(8,128)(2,1)S(1)}, u32[]{:S(2)}, u32[]{:S(2)}) collective-permute-start(bf16[2,2,144,128]{3,2,1,0:T(8,128)(2,1)S(1)} %collective-permute-done.13.refs_1_), channel_id=1, source_target_pairs={{0,1},{1,0},{2,3},{3,2},{4,5},{5,4},{6,7},{7,6},{8,9},{9,8},{10,11... | collective-permute-start | bytes 442376 | tf_op jit(solution)/shard_map/ppermute | solution.py:340
  202.0 4.6 %collective-permute-start.18 = (bf16[2,2,144,128]{3,2,1,0:T(8,128)(2,1)S(1)}, bf16[2,2,144,128]{3,2,1,0:T(8,128)(2,1)S(1)}, u32[]{:S(2)}, u32[]{:S(2)}) collective-permute-start(bf16[2,2,144,128]{3,2,1,0:T(8,128)(2,1)S(1)} %collective-permute-done.14.refs_2_), channel_id=1, source_target_pairs={{0,1},{1,0},{2,3},{3,2},{4,5},{5,4},{6,7},{7,6},{8,9},{9,8},{10,11... | collective-permute-start | bytes 442376 | tf_op jit(solution)/shard_map/ppermute | solution.py:340
  204.9 2.7 %collective-permute-start.19 = (bf16[2,2,144,128]{3,2,1,0:T(8,128)(2,1)S(1)}, bf16[2,2,144,128]{3,2,1,0:T(8,128)(2,1)S(1)}, u32[]{:S(2)}, u32[]{:S(2)}) collective-permute-start(bf16[2,2,144,128]{3,2,1,0:T(8,128)(2,1)S(1)} %collective-permute-done.15.refs_3_), channel_id=1, source_target_pairs={{0,1},{1,0},{2,3},{3,2},{4,5},{5,4},{6,7},{7,6},{8,9},{9,8},{10,11... | collective-permute-start | bytes 442376 | tf_op jit(solution)/shard_map/ppermute | solution.py:340

commit v5 on v4

--- a/solution.py
+++ b/solution.py
@@ -355,7 +355,7 @@
     return pltpu.with_memory_space_constraint(x, pltpu.HBM)
 
 
-def pack_kernel(place_ref, rgb_ref, flow_ref, decay_ref, sent_ref, parts_ref, map_sems, part_sems):
+def pack_kernel(place_ref, rgb_ref, flow_ref, decay_ref, sent_ref, map_sems):
     half = place_ref[0]
     clips, cells, channels = rgb_ref.shape
     frames = decay_ref.shape[1]
@@ -371,16 +371,12 @@
         high = decays.astype(BF16).astype(F32)
         middle = (decays - high).astype(BF16).astype(F32)
         low = decays - high - middle
-        parts = [high, middle, low, jnp.zeros((parts_ref.shape[1] - 3 * frames, channels), F32)]
-        parts_ref[v] = jnp.concatenate(parts).astype(BF16)
-    late = []
-    for v in range(2):
+        rows = sent_ref.shape[1] - cells
+        parts = [high, middle, low, jnp.zeros((rows - 3 * frames, channels), F32)]
+        parts = jnp.concatenate(parts).astype(BF16)
         for c in range(clips):
-            to = sent_ref.at[(v ^ half) * clips + c, cells:]
-            late.append(pltpu.make_async_copy(parts_ref.at[v], to, part_sems.at[v, c]))
-    for copy in late:
-        copy.start()
-    for copy in copies + late:
+            sent_ref[(v ^ half) * clips + c, cells:] = parts
+    for copy in copies:
         copy.wait()
 
 
@@ -390,14 +386,10 @@
     hbm = pl.BlockSpec(memory_space=pltpu.HBM)
     sent = pl.pallas_call(
         pack_kernel,
-        out_shape=pltpu.HBM((2 * clips, cells + 16, channels), BF16),
+        out_shape=jax.ShapeDtypeStruct((2 * clips, cells + 16, channels), BF16),
         in_specs=[pl.BlockSpec(memory_space=pltpu.SMEM), hbm, hbm, pl.BlockSpec(memory_space=pltpu.VMEM)],
-        out_specs=hbm,
-        scratch_shapes=[
-            pltpu.VMEM((2, 16, channels), BF16),
-            pltpu.SemaphoreType.DMA((2, clips)),
-            pltpu.SemaphoreType.DMA((2, clips)),
-        ],
+        out_specs=pl.BlockSpec(memory_space=pltpu.VMEM),
+        scratch_shapes=[pltpu.SemaphoreType.DMA((2, clips))],
         compiler_params=pltpu.CompilerParams(vmem_limit_bytes=16 << 20),
     )(place, *(in_hbm(maps.reshape(clips, cells, channels)) for maps in (rgb_maps, flow_maps)), decay)
     return lax.all_to_all(sent, TIME, 0, 0, tiled=True)

time: 210 us -> 146 us (0.70)
  Pallas kernels: 108 us -> 44.6 us
    pallas_call x1, Pallas kernels: 65.3 us -> 2.12 us  [clips_to_devices(): pl.pallas_call(pack_kernel, out_shape=jax.ShapeDtypeStruct((2 * clips, ce...]
  transfers between devices with their start and end apart: 21 -> 21, of which waited for: 12 -> 12; matrix products, arithmetic and copies ran while one was open for 0% -> 0% of each run, Pallas kernels for 3% -> 4%
where the time goes in v5:
time: 146 us
  Pallas kernels  44.6 us (31%)
  starting transfers between devices  42.1 us (29%)
  blocking collectives  32.4 us (22%)
  waiting for transfers between devices  24.3 us (17%)
  local copies, waits for them, and re-layouts  1.48 us (1%)
    all_to_all x1, blocking collectives, clips_to_devices(): return lax.all_to_all(sent, TIME, 0, 0, tiled=True)  32.4 us
    ppermute x12, starting transfers between devices, from_peer(): return lax.ppermute(x, axes, [(i, i ^ k) for i in range(4)])  15.7 us
    ppermute x6, starting transfers between devices, swapped(): return lax.ppermute(x, 'core', [(0, 1), (1, 0)])  15.7 us
    ppermute x12, waiting for transfers between devices, from_peer(): return lax.ppermute(x, axes, [(i, i ^ k) for i in range(4)])  9 us
    pallas_call x1, Pallas kernels, projector_back(): pl.pallas_call(functools.partial(projector_kernel, cell_count=cell_count)...  8.71 us
    all_to_all x1, waiting for transfers between devices, from_all(): lax.all_to_all(jnp.broadcast_to(x[None], (peers, *x.shape)), axes, 0, 0,...  8.46 us
    pallas_call x1, Pallas kernels, per_device(): plan.call(mixed_step, False, [here, 2, None, 'view', 'view'], [plan.maps_...  8.02 us
    all_to_all x1, starting transfers between devices, from_all(): lax.all_to_all(jnp.broadcast_to(x[None], (peers, *x.shape)), axes, 0, 0,...  7.92 us
  transfers between devices with their start and end apart: 21, of which 12 were waited for; matrix products, arithmetic and copies ran while one was open for 0% of the time, Pallas kernels for 4%

profile of v5, /device:TPU:1, one launch (start us, length us, event | category | flops | bytes accessed | tf_op | source)
XLA Modules:
  0.0 146.0 jit_solution(6962455892527502700)
XLA Ops:
  1.4 2.1 %shard_map.104 = bf16[8,1040,128]{2,1,0:T(8,128)(2,1)S(1)} custom-call(s32[5]{0:T(128)S(1)} %stack.53.place_ref, bf16[4,1024,128]{2,1,0:T(8,128)(2,1)} %bitcast.55, bf16[4,1024,128]{2,1,0:T(8,128)(2,1)} %bitcast.56, f32[2,4,128]{2,1,0:T(4,128)S(1)} %copy-done.2), custom_call_target="tpu_custom_call" | custom-call | tf_op jit(solution)/shard_map/pallas_call | solution.py:387
  3.6 32.4 %all_to_all.10.refs_0_ = bf16[8,1040,128]{2,1,0:T(8,128)(2,1)S(1)} all-to-all(bf16[8,1040,128]{2,1,0:T(8,128)(2,1)S(1)} %shard_map.104), channel_id=1, replica_groups=mesh['xh'=2,'xl'=2,'y'=4,'z'=4,'core'=2] {'xl','y'}, dimensions={0} | all-to-all | bytes 4259840 | tf_op jit(solution)/shard_map/all_to_all | solution.py:395
  36.0 5.1 %shard_map.105 = (bf16[32,8,2,16,128]{4,3,2,1,0:T(8,128)(2,1)S(1)}, f32[8,4,128]{2,1,0:T(4,128)S(1)}, f32[8,2,16,128]{3,2,1,0:T(8,128)S(1)}) custom-call(s32[5]{0:T(128)S(1)} %stack.53.place_ref, bf16[8,1040,128]{2,1,0:T(8,128)(2,1)S(1)} %all_to_all.10.refs_0_, bf16[2,1152,128]{2,1,0:T(8,128)(2,1)S(1)} %copy-done.3), custom_call_target="tpu_custom_call" | custom-call | flops 4831838208 | bytes 4194304 | tf_op jit(solution)/shard_map/pallas_call | solution.py:547
  41.1 1.7 %collective-permute-start = (f32[8,2,16,128]{3,2,1,0:T(8,128)S(1)}, f32[8,2,16,128]{3,2,1,0:T(8,128)S(1)}, u32[]{:S(2)}, u32[]{:S(2)}) collective-permute-start(f32[8,2,16,128]{3,2,1,0:T(8,128)S(1)} %get-tuple-element.13), channel_id=1, source_target_pairs={{0,96},{32,64},{64,32},{96,0},{1,97},{33,65},{65,33},{97,1},{2,98}... | collective-permute-start | bytes 393224 | tf_op jit(solution)/shard_map/ppermute | solution.py:481
  42.8 3.4 %collective-permute-done.refs_2_ = f32[8,2,16,128]{3,2,1,0:T(8,128)S(1)} collective-permute-done((f32[8,2,16,128]{3,2,1,0:T(8,128)S(1)}, f32[8,2,16,128]{3,2,1,0:T(8,128)S(1)}, u32[]{:S(2)}, u32[]{:S(2)}) %collective-permute-start) | collective-permute-done | bytes 131104 | tf_op jit(solution)/shard_map/ppermute | solution.py:481
  46.3 8.0 %shard_map.106 = (bf16[32,8,2,16,128]{4,3,2,1,0:T(8,128)(2,1)}, f32[32,8,2,16,128]{4,3,2,1,0:T(8,128)}, f32[1,128]{1,0:T(1,128)S(1)}) custom-call(s32[5]{0:T(128)S(1)} %stack.53.place_ref, bf16[32,8,2,16,128]{4,3,2,1,0:T(8,128)(2,1)S(1)} %get-tuple-element.11.refs_0_, f32[8,4,128]{2,1,0:T(4,128)S(1)} %get-tuple-element.12.refs_1_.refs_3_, ...), custom_call_target="tpu_custom_call" | custom-call | flops 4831838208 | bytes 4194304 | tf_op jit(solution)/shard_map/pallas_call | solution.py:556
  54.3 3.4 %collective-permute-start.1 = (f32[128]{0:T(128)S(1)}, f32[128]{0:T(128)S(1)}, u32[]{:S(2)}, u32[]{:S(2)}) collective-permute-start(f32[128]{0:T(128)S(1)} %bitcast.52), channel_id=1, source_target_pairs={{0,1},{1,0},{2,3},{3,2},{4,5},{5,4},{6,7},{7,6},{8,9},{9,8},{10,11... | collective-permute-start | bytes 1544 | tf_op jit(solution)/shard_map/ppermute | solution.py:340
  59.2 7.9 %all-to-all-start.1 = ((f32[64,2,128]{2,1,0:T(2,128)}), f32[64,2,128]{2,1,0:T(2,128)S(1)}, u32[]{:S(2)}, u32[]{:S(2)}) async-start(f32[64,2,128]{2,1,0:T(2,128)} %broadcast_in_dim.2), calls=%async_computation.1 | async-start | bytes 131072 | tf_op jit(solution)/shard_map/all_to_all | solution.py:351
  67.1 8.5 %all-to-all-done.1 = f32[64,2,128]{2,1,0:T(2,128)S(1)} async-done(((f32[64,2,128]{2,1,0:T(2,128)}), f32[64,2,128]{2,1,0:T(2,128)S(1)}, u32[]{:S(2)}, u32[]{:S(2)}) %all-to-all-start.1) | async-done | bytes 65568 | tf_op jit(solution)/shard_map/all_to_all | solution.py:351
  75.6 8.7 %shard_map.107.refs_2_.refs_5_ = f32[1,128]{1,0:T(1,128)S(1)} custom-call(s32[5]{0:T(128)S(1)} %stack.53.place_ref, f32[4,32,128]{2,1,0:T(8,128)S(1)} %bitcast.50, f32[128,2048]{1,0:T(8,128)S(1)} %copy-done, f32[1,2048]{1,0:T(1,128)S(1)} %bitcast.51, bf16[2048,2048]{1,0:T(8,128)(2,1)} %far_ref.1), custom_call_target="tpu_custom_call" | custom-call | flops 805306368 | bytes 8388608 | tf_op jit(solution)/shard_map/pallas_call | solution.py:461
  84.3 5.8 %shard_map.108 = (bf16[32,8,2,16,128]{4,3,2,1,0:T(8,128)(2,1)S(1)}, f32[32,8,2,16,128]{4,3,2,1,0:T(8,128)S(1)}, f32[8,2,16,128]{3,2,1,0:T(8,128)S(1)}) custom-call(s32[5]{0:T(128)S(1)} %stack.53.place_ref, f32[32,8,2,16,128]{4,3,2,1,0:T(8,128)S(1)} %copy-done.7, f32[8,4,128]{2,1,0:T(4,128)S(1)} %get-tuple-element.12.refs_1_.refs_3_, ...), custom_call_target="tpu_custom_call" | custom-call | flops 4831838208 | bytes 4194304 | tf_op jit(solution)/shard_map/pallas_call | solution.py:569
  91.2 5.7 %shard_map.110 = f32[1152,128]{1,0:T(8,128)S(1)} custom-call(s32[5]{0:T(128)S(1)} %stack.53.place_ref, bf16[32,8,2,16,128]{4,3,2,1,0:T(8,128)(2,1)S(1)} %copy-done.8, bf16[32,8,2,16,128]{4,3,2,1,0:T(8,128)(2,1)S(1)} %get-tuple-element.19.refs_1_), custom_call_target="tpu_custom_call" | custom-call | flops 4831838208 | bytes 4194304 | tf_op jit(solution)/shard_map/pallas_call | solution.py:578
  96.9 7.0 %shard_map.109 = f32[1152,128]{1,0:T(8,128)S(1)} custom-call(s32[5]{0:T(128)S(1)} %stack.53.place_ref, bf16[8,1040,128]{2,1,0:T(8,128)(2,1)S(1)} %all_to_all.10.refs_0_, f32[32,8,2,16,128]{4,3,2,1,0:T(8,128)S(1)} %copy-done.7, f32[32,8,2,16,128]{4,3,2,1,0:T(8,128)S(1)} %get-tuple-element.16.refs_2_, f32[8,4,128]{2,1,0:T(4,128)S(1)} %get-tuple-element.12.refs_1_.refs_3_, ...), custom_call_target="tpu_custom_call" | custom-call | flops 4831838208 | bytes 4194304 | tf_op jit(solution)/shard_map/pallas_call | solution.py:586
  103.9 2.0 %collective-permute-start.3 = (f32[2,4,144,128]{3,2,0,1:T(8,128)S(1)}, f32[2,4,144,128]{3,2,0,1:T(8,128)S(1)}, u32[]{:S(2)}, u32[]{:S(2)}) collective-permute-start(f32[2,4,144,128]{3,2,0,1:T(8,128)S(1)} %fusion.1), channel_id=1, source_target_pairs={{0,1},{1,0},{2,3},{3,2},{4,5},{5,4},{6,7},{7,6},{8,9},{9,8},{10,11... | collective-permute-start | bytes 1769480 | tf_op jit(solution)/shard_map/ppermute | solution.py:340
  106.0 1.6 %collective-permute-done.3 = f32[2,4,144,128]{3,2,0,1:T(8,128)S(1)} collective-permute-done((f32[2,4,144,128]{3,2,0,1:T(8,128)S(1)}, f32[2,4,144,128]{3,2,0,1:T(8,128)S(1)}, u32[]{:S(2)}, u32[]{:S(2)}) %collective-permute-start.3) | collective-permute-done | bytes 589856 | tf_op jit(solution)/shard_map/ppermute | solution.py:340
  108.1 1.9 %collective-permute-start.5 = (bf16[2,144,128]{2,1,0:T(8,128)(2,1)S(1)}, bf16[2,144,128]{2,1,0:T(8,128)(2,1)S(1)}, u32[]{:S(2)}, u32[]{:S(2)}) collective-permute-start(bf16[2,144,128]{2,1,0:T(8,128)(2,1)S(1)} %get-tuple-element.22), channel_id=1, source_target_pairs={{0,4},{2,6},{4,0},{6,2},{1,5},{3,7},{5,1},{7,3},{8,12},{10,14},{12... | collective-permute-start | bytes 221192 | tf_op jit(solution)/shard_map/ppermute | solution.py:485
  110.0 1.7 %collective-permute-start.6 = (bf16[2,144,128]{2,1,0:T(8,128)(2,1)S(1)}, bf16[2,144,128]{2,1,0:T(8,128)(2,1)S(1)}, u32[]{:S(2)}, u32[]{:S(2)}) collective-permute-start(bf16[2,144,128]{2,1,0:T(8,128)(2,1)S(1)} %get-tuple-element.21), channel_id=1, source_target_pairs={{0,6},{2,4},{4,2},{6,0},{1,7},{3,5},{5,3},{7,1},{8,14},{10,12},{12... | collective-permute-start | bytes 221192 | tf_op jit(solution)/shard_map/ppermute | solution.py:485
  111.6 2.2 %collective-permute-done.5 = bf16[2,144,128]{2,1,0:T(8,128)(2,1)S(1)} collective-permute-done((bf16[2,144,128]{2,1,0:T(8,128)(2,1)S(1)}, bf16[2,144,128]{2,1,0:T(8,128)(2,1)S(1)}, u32[]{:S(2)}, u32[]{:S(2)}) %collective-permute-start.5) | collective-permute-done | bytes 73760 | tf_op jit(solution)/shard_map/ppermute | solution.py:485
  113.8 1.1 collective-permute-done.6
  115.4 1.8 %collective-permute-start.8 = (bf16[2,144,128]{2,1,0:T(8,128)(2,1)S(1)}, bf16[2,144,128]{2,1,0:T(8,128)(2,1)S(1)}, u32[]{:S(2)}, u32[]{:S(2)}) collective-permute-start(bf16[2,144,128]{2,1,0:T(8,128)(2,1)S(1)} %fusion.8), channel_id=1, source_target_pairs={{0,16},{8,24},{16,0},{24,8},{1,17},{9,25},{17,1},{25,9},{2,18},{10... | collective-permute-start | bytes 221192 | tf_op jit(solution)/shard_map/ppermute | solution.py:485
  117.2 1.7 %collective-permute-start.9 = (bf16[2,144,128]{2,1,0:T(8,128)(2,1)S(1)}, bf16[2,144,128]{2,1,0:T(8,128)(2,1)S(1)}, u32[]{:S(2)}, u32[]{:S(2)}) collective-permute-start(bf16[2,144,128]{2,1,0:T(8,128)(2,1)S(1)} %fusion.8), channel_id=1, source_target_pairs={{0,24},{8,16},{16,8},{24,0},{1,25},{9,17},{17,9},{25,1},{2,26},{10... | collective-permute-start | bytes 221192 | tf_op jit(solution)/shard_map/ppermute | solution.py:485
  118.9 1.2 collective-permute-done.8
  120.1 1.5 %collective-permute-done.9 = bf16[2,144,128]{2,1,0:T(8,128)(2,1)S(1)} collective-permute-done((bf16[2,144,128]{2,1,0:T(8,128)(2,1)S(1)}, bf16[2,144,128]{2,1,0:T(8,128)(2,1)S(1)}, u32[]{:S(2)}, u32[]{:S(2)}) %collective-permute-start.9) | collective-permute-done | bytes 73760 | tf_op jit(solution)/shard_map/ppermute | solution.py:485
  121.6 2.3 %collective-permute-start.10 = (bf16[2,144,128]{2,1,0:T(8,128)(2,1)S(1)}, bf16[2,144,128]{2,1,0:T(8,128)(2,1)S(1)}, u32[]{:S(2)}, u32[]{:S(2)}) collective-permute-start(bf16[2,144,128]{2,1,0:T(8,128)(2,1)S(1)} %add_convert_fusion.2), channel_id=1, source_target_pairs={{0,96},{32,64},{64,32},{96,0},{1,97},{33,65},{65,33},{97,1},{2,98}... | collective-permute-start | bytes 221192 | tf_op jit(solution)/shard_map/ppermute | solution.py:485
  123.9 1.6 %collective-permute-start.12 = (bf16[2,144,128]{2,1,0:T(8,128)(2,1)S(1)}, bf16[2,144,128]{2,1,0:T(8,128)(2,1)S(1)}, u32[]{:S(2)}, u32[]{:S(2)}) collective-permute-start(bf16[2,144,128]{2,1,0:T(8,128)(2,1)S(1)} %add_convert_fusion.2), channel_id=1, source_target_pairs={{0,64},{32,96},{64,0},{96,32},{1,65},{33,97},{65,1},{97,33},{2,66}... | collective-permute-start | bytes 221192 | tf_op jit(solution)/shard_map/ppermute | solution.py:485
  127.1 1.5 %collective-permute-done.12 = bf16[2,144,128]{2,1,0:T(8,128)(2,1)S(1)} collective-permute-done((bf16[2,144,128]{2,1,0:T(8,128)(2,1)S(1)}, bf16[2,144,128]{2,1,0:T(8,128)(2,1)S(1)}, u32[]{:S(2)}, u32[]{:S(2)}) %collective-permute-start.12) | collective-permute-done | bytes 73760 | tf_op jit(solution)/shard_map/ppermute | solution.py:485
  128.8 2.5 %collective-permute-start.14 = (bf16[2,2,144,128]{3,2,1,0:T(8,128)(2,1)S(1)}, bf16[2,2,144,128]{3,2,1,0:T(8,128)(2,1)S(1)}, u32[]{:S(2)}, u32[]{:S(2)}) collective-permute-start(bf16[2,2,144,128]{3,2,1,0:T(8,128)(2,1)S(1)} %pad_maximum_fusion.refs_0_), channel_id=1, source_target_pairs={{0,4},{2,6},{4,0},{6,2},{1,5},{3,7},{5,1},{7,3},{8,12},{10,14},{12... | collective-permute-start | bytes 442376 | tf_op jit(solution)/shard_map/ppermute | solution.py:485
  131.3 1.4 collective-permute-start.15
  132.6 5.2 %collective-permute-start.16 = (bf16[2,2,144,128]{3,2,1,0:T(8,128)(2,1)S(1)}, bf16[2,2,144,128]{3,2,1,0:T(8,128)(2,1)S(1)}, u32[]{:S(2)}, u32[]{:S(2)}) collective-permute-start(bf16[2,2,144,128]{3,2,1,0:T(8,128)(2,1)S(1)} %pad_maximum_fusion.refs_0_), channel_id=1, source_target_pairs={{0,1},{1,0},{2,3},{3,2},{4,5},{5,4},{6,7},{7,6},{8,9},{9,8},{10,11... | collective-permute-start | bytes 442376 | tf_op jit(solution)/shard_map/ppermute | solution.py:340
  138.3 3.0 %collective-permute-start.18 = (bf16[2,2,144,128]{3,2,1,0:T(8,128)(2,1)S(1)}, bf16[2,2,144,128]{3,2,1,0:T(8,128)(2,1)S(1)}, u32[]{:S(2)}, u32[]{:S(2)}) collective-permute-start(bf16[2,2,144,128]{3,2,1,0:T(8,128)(2,1)S(1)} %collective-permute-done.14.refs_2_), channel_id=1, source_target_pairs={{0,1},{1,0},{2,3},{3,2},{4,5},{5,4},{6,7},{7,6},{8,9},{9,8},{10,11... | collective-permute-start | bytes 442376 | tf_op jit(solution)/shard_map/ppermute | solution.py:340
  141.3 1.7 %collective-permute-start.19 = (bf16[2,2,144,128]{3,2,1,0:T(8,128)(2,1)S(1)}, bf16[2,2,144,128]{3,2,1,0:T(8,128)(2,1)S(1)}, u32[]{:S(2)}, u32[]{:S(2)}) collective-permute-start(bf16[2,2,144,128]{3,2,1,0:T(8,128)(2,1)S(1)} %collective-permute-done.15.refs_3_), channel_id=1, source_target_pairs={{0,1},{1,0},{2,3},{3,2},{4,5},{5,4},{6,7},{7,6},{8,9},{9,8},{10,11... | collective-permute-start | bytes 442376 | tf_op jit(solution)/shard_map/ppermute | solution.py:340
  143.9 2.1 %shard_map.111 = (f32[2,1152,128]{2,1,0:T(8,128)}, f32[2,1152,128]{2,1,0:T(8,128)}) custom-call(s32[5]{0:T(128)S(1)} %stack.53.place_ref, bf16[2,2,144,128]{3,2,1,0:T(8,128)(2,1)S(1)} %pad_maximum_fusion.refs_0_, bf16[2,2,144,128]{3,2,1,0:T(8,128)(2,1)S(1)} %collective-permute-done.13.refs_1_, bf16[2,2,144,128]{3,2,1,0:T(8,128)(2,1)S(1)} %collective-permute-done.14.refs_2_, ...), custom_call_target="tpu_custom_call" | custom-call | tf_op jit(solution)/shard_map/pallas_call | solution.py:524
  (49 shorter events, 7.5 us)
Async XLA Ops:
  0.7 0.7 copy-start.2
  3.5 32.4 %copy-start.3 = (bf16[2,1152,128]{2,1,0:T(8,128)(2,1)S(1)}, bf16[2,1152,128]{2,1,0:T(8,128)(2,1)}, u32[]{:S(2)}) copy-start(bf16[2,1152,128]{2,1,0:T(8,128)(2,1)} %refs_1_.1) | copy-start | bytes 1769476
  36.0 10.3 %copy-start.4 = (bf16[2,1152,128]{2,1,0:T(8,128)(2,1)S(1)}, bf16[2,1152,128]{2,1,0:T(8,128)(2,1)}, u32[]{:S(2)}) copy-start(bf16[2,1152,128]{2,1,0:T(8,128)(2,1)} %refs_3_.1) | copy-start | bytes 1769476
  36.0 10.3 %copy-start.6 = (f32[2,128]{1,0:T(2,128)S(1)}, f32[2,128]{1,0:T(2,128)}, u32[]{:S(2)}) copy-start(f32[2,128]{1,0:T(2,128)} %param.14) | copy-start | bytes 3076
  41.1 5.1 %collective-permute-start = (f32[8,2,16,128]{3,2,1,0:T(8,128)S(1)}, f32[8,2,16,128]{3,2,1,0:T(8,128)S(1)}, u32[]{:S(2)}, u32[]{:S(2)}) collective-permute-start(f32[8,2,16,128]{3,2,1,0:T(8,128)S(1)} %get-tuple-element.13), channel_id=1, source_target_pairs={{0,96},{32,64},{64,32},{96,0},{1,97},{33,65},{65,33},{97,1},{2,98}... | collective-permute-start | bytes 393224 | tf_op jit(solution)/shard_map/ppermute | solution.py:481
  46.3 29.3 %copy-start = (f32[128,2048]{1,0:T(8,128)S(1)}, f32[128,2048]{1,0:T(8,128)}, u32[]{:S(2)}) copy-start(f32[128,2048]{1,0:T(8,128)} %in_ref.1) | copy-start | bytes 3145732
  46.3 29.3 %copy-start.1 = (f32[2048]{0:T(1024)S(1)}, f32[2048]{0:T(1024)}, u32[]{:S(2)}) copy-start(f32[2048]{0:T(1024)} %param.16) | copy-start | bytes 24580
  54.3 4.2 %collective-permute-start.1 = (f32[128]{0:T(128)S(1)}, f32[128]{0:T(128)S(1)}, u32[]{:S(2)}, u32[]{:S(2)}) collective-permute-start(f32[128]{0:T(128)S(1)} %bitcast.52), channel_id=1, source_target_pairs={{0,1},{1,0},{2,3},{3,2},{4,5},{5,4},{6,7},{7,6},{8,9},{9,8},{10,11... | collective-permute-start | bytes 1544 | tf_op jit(solution)/shard_map/ppermute | solution.py:340
  59.2 16.4 %all-to-all-start.1 = ((f32[64,2,128]{2,1,0:T(2,128)}), f32[64,2,128]{2,1,0:T(2,128)S(1)}, u32[]{:S(2)}, u32[]{:S(2)}) async-start(f32[64,2,128]{2,1,0:T(2,128)} %broadcast_in_dim.2), calls=%async_computation.1 | async-start | bytes 131072 | tf_op jit(solution)/shard_map/all_to_all | solution.py:351
  75.6 8.7 %copy-start.5 = (bf16[2,1152,128]{2,1,0:T(8,128)(2,1)S(1)}, bf16[2,1152,128]{2,1,0:T(8,128)(2,1)}, u32[]{:S(2)}) copy-start(bf16[2,1152,128]{2,1,0:T(8,128)(2,1)} %refs_3_.1) | copy-start | bytes 1769476
  75.6 8.7 %copy-start.7 = (f32[32,8,2,16,128]{4,3,2,1,0:T(8,128)S(1)}, f32[32,8,2,16,128]{4,3,2,1,0:T(8,128)}, u32[]{:S(2)}) copy-start(f32[32,8,2,16,128]{4,3,2,1,0:T(8,128)} %get-tuple-element.14.refs_0_.refs_1_) | copy-start | bytes 12582916
  84.3 6.9 %copy-start.8 = (bf16[32,8,2,16,128]{4,3,2,1,0:T(8,128)(2,1)S(1)}, bf16[32,8,2,16,128]{4,3,2,1,0:T(8,128)(2,1)}, u32[]{:S(2)}) copy-start(bf16[32,8,2,16,128]{4,3,2,1,0:T(8,128)(2,1)} %get-tuple-element.18.refs_0_) | copy-start | bytes 6291460
  90.2 6.7 %collective-permute-start.2 = (f32[8,2,16,128]{3,2,1,0:T(8,128)S(1)}, f32[8,2,16,128]{3,2,1,0:T(8,128)S(1)}, u32[]{:S(2)}, u32[]{:S(2)}) collective-permute-start(f32[8,2,16,128]{3,2,1,0:T(8,128)S(1)} %get-tuple-element.17), channel_id=1, source_target_pairs={{0,96},{32,64},{64,32},{96,0},{1,97},{33,65},{65,33},{97,1},{2,98}... | collective-permute-start | bytes 393224 | tf_op jit(solution)/shard_map/ppermute | solution.py:481
  103.9 3.7 %collective-permute-start.3 = (f32[2,4,144,128]{3,2,0,1:T(8,128)S(1)}, f32[2,4,144,128]{3,2,0,1:T(8,128)S(1)}, u32[]{:S(2)}, u32[]{:S(2)}) collective-permute-start(f32[2,4,144,128]{3,2,0,1:T(8,128)S(1)} %fusion.1), channel_id=1, source_target_pairs={{0,1},{1,0},{2,3},{3,2},{4,5},{5,4},{6,7},{7,6},{8,9},{9,8},{10,11... | collective-permute-start | bytes 1769480 | tf_op jit(solution)/shard_map/ppermute | solution.py:340
  107.7 3.9 %collective-permute-start.4 = (bf16[2,144,128]{2,1,0:T(8,128)(2,1)S(1)}, bf16[2,144,128]{2,1,0:T(8,128)(2,1)S(1)}, u32[]{:S(2)}, u32[]{:S(2)}) collective-permute-start(bf16[2,144,128]{2,1,0:T(8,128)(2,1)S(1)} %get-tuple-element.20), channel_id=1, source_target_pairs={{0,2},{2,0},{4,6},{6,4},{1,3},{3,1},{5,7},{7,5},{8,10},{10,8},{12,... | collective-permute-start | bytes 221192 | tf_op jit(solution)/shard_map/ppermute | solution.py:485
  108.1 5.7 %collective-permute-start.5 = (bf16[2,144,128]{2,1,0:T(8,128)(2,1)S(1)}, bf16[2,144,128]{2,1,0:T(8,128)(2,1)S(1)}, u32[]{:S(2)}, u32[]{:S(2)}) collective-permute-start(bf16[2,144,128]{2,1,0:T(8,128)(2,1)S(1)} %get-tuple-element.22), channel_id=1, source_target_pairs={{0,4},{2,6},{4,0},{6,2},{1,5},{3,7},{5,1},{7,3},{8,12},{10,14},{12... | collective-permute-start | bytes 221192 | tf_op jit(solution)/shard_map/ppermute | solution.py:485
  110.0 4.9 %collective-permute-start.6 = (bf16[2,144,128]{2,1,0:T(8,128)(2,1)S(1)}, bf16[2,144,128]{2,1,0:T(8,128)(2,1)S(1)}, u32[]{:S(2)}, u32[]{:S(2)}) collective-permute-start(bf16[2,144,128]{2,1,0:T(8,128)(2,1)S(1)} %get-tuple-element.21), channel_id=1, source_target_pairs={{0,6},{2,4},{4,2},{6,0},{1,7},{3,5},{5,3},{7,1},{8,14},{10,12},{12... | collective-permute-start | bytes 221192 | tf_op jit(solution)/shard_map/ppermute | solution.py:485
  115.0 3.9 %collective-permute-start.7 = (bf16[2,144,128]{2,1,0:T(8,128)(2,1)S(1)}, bf16[2,144,128]{2,1,0:T(8,128)(2,1)S(1)}, u32[]{:S(2)}, u32[]{:S(2)}) collective-permute-start(bf16[2,144,128]{2,1,0:T(8,128)(2,1)S(1)} %fusion.8), channel_id=1, source_target_pairs={{0,8},{8,0},{16,24},{24,16},{1,9},{9,1},{17,25},{25,17},{2,10},{10... | collective-permute-start | bytes 221192 | tf_op jit(solution)/shard_map/ppermute | solution.py:485
  115.4 4.7 %collective-permute-start.8 = (bf16[2,144,128]{2,1,0:T(8,128)(2,1)S(1)}, bf16[2,144,128]{2,1,0:T(8,128)(2,1)S(1)}, u32[]{:S(2)}, u32[]{:S(2)}) collective-permute-start(bf16[2,144,128]{2,1,0:T(8,128)(2,1)S(1)} %fusion.8), channel_id=1, source_target_pairs={{0,16},{8,24},{16,0},{24,8},{1,17},{9,25},{17,1},{25,9},{2,18},{10... | collective-permute-start | bytes 221192 | tf_op jit(solution)/shard_map/ppermute | solution.py:485
  117.2 4.4 %collective-permute-start.9 = (bf16[2,144,128]{2,1,0:T(8,128)(2,1)S(1)}, bf16[2,144,128]{2,1,0:T(8,128)(2,1)S(1)}, u32[]{:S(2)}, u32[]{:S(2)}) collective-permute-start(bf16[2,144,128]{2,1,0:T(8,128)(2,1)S(1)} %fusion.8), channel_id=1, source_target_pairs={{0,24},{8,16},{16,8},{24,0},{1,25},{9,17},{17,9},{25,1},{2,26},{10... | collective-permute-start | bytes 221192 | tf_op jit(solution)/shard_map/ppermute | solution.py:485
  121.6 4.5 %collective-permute-start.10 = (bf16[2,144,128]{2,1,0:T(8,128)(2,1)S(1)}, bf16[2,144,128]{2,1,0:T(8,128)(2,1)S(1)}, u32[]{:S(2)}, u32[]{:S(2)}) collective-permute-start(bf16[2,144,128]{2,1,0:T(8,128)(2,1)S(1)} %add_convert_fusion.2), channel_id=1, source_target_pairs={{0,96},{32,64},{64,32},{96,0},{1,97},{33,65},{65,33},{97,1},{2,98}... | collective-permute-start | bytes 221192 | tf_op jit(solution)/shard_map/ppermute | solution.py:485
  123.9 3.2 %collective-permute-start.11 = (bf16[2,144,128]{2,1,0:T(8,128)(2,1)S(1)}, bf16[2,144,128]{2,1,0:T(8,128)(2,1)S(1)}, u32[]{:S(2)}, u32[]{:S(2)}) collective-permute-start(bf16[2,144,128]{2,1,0:T(8,128)(2,1)S(1)} %add_convert_fusion.2), channel_id=1, source_target_pairs={{0,32},{32,0},{64,96},{96,64},{1,33},{33,1},{65,97},{97,65},{2,34}... | collective-permute-start | bytes 221192 | tf_op jit(solution)/shard_map/ppermute | solution.py:485
  123.9 4.7 %collective-permute-start.12 = (bf16[2,144,128]{2,1,0:T(8,128)(2,1)S(1)}, bf16[2,144,128]{2,1,0:T(8,128)(2,1)S(1)}, u32[]{:S(2)}, u32[]{:S(2)}) collective-permute-start(bf16[2,144,128]{2,1,0:T(8,128)(2,1)S(1)} %add_convert_fusion.2), channel_id=1, source_target_pairs={{0,64},{32,96},{64,0},{96,32},{1,65},{33,97},{65,1},{97,33},{2,66}... | collective-permute-start | bytes 221192 | tf_op jit(solution)/shard_map/ppermute | solution.py:485
  128.7 9.2 %collective-permute-start.13 = (bf16[2,2,144,128]{3,2,1,0:T(8,128)(2,1)S(1)}, bf16[2,2,144,128]{3,2,1,0:T(8,128)(2,1)S(1)}, u32[]{:S(2)}, u32[]{:S(2)}) collective-permute-start(bf16[2,2,144,128]{3,2,1,0:T(8,128)(2,1)S(1)} %pad_maximum_fusion.refs_0_), channel_id=1, source_target_pairs={{0,2},{2,0},{4,6},{6,4},{1,3},{3,1},{5,7},{7,5},{8,10},{10,8},{12,... | collective-permute-start | bytes 442376 | tf_op jit(solution)/shard_map/ppermute | solution.py:485
  128.8 9.5 %collective-permute-start.14 = (bf16[2,2,144,128]{3,2,1,0:T(8,128)(2,1)S(1)}, bf16[2,2,144,128]{3,2,1,0:T(8,128)(2,1)S(1)}, u32[]{:S(2)}, u32[]{:S(2)}) collective-permute-start(bf16[2,2,144,128]{3,2,1,0:T(8,128)(2,1)S(1)} %pad_maximum_fusion.refs_0_), channel_id=1, source_target_pairs={{0,4},{2,6},{4,0},{6,2},{1,5},{3,7},{5,1},{7,3},{8,12},{10,14},{12... | collective-permute-start | bytes 442376 | tf_op jit(solution)/shard_map/ppermute | solution.py:485
  131.3 10.0 %collective-permute-start.15 = (bf16[2,2,144,128]{3,2,1,0:T(8,128)(2,1)S(1)}, bf16[2,2,144,128]{3,2,1,0:T(8,128)(2,1)S(1)}, u32[]{:S(2)}, u32[]{:S(2)}) collective-permute-start(bf16[2,2,144,128]{3,2,1,0:T(8,128)(2,1)S(1)} %pad_maximum_fusion.refs_0_), channel_id=1, source_target_pairs={{0,6},{2,4},{4,2},{6,0},{1,7},{3,5},{5,3},{7,1},{8,14},{10,12},{12... | collective-permute-start | bytes 442376 | tf_op jit(solution)/shard_map/ppermute | solution.py:485
  132.6 10.3 %collective-permute-start.16 = (bf16[2,2,144,128]{3,2,1,0:T(8,128)(2,1)S(1)}, bf16[2,2,144,128]{3,2,1,0:T(8,128)(2,1)S(1)}, u32[]{:S(2)}, u32[]{:S(2)}) collective-permute-start(bf16[2,2,144,128]{3,2,1,0:T(8,128)(2,1)S(1)} %pad_maximum_fusion.refs_0_), channel_id=1, source_target_pairs={{0,1},{1,0},{2,3},{3,2},{4,5},{5,4},{6,7},{7,6},{8,9},{9,8},{10,11... | collective-permute-start | bytes 442376 | tf_op jit(solution)/shard_map/ppermute | solution.py:340
  137.9 5.1 %collective-permute-start.17 = (bf16[2,2,144,128]{3,2,1,0:T(8,128)(2,1)S(1)}, bf16[2,2,144,128]{3,2,1,0:T(8,128)(2,1)S(1)}, u32[]{:S(2)}, u32[]{:S(2)}) collective-permute-start(bf16[2,2,144,128]{3,2,1,0:T(8,128)(2,1)S(1)} %collective-permute-done.13.refs_1_), channel_id=1, source_target_pairs={{0,1},{1,0},{2,3},{3,2},{4,5},{5,4},{6,7},{7,6},{8,9},{9,8},{10,11... | collective-permute-start | bytes 442376 | tf_op jit(solution)/shard_map/ppermute | solution.py:340
  138.3 4.6 %collective-permute-start.18 = (bf16[2,2,144,128]{3,2,1,0:T(8,128)(2,1)S(1)}, bf16[2,2,144,128]{3,2,1,0:T(8,128)(2,1)S(1)}, u32[]{:S(2)}, u32[]{:S(2)}) collective-permute-start(bf16[2,2,144,128]{3,2,1,0:T(8,128)(2,1)S(1)} %collective-permute-done.14.refs_2_), channel_id=1, source_target_pairs={{0,1},{1,0},{2,3},{3,2},{4,5},{5,4},{6,7},{7,6},{8,9},{9,8},{10,11... | collective-permute-start | bytes 442376 | tf_op jit(solution)/shard_map/ppermute | solution.py:340
  141.3 2.7 %collective-permute-start.19 = (bf16[2,2,144,128]{3,2,1,0:T(8,128)(2,1)S(1)}, bf16[2,2,144,128]{3,2,1,0:T(8,128)(2,1)S(1)}, u32[]{:S(2)}, u32[]{:S(2)}) collective-permute-start(bf16[2,2,144,128]{3,2,1,0:T(8,128)(2,1)S(1)} %collective-permute-done.15.refs_3_), channel_id=1, source_target_pairs={{0,1},{1,0},{2,3},{3,2},{4,5},{5,4},{6,7},{7,6},{8,9},{9,8},{10,11... | collective-permute-start | bytes 442376 | tf_op jit(solution)/shard_map/ppermute | solution.py:340

commit v6 on v5

--- a/solution.py
+++ b/solution.py
@@ -124,33 +124,40 @@
     return decays_ref[t // group, t % group : t % group + 1]
 
 
-def inputs_step(step, last, place_ref, got_ref, weights_ref, inputs_ref, decays_ref, end_ref, cols_a, cols_b, both_ref, carry_ref):
-    cols = (cols_a, cols_b)
+def pair_kernel(place_ref, weights_ref, both_ref):
+    pair_weights(weights_ref.at[pl.ds(place_ref[1], 1)], both_ref)
+
+
+def piece_kernel(piece_ref, both_ref, inputs_ref, cols_ref):
     frames, _, _, side, _ = inputs_ref.shape
-    group = frames // 2
-    cells = group * side * side
-
-    @pl.when(step == 0)
-    def _():
-        clear_edges(cols_a)
-        clear_edges(cols_b)
-        pair_weights(weights_ref, both_ref)
-        carry_ref[...] = jnp.zeros_like(carry_ref)
-
-    spread_groups(got_maps(got_ref, inputs_ref.shape), cols)
-    for h in range(2):
-        parts = got_ref[h, cells:].astype(F32)
-        decays_ref[h] = parts[:group] + parts[group : 2 * group] + parts[2 * group : 3 * group]
-        for k, rows in enumerate(pair_convolve(cols[h], both_ref)):
-            inputs_ref[h * group : (h + 1) * group, :, k] = rows.astype(BF16)
-    carried = carry_ref[...]
-    for t in range(frames):
-        carried = decay_of(decays_ref, t) * carried + inputs_ref[t].astype(F32)
-    carry_ref[...] = carried
-
-    @pl.when(step == last)
-    def _():
+    clear_edges(cols_ref)
+    spread_columns(piece_ref[: frames * side * side].reshape(inputs_ref.shape), cols_ref)
+    for k, rows in enumerate(pair_convolve(cols_ref, both_ref)):
+        inputs_ref[:, :, k] = rows.astype(BF16)
+
+
+def order_kernel(place_ref, *refs):
+    for k in range(8):
+        refs[8][place_ref[5] ^ k] = refs[k][...]
+
+
+def gather_kernel(place_ref, *refs):
+    pieces, convolved, (inputs_ref, decays_ref, end_ref) = refs[:8], refs[8:16], refs[16:]
+    group = convolved[0].shape[0]
+    cells = pieces[0].shape[0] - 16
+    for k in range(8):
+        sender = place_ref[5] ^ k
+        inputs_ref[pl.ds(sender * group, group)] = convolved[k][...]
+        parts = pieces[k][cells:].astype(F32)
+        decays_ref[sender] = parts[:group] + parts[group : 2 * group] + parts[2 * group : 3 * group]
+
+    def advance(t, carried):
+        for n in range(group):
+            carried = decays_ref[t, n : n + 1] * carried + inputs_ref[t * group + n].astype(F32)
         end_ref[...] = carried
+        return carried
+
+    lax.fori_loop(0, 8, advance, jnp.zeros(end_ref.shape, F32))
 
 
 def mixed_step(step, last, place_ref, inputs_ref, decays_ref, income_ref, skip_ref, weights_ref, states_ref, slope_ref, pooled_ref, cols_a, cols_b, both_ref, carry_ref, sum_ref):
@@ -284,6 +291,16 @@
     def both(self):
         return pltpu.VMEM((12 * self.channels, 2 * self.channels), BF16)
 
+    def small(self, kernel, arity, out_shape, scratch=(), placed=True):
+        vmem = pl.BlockSpec(memory_space=pltpu.VMEM)
+        return pl.pallas_call(
+            kernel,
+            out_shape=out_shape,
+            in_specs=[pl.BlockSpec(memory_space=pltpu.SMEM) if placed else vmem] + [vmem] * (arity - 1),
+            scratch_shapes=list(scratch),
+            compiler_params=pltpu.CompilerParams(vmem_limit_bytes=16 << 20),
+        )
+
     def call(self, run, back, takes, out_shape, gives, scratch, kept=()):
         cells = self.steps * self.frames * self.side * self.side
         work = 2 * 9 * cells * self.channels * self.channels
@@ -319,7 +336,11 @@
                     copy_of(k, at).start()
                 return 0
 
-            lax.fori_loop(0, self.steps, step, 0)
+            if kept:
+                lax.fori_loop(0, self.steps, step, 0)
+            else:
+                for i in range(self.steps):
+                    step(i, 0)
             for k in range(len(kept)):
                 for i in range(self.steps):
                     copy_of(k, i).wait()
@@ -355,29 +376,38 @@
     return pltpu.with_memory_space_constraint(x, pltpu.HBM)
 
 
-def pack_kernel(place_ref, rgb_ref, flow_ref, decay_ref, sent_ref, map_sems):
-    half = place_ref[0]
+def pack_kernel(place_ref, rgb_ref, flow_ref, decay_ref, *refs):
+    sent, (parts_ref, sems, part_sem) = refs[:8], refs[8:]
+    view, clip = place_ref[1], place_ref[6]
     clips, cells, channels = rgb_ref.shape
     frames = decay_ref.shape[1]
-    copies = []
-    for v, maps_ref in enumerate((rgb_ref, flow_ref)):
-        for c in range(clips):
-            to = sent_ref.at[(v ^ half) * clips + c, :cells]
-            copies.append(pltpu.make_async_copy(maps_ref.at[c], to, map_sems.at[v, c]))
-    for copy in copies:
-        copy.start()
-    for v in range(2):
-        decays = decay_ref[v]
+
+    def copy_of(maps_ref, k):
+        return pltpu.make_async_copy(maps_ref.at[clip ^ (k % clips)], sent[k].at[:cells], sems.at[k])
+
+    decay_copy = pltpu.make_async_copy(decay_ref, parts_ref, part_sem)
+    decay_copy.start()
+    for second in range(2):
+        for v, maps_ref in enumerate((rgb_ref, flow_ref)):
+
+            @pl.when((view ^ second) == v)
+            def _(second=second, maps_ref=maps_ref):
+                for k in range(second * clips, (second + 1) * clips):
+                    copy_of(maps_ref, k).start()
+
+    decay_copy.wait()
+    for second in range(2):
+        decays = parts_ref[view ^ second]
         high = decays.astype(BF16).astype(F32)
         middle = (decays - high).astype(BF16).astype(F32)
         low = decays - high - middle
-        rows = sent_ref.shape[1] - cells
+        rows = sent[0].shape[0] - cells
         parts = [high, middle, low, jnp.zeros((rows - 3 * frames, channels), F32)]
         parts = jnp.concatenate(parts).astype(BF16)
-        for c in range(clips):
-            sent_ref[(v ^ half) * clips + c, cells:] = parts
-    for copy in copies:
-        copy.wait()
+        for k in range(second * clips, (second + 1) * clips):
+            sent[k][cells:] = parts
+    for k in range(2 * clips):
+        copy_of(rgb_ref, k).wait()
 
 
 def clips_to_devices(rgb_maps, flow_maps, decay, place):
@@ -386,13 +416,18 @@
     hbm = pl.BlockSpec(memory_space=pltpu.HBM)
     sent = pl.pallas_call(
         pack_kernel,
-        out_shape=jax.ShapeDtypeStruct((2 * clips, cells + 16, channels), BF16),
-        in_specs=[pl.BlockSpec(memory_space=pltpu.SMEM), hbm, hbm, pl.BlockSpec(memory_space=pltpu.VMEM)],
-        out_specs=pl.BlockSpec(memory_space=pltpu.VMEM),
-        scratch_shapes=[pltpu.SemaphoreType.DMA((2, clips))],
+        out_shape=[jax.ShapeDtypeStruct((cells + 16, channels), BF16)] * (2 * clips),
+        in_specs=[pl.BlockSpec(memory_space=pltpu.SMEM), hbm, hbm, hbm],
+        out_specs=[pl.BlockSpec(memory_space=pltpu.VMEM)] * (2 * clips),
+        scratch_shapes=[
+            pltpu.VMEM(decay.shape, F32),
+            pltpu.SemaphoreType.DMA((2 * clips,)),
+            pltpu.SemaphoreType.DMA,
+        ],
         compiler_params=pltpu.CompilerParams(vmem_limit_bytes=16 << 20),
-    )(place, *(in_hbm(maps.reshape(clips, cells, channels)) for maps in (rgb_maps, flow_maps)), decay)
-    return lax.all_to_all(sent, TIME, 0, 0, tiled=True)
+    )(place, *(in_hbm(maps.reshape(clips, cells, channels)) for maps in (rgb_maps, flow_maps)), in_hbm(decay))
+    peers = 2 * clips
+    return [sent[0]] + [lax.ppermute(sent[k], TIME, [(i, i ^ k) for i in range(peers)]) for k in range(1, peers)]
 
 
 def batch_norm(values):
@@ -536,22 +571,21 @@
     half = lax.axis_index("xh")
     view = lax.axis_index("xl") ^ half
     _, frames_here, side, _, channels = rgb_maps.shape
-    place = jnp.stack([half, view, lax.axis_index("core"), lax.axis_index("z"), lax.axis_index(("y", "z", "core"))])
+    place = jnp.stack([half, view, lax.axis_index("core"), lax.axis_index("z"), lax.axis_index(("y", "z", "core")), lax.axis_index(TIME), lax.axis_index("y")])
     place = place.astype(jnp.int32)
-    got = clips_to_devices(rgb_maps, flow_maps, decay, place)
-    senders, rows, _ = got.shape
+    pieces = clips_to_devices(rgb_maps, flow_maps, decay, place)
+    senders = len(pieces)
     cell_count = 2 * senders * frames_here * side * side
     plan = Plan(senders, frames_here, side, channels)
     skips = skip.reshape(2, 1, channels)
     here = plan.frames
-    inputs, decays, end = plan.call(
-        inputs_step,
-        False,
-        [2, "view"],
-        [plan.maps_of(BF16), plan.decays_of(), plan.carry_of()],
-        [here, 2, None],
-        [*plan.cols(), plan.both(), plan.carry()],
-    )(place, got, in_weights)
+    both = plan.small(pair_kernel, 2, jax.ShapeDtypeStruct((12 * channels, 2 * channels), BF16))(place, in_weights)
+    piece_of = jax.ShapeDtypeStruct((frames_here, *plan.map), BF16)
+    convolved = [plan.small(piece_kernel, 2, piece_of, plan.cols()[:1], False)(piece, both) for piece in pieces]
+    inputs, decays, end = plan.small(gather_kernel, 17, [plan.maps_of(BF16), plan.decays_of(), plan.carry_of()])(
+        place, *pieces, *convolved
+    )
+    got = plan.small(order_kernel, 9, jax.ShapeDtypeStruct((senders, *pieces[0].shape), BF16))(place, *pieces)
     income = from_other_half(end)
     states_b, slope, pooled_part = plan.call(
         mixed_step,

time: 146 us -> 142 us (0.973)
  blocking collectives: 32.4 us -> 0 us
  waiting for transfers between devices: 24.3 us -> 39.9 us
  starting transfers between devices: 42.1 us -> 55.2 us
    all_to_all x1 -> x0, blocking collectives: 32.4 us -> none  [clips_to_devices(): return lax.all_to_all(sent, TIME, 0, 0, tiled=True)]
    ppermute x0 -> x7, waiting for transfers between devices: none -> 18.2 us  [clips_to_devices(): lax.ppermute(sent[k], TIME, [(i, i ^ k) for i in range(peers)])]
    ppermute x0 -> x7, starting transfers between devices: none -> 13 us  [clips_to_devices(): lax.ppermute(sent[k], TIME, [(i, i ^ k) for i in range(peers)])]
    all_to_all x1, waiting for transfers between devices: 8.46 us -> 6.17 us  [from_all(): lax.all_to_all(jnp.broadcast_to(x[None], (peers, *x.shape)), axes, 0, 0,...]
    pallas_call x2 -> x12, Pallas kernels: 7.26 us -> 9.4 us  [the longest x8 4.78 us: per_device(): plan.small(piece_kernel, 2, piece_of, plan.cols()[:1], False)(piece, both)]
    pallas_call x1, Pallas kernels: 6.96 us -> 5.46 us  [per_device(): plan.call(in_grad_step, True, [2, here, here, 2, None, None, 'view'], [pl...]
  transfers between devices with their start and end apart: 21 -> 28, of which waited for: 12 -> 16; matrix products, arithmetic and copies ran while one was open for 0% -> 0% of each run, Pallas kernels for 4% -> 7%
where the time goes in v6:
time: 142 us
  starting transfers between devices  55.2 us (39%)
  Pallas kernels  43.5 us (31%)
  waiting for transfers between devices  39.9 us (28%)
  local copies, waits for them, and re-layouts  2.18 us (2%)
    ppermute x7, waiting for transfers between devices, clips_to_devices(): lax.ppermute(sent[k], TIME, [(i, i ^ k) for i in range(peers)])  18.2 us
    ppermute x12, starting transfers between devices, from_peer(): return lax.ppermute(x, axes, [(i, i ^ k) for i in range(4)])  15.7 us
    ppermute x6, starting transfers between devices, swapped(): return lax.ppermute(x, 'core', [(0, 1), (1, 0)])  14.4 us
    ppermute x7, starting transfers between devices, clips_to_devices(): lax.ppermute(sent[k], TIME, [(i, i ^ k) for i in range(peers)])  13 us
    pallas_call x1, Pallas kernels, projector_back(): pl.pallas_call(functools.partial(projector_kernel, cell_count=cell_count)...  8.7 us
    ppermute x12, waiting for transfers between devices, from_peer(): return lax.ppermute(x, axes, [(i, i ^ k) for i in range(4)])  8.66 us
    all_to_all x1, starting transfers between devices, from_all(): lax.all_to_all(jnp.broadcast_to(x[None], (peers, *x.shape)), axes, 0, 0,...  8.5 us
    pallas_call x1, Pallas kernels, per_device(): plan.call(mixed_step, False, [here, 2, None, 'view', 'view'], [plan.maps_...  8.02 us
  transfers between devices with their start and end apart: 28, of which 16 were waited for; matrix products, arithmetic and copies ran while one was open for 0% of the time, Pallas kernels for 7%

profile of v6, /device:TPU:1, one launch (start us, length us, event | category | flops | bytes accessed | tf_op | source)
XLA Modules:
  0.0 142.0 jit_solution(9147499178591786766)
XLA Ops:
  0.7 2.1 %shard_map.104 = (bf16[1040,128]{1,0:T(8,128)(2,1)S(1)}, bf16[1040,128]{1,0:T(8,128)(2,1)S(1)}, bf16[1040,128]{1,0:T(8,128)(2,1)S(1)}, bf16[1040,128]{1,0:T(8,12...) custom-call(s32[7]{0:T(128)S(1)} %stack.61.place_ref, ...), custom_call_target="tpu_custom_call" | custom-call | tf_op jit(solution)/shard_map/pallas_call | solution.py:417
  2.9 3.1 %collective-permute-start.4 = (bf16[1040,128]{1,0:T(8,128)(2,1)S(1)}, bf16[1040,128]{1,0:T(8,128)(2,1)S(1)}, u32[]{:S(2)}, u32[]{:S(2)}) collective-permute-start(bf16[1040,128]{1,0:T(8,128)(2,1)S(1)} %get-tuple-element.24), channel_id=1, source_target_pairs={{0,40},{8,32},{16,56},{24,48},{32,8},{40,0},{48,24},{56,16},{1,41}... | collective-permute-start | bytes 798728 | tf_op jit(solution)/shard_map/ppermute | solution.py:430
  6.0 2.6 %collective-permute-start.5 = (bf16[1040,128]{1,0:T(8,128)(2,1)S(1)}, bf16[1040,128]{1,0:T(8,128)(2,1)S(1)}, u32[]{:S(2)}, u32[]{:S(2)}) collective-permute-start(bf16[1040,128]{1,0:T(8,128)(2,1)S(1)} %get-tuple-element.25), channel_id=1, source_target_pairs={{0,48},{8,56},{16,32},{24,40},{32,16},{40,24},{48,0},{56,8},{1,49}... | collective-permute-start | bytes 798728 | tf_op jit(solution)/shard_map/ppermute | solution.py:430
  9.6 3.8 %collective-permute-start.1 = (bf16[1040,128]{1,0:T(8,128)(2,1)S(1)}, bf16[1040,128]{1,0:T(8,128)(2,1)S(1)}, u32[]{:S(2)}, u32[]{:S(2)}) collective-permute-start(bf16[1040,128]{1,0:T(8,128)(2,1)S(1)} %get-tuple-element.21), channel_id=1, source_target_pairs={{0,16},{8,24},{16,0},{24,8},{32,48},{40,56},{48,32},{56,40},{1,17}... | collective-permute-start | bytes 798728 | tf_op jit(solution)/shard_map/ppermute | solution.py:430
  14.7 5.7 %collective-permute-done.5.refs_6_.piece_ref = bf16[1040,128]{1,0:T(8,128)(2,1)S(1)} collective-permute-done((bf16[1040,128]{1,0:T(8,128)(2,1)S(1)}, bf16[1040,128]{1,0:T(8,128)(2,1)S(1)}, u32[]{:S(2)}, u32[]{:S(2)}) %collective-permute-start.5) | collective-permute-done | bytes 266272 | tf_op jit(solution)/shard_map/ppermute | solution.py:430
  24.1 1.9 %collective-permute-done.6.refs_7_.piece_ref = bf16[1040,128]{1,0:T(8,128)(2,1)S(1)} collective-permute-done((bf16[1040,128]{1,0:T(8,128)(2,1)S(1)}, bf16[1040,128]{1,0:T(8,128)(2,1)S(1)}, u32[]{:S(2)}, u32[]{:S(2)}) %collective-permute-start.6) | collective-permute-done | bytes 266272 | tf_op jit(solution)/shard_map/ppermute | solution.py:430
  27.2 5.9 %collective-permute-done.1.refs_2_.piece_ref = bf16[1040,128]{1,0:T(8,128)(2,1)S(1)} collective-permute-done((bf16[1040,128]{1,0:T(8,128)(2,1)S(1)}, bf16[1040,128]{1,0:T(8,128)(2,1)S(1)}, u32[]{:S(2)}, u32[]{:S(2)}) %collective-permute-start.1) | collective-permute-done | bytes 266272 | tf_op jit(solution)/shard_map/ppermute | solution.py:430
  33.7 4.7 %collective-permute-done.2.refs_3_.piece_ref = bf16[1040,128]{1,0:T(8,128)(2,1)S(1)} collective-permute-done((bf16[1040,128]{1,0:T(8,128)(2,1)S(1)}, bf16[1040,128]{1,0:T(8,128)(2,1)S(1)}, u32[]{:S(2)}, u32[]{:S(2)}) %collective-permute-start.2) | collective-permute-done | bytes 266272 | tf_op jit(solution)/shard_map/ppermute | solution.py:430
  40.8 2.4 %collective-permute-start.7 = (f32[8,2,16,128]{3,2,1,0:T(8,128)S(1)}, f32[8,2,16,128]{3,2,1,0:T(8,128)S(1)}, u32[]{:S(2)}, u32[]{:S(2)}) collective-permute-start(f32[8,2,16,128]{3,2,1,0:T(8,128)S(1)} %get-tuple-element.29), channel_id=1, source_target_pairs={{0,96},{32,64},{64,32},{96,0},{1,97},{33,65},{65,33},{97,1},{2,98}... | collective-permute-start | bytes 393224 | tf_op jit(solution)/shard_map/ppermute | solution.py:516
  43.2 3.4 %collective-permute-done.7.refs_2_ = f32[8,2,16,128]{3,2,1,0:T(8,128)S(1)} collective-permute-done((f32[8,2,16,128]{3,2,1,0:T(8,128)S(1)}, f32[8,2,16,128]{3,2,1,0:T(8,128)S(1)}, u32[]{:S(2)}, u32[]{:S(2)}) %collective-permute-start.7) | collective-permute-done | bytes 131104 | tf_op jit(solution)/shard_map/ppermute | solution.py:516
  46.6 8.0 %shard_map.116 = (bf16[32,8,2,16,128]{4,3,2,1,0:T(8,128)(2,1)}, f32[32,8,2,16,128]{4,3,2,1,0:T(8,128)}, f32[1,128]{1,0:T(1,128)S(1)}) custom-call(s32[7]{0:T(128)S(1)} %stack.61.place_ref, bf16[32,8,2,16,128]{4,3,2,1,0:T(8,128)(2,1)S(1)} %get-tuple-element.27.refs_0_, f32[8,4,128]{2,1,0:T(4,128)S(1)} %get-tuple-element.28.refs_1_.refs_3_, ...), custom_call_target="tpu_custom_call" | custom-call | flops 4831838208 | bytes 4194304 | tf_op jit(solution)/shard_map/pallas_call | solution.py:590
  57.6 8.5 %all-to-all-start = ((f32[64,2,128]{2,1,0:T(2,128)}), f32[64,2,128]{2,1,0:T(2,128)S(1)}, u32[]{:S(2)}, u32[]{:S(2)}) async-start(f32[64,2,128]{2,1,0:T(2,128)} %broadcast_in_dim.2), calls=%async_computation | async-start | bytes 131072 | tf_op jit(solution)/shard_map/all_to_all | solution.py:372
  68.2 6.2 %all-to-all-done = f32[64,2,128]{2,1,0:T(2,128)S(1)} async-done(((f32[64,2,128]{2,1,0:T(2,128)}), f32[64,2,128]{2,1,0:T(2,128)S(1)}, u32[]{:S(2)}, u32[]{:S(2)}) %all-to-all-start) | async-done | bytes 65568 | tf_op jit(solution)/shard_map/all_to_all | solution.py:372
  74.4 8.7 %shard_map.117.refs_2_.refs_5_ = f32[1,128]{1,0:T(1,128)S(1)} custom-call(s32[7]{0:T(128)S(1)} %stack.61.place_ref, f32[4,32,128]{2,1,0:T(8,128)S(1)} %bitcast.52, f32[128,2048]{1,0:T(8,128)S(1)} %copy-done.2, f32[1,2048]{1,0:T(1,128)S(1)} %bitcast.53, bf16[2048,2048]{1,0:T(8,128)(2,1)} %far_ref.1), custom_call_target="tpu_custom_call" | custom-call | flops 805306368 | bytes 8388608 | tf_op jit(solution)/shard_map/pallas_call | solution.py:496
  83.1 5.3 %shard_map.118 = (bf16[32,8,2,16,128]{4,3,2,1,0:T(8,128)(2,1)S(1)}, f32[32,8,2,16,128]{4,3,2,1,0:T(8,128)S(1)}, f32[8,2,16,128]{3,2,1,0:T(8,128)S(1)}) custom-call(s32[7]{0:T(128)S(1)} %stack.61.place_ref, f32[32,8,2,16,128]{4,3,2,1,0:T(8,128)S(1)} %copy-done.8, f32[8,4,128]{2,1,0:T(4,128)S(1)} %get-tuple-element.28.refs_1_.refs_3_, ...), custom_call_target="tpu_custom_call" | custom-call | flops 4831838208 | bytes 4194304 | tf_op jit(solution)/shard_map/pallas_call | solution.py:603
  89.4 4.5 %shard_map.120 = f32[1152,128]{1,0:T(8,128)S(1)} custom-call(s32[7]{0:T(128)S(1)} %stack.61.place_ref, bf16[32,8,2,16,128]{4,3,2,1,0:T(8,128)(2,1)S(1)} %copy-done.9, bf16[32,8,2,16,128]{4,3,2,1,0:T(8,128)(2,1)S(1)} %get-tuple-element.35.refs_1_), custom_call_target="tpu_custom_call" | custom-call | flops 4831838208 | bytes 4194304 | tf_op jit(solution)/shard_map/pallas_call | solution.py:612
  94.0 5.5 %shard_map.119 = f32[1152,128]{1,0:T(8,128)S(1)} custom-call(s32[7]{0:T(128)S(1)} %stack.61.place_ref, bf16[8,1040,128]{2,1,0:T(8,128)(2,1)S(1)} %copy-done.1, f32[32,8,2,16,128]{4,3,2,1,0:T(8,128)S(1)} %copy-done.8, f32[32,8,2,16,128]{4,3,2,1,0:T(8,128)S(1)} %get-tuple-element.32.refs_2_, f32[8,4,128]{2,1,0:T(4,128)S(1)} %get-tuple-element.28.refs_1_.refs_3_, ...), custom_call_target="tpu_custom_call" | custom-call | flops 4831838208 | bytes 4194304 | tf_op jit(solution)/shard_map/pallas_call | solution.py:620
  99.5 2.7 %collective-permute-start.10 = (f32[2,4,144,128]{3,2,0,1:T(8,128)S(1)}, f32[2,4,144,128]{3,2,0,1:T(8,128)S(1)}, u32[]{:S(2)}, u32[]{:S(2)}) collective-permute-start(f32[2,4,144,128]{3,2,0,1:T(8,128)S(1)} %fusion.1), channel_id=1, source_target_pairs={{0,1},{1,0},{2,3},{3,2},{4,5},{5,4},{6,7},{7,6},{8,9},{9,8},{10,11... | collective-permute-start | bytes 1769480 | tf_op jit(solution)/shard_map/ppermute | solution.py:361
  102.2 1.6 %collective-permute-done.10 = f32[2,4,144,128]{3,2,0,1:T(8,128)S(1)} collective-permute-done((f32[2,4,144,128]{3,2,0,1:T(8,128)S(1)}, f32[2,4,144,128]{3,2,0,1:T(8,128)S(1)}, u32[]{:S(2)}, u32[]{:S(2)}) %collective-permute-start.10) | collective-permute-done | bytes 589856 | tf_op jit(solution)/shard_map/ppermute | solution.py:361
  104.4 1.8 %collective-permute-start.12 = (bf16[2,144,128]{2,1,0:T(8,128)(2,1)S(1)}, bf16[2,144,128]{2,1,0:T(8,128)(2,1)S(1)}, u32[]{:S(2)}, u32[]{:S(2)}) collective-permute-start(bf16[2,144,128]{2,1,0:T(8,128)(2,1)S(1)} %get-tuple-element.38), channel_id=1, source_target_pairs={{0,4},{2,6},{4,0},{6,2},{1,5},{3,7},{5,1},{7,3},{8,12},{10,14},{12... | collective-permute-start | bytes 221192 | tf_op jit(solution)/shard_map/ppermute | solution.py:520
  106.2 1.8 %collective-permute-start.13 = (bf16[2,144,128]{2,1,0:T(8,128)(2,1)S(1)}, bf16[2,144,128]{2,1,0:T(8,128)(2,1)S(1)}, u32[]{:S(2)}, u32[]{:S(2)}) collective-permute-start(bf16[2,144,128]{2,1,0:T(8,128)(2,1)S(1)} %get-tuple-element.37), channel_id=1, source_target_pairs={{0,6},{2,4},{4,2},{6,0},{1,7},{3,5},{5,3},{7,1},{8,14},{10,12},{12... | collective-permute-start | bytes 221192 | tf_op jit(solution)/shard_map/ppermute | solution.py:520
  107.9 2.0 %collective-permute-done.12 = bf16[2,144,128]{2,1,0:T(8,128)(2,1)S(1)} collective-permute-done((bf16[2,144,128]{2,1,0:T(8,128)(2,1)S(1)}, bf16[2,144,128]{2,1,0:T(8,128)(2,1)S(1)}, u32[]{:S(2)}, u32[]{:S(2)}) %collective-permute-start.12) | collective-permute-done | bytes 73760 | tf_op jit(solution)/shard_map/ppermute | solution.py:520
  111.5 1.8 %collective-permute-start.15 = (bf16[2,144,128]{2,1,0:T(8,128)(2,1)S(1)}, bf16[2,144,128]{2,1,0:T(8,128)(2,1)S(1)}, u32[]{:S(2)}, u32[]{:S(2)}) collective-permute-start(bf16[2,144,128]{2,1,0:T(8,128)(2,1)S(1)} %fusion.8), channel_id=1, source_target_pairs={{0,16},{8,24},{16,0},{24,8},{1,17},{9,25},{17,1},{25,9},{2,18},{10... | collective-permute-start | bytes 221192 | tf_op jit(solution)/shard_map/ppermute | solution.py:520
  113.3 1.8 %collective-permute-start.16 = (bf16[2,144,128]{2,1,0:T(8,128)(2,1)S(1)}, bf16[2,144,128]{2,1,0:T(8,128)(2,1)S(1)}, u32[]{:S(2)}, u32[]{:S(2)}) collective-permute-start(bf16[2,144,128]{2,1,0:T(8,128)(2,1)S(1)} %fusion.8), channel_id=1, source_target_pairs={{0,24},{8,16},{16,8},{24,0},{1,25},{9,17},{17,9},{25,1},{2,26},{10... | collective-permute-start | bytes 221192 | tf_op jit(solution)/shard_map/ppermute | solution.py:520
  116.2 1.9 %collective-permute-done.16 = bf16[2,144,128]{2,1,0:T(8,128)(2,1)S(1)} collective-permute-done((bf16[2,144,128]{2,1,0:T(8,128)(2,1)S(1)}, bf16[2,144,128]{2,1,0:T(8,128)(2,1)S(1)}, u32[]{:S(2)}, u32[]{:S(2)}) %collective-permute-start.16) | collective-permute-done | bytes 73760 | tf_op jit(solution)/shard_map/ppermute | solution.py:520
  119.5 2.5 %collective-permute-start.19 = (bf16[2,144,128]{2,1,0:T(8,128)(2,1)S(1)}, bf16[2,144,128]{2,1,0:T(8,128)(2,1)S(1)}, u32[]{:S(2)}, u32[]{:S(2)}) collective-permute-start(bf16[2,144,128]{2,1,0:T(8,128)(2,1)S(1)} %add_convert_fusion.2), channel_id=1, source_target_pairs={{0,64},{32,96},{64,0},{96,32},{1,65},{33,97},{65,1},{97,33},{2,66}... | collective-permute-start | bytes 221192 | tf_op jit(solution)/shard_map/ppermute | solution.py:520
  122.7 1.9 %collective-permute-done.19 = bf16[2,144,128]{2,1,0:T(8,128)(2,1)S(1)} collective-permute-done((bf16[2,144,128]{2,1,0:T(8,128)(2,1)S(1)}, bf16[2,144,128]{2,1,0:T(8,128)(2,1)S(1)}, u32[]{:S(2)}, u32[]{:S(2)}) %collective-permute-start.19) | collective-permute-done | bytes 73760 | tf_op jit(solution)/shard_map/ppermute | solution.py:520
  124.7 2.5 %collective-permute-start.21 = (bf16[2,2,144,128]{3,2,1,0:T(8,128)(2,1)S(1)}, bf16[2,2,144,128]{3,2,1,0:T(8,128)(2,1)S(1)}, u32[]{:S(2)}, u32[]{:S(2)}) collective-permute-start(bf16[2,2,144,128]{3,2,1,0:T(8,128)(2,1)S(1)} %pad_maximum_fusion.refs_0_), channel_id=1, source_target_pairs={{0,4},{2,6},{4,0},{6,2},{1,5},{3,7},{5,1},{7,3},{8,12},{10,14},{12... | collective-permute-start | bytes 442376 | tf_op jit(solution)/shard_map/ppermute | solution.py:520
  128.6 5.2 %collective-permute-start.23 = (bf16[2,2,144,128]{3,2,1,0:T(8,128)(2,1)S(1)}, bf16[2,2,144,128]{3,2,1,0:T(8,128)(2,1)S(1)}, u32[]{:S(2)}, u32[]{:S(2)}) collective-permute-start(bf16[2,2,144,128]{3,2,1,0:T(8,128)(2,1)S(1)} %pad_maximum_fusion.refs_0_), channel_id=1, source_target_pairs={{0,1},{1,0},{2,3},{3,2},{4,5},{5,4},{6,7},{7,6},{8,9},{9,8},{10,11... | collective-permute-start | bytes 442376 | tf_op jit(solution)/shard_map/ppermute | solution.py:361
  134.3 3.0 %collective-permute-start.25 = (bf16[2,2,144,128]{3,2,1,0:T(8,128)(2,1)S(1)}, bf16[2,2,144,128]{3,2,1,0:T(8,128)(2,1)S(1)}, u32[]{:S(2)}, u32[]{:S(2)}) collective-permute-start(bf16[2,2,144,128]{3,2,1,0:T(8,128)(2,1)S(1)} %collective-permute-done.21.refs_2_), channel_id=1, source_target_pairs={{0,1},{1,0},{2,3},{3,2},{4,5},{5,4},{6,7},{7,6},{8,9},{9,8},{10,11... | collective-permute-start | bytes 442376 | tf_op jit(solution)/shard_map/ppermute | solution.py:361
  137.2 1.7 %collective-permute-start.26 = (bf16[2,2,144,128]{3,2,1,0:T(8,128)(2,1)S(1)}, bf16[2,2,144,128]{3,2,1,0:T(8,128)(2,1)S(1)}, u32[]{:S(2)}, u32[]{:S(2)}) collective-permute-start(bf16[2,2,144,128]{3,2,1,0:T(8,128)(2,1)S(1)} %collective-permute-done.22.refs_3_), channel_id=1, source_target_pairs={{0,1},{1,0},{2,3},{3,2},{4,5},{5,4},{6,7},{7,6},{8,9},{9,8},{10,11... | collective-permute-start | bytes 442376 | tf_op jit(solution)/shard_map/ppermute | solution.py:361
  139.9 2.1 %shard_map.121 = (f32[2,1152,128]{2,1,0:T(8,128)}, f32[2,1152,128]{2,1,0:T(8,128)}) custom-call(s32[7]{0:T(128)S(1)} %stack.61.place_ref, bf16[2,2,144,128]{3,2,1,0:T(8,128)(2,1)S(1)} %pad_maximum_fusion.refs_0_, bf16[2,2,144,128]{3,2,1,0:T(8,128)(2,1)S(1)} %collective-permute-done.20.refs_1_, bf16[2,2,144,128]{3,2,1,0:T(8,128)(2,1)S(1)} %collective-permute-done.21.refs_2_, ...), custom_call_target="tpu_custom_call" | custom-call | tf_op jit(solution)/shard_map/pallas_call | solution.py:559
  (74 shorter events, 24.4 us)
Async XLA Ops:
  0.6 21.0 %copy-start.3 = (bf16[2,1152,128]{2,1,0:T(8,128)(2,1)S(1)}, bf16[2,1152,128]{2,1,0:T(8,128)(2,1)}, u32[]{:S(2)}) copy-start(bf16[2,1152,128]{2,1,0:T(8,128)(2,1)} %weights_ref.1) | copy-start | bytes 1769476
  2.9 10.5 %collective-permute-start.4 = (bf16[1040,128]{1,0:T(8,128)(2,1)S(1)}, bf16[1040,128]{1,0:T(8,128)(2,1)S(1)}, u32[]{:S(2)}, u32[]{:S(2)}) collective-permute-start(bf16[1040,128]{1,0:T(8,128)(2,1)S(1)} %get-tuple-element.24), channel_id=1, source_target_pairs={{0,40},{8,32},{16,56},{24,48},{32,8},{40,0},{48,24},{56,16},{1,41}... | collective-permute-start | bytes 798728 | tf_op jit(solution)/shard_map/ppermute | solution.py:430
  6.0 14.4 %collective-permute-start.5 = (bf16[1040,128]{1,0:T(8,128)(2,1)S(1)}, bf16[1040,128]{1,0:T(8,128)(2,1)S(1)}, u32[]{:S(2)}, u32[]{:S(2)}) collective-permute-start(bf16[1040,128]{1,0:T(8,128)(2,1)S(1)} %get-tuple-element.25), channel_id=1, source_target_pairs={{0,48},{8,56},{16,32},{24,40},{32,16},{40,24},{48,0},{56,8},{1,49}... | collective-permute-start | bytes 798728 | tf_op jit(solution)/shard_map/ppermute | solution.py:430
  8.6 17.4 %collective-permute-start.6 = (bf16[1040,128]{1,0:T(8,128)(2,1)S(1)}, bf16[1040,128]{1,0:T(8,128)(2,1)S(1)}, u32[]{:S(2)}, u32[]{:S(2)}) collective-permute-start(bf16[1040,128]{1,0:T(8,128)(2,1)S(1)} %get-tuple-element.26), channel_id=1, source_target_pairs={{0,56},{8,48},{16,40},{24,32},{32,24},{40,16},{48,8},{56,0},{1,57}... | collective-permute-start | bytes 798728 | tf_op jit(solution)/shard_map/ppermute | solution.py:430
  9.5 17.1 %collective-permute-start = (bf16[1040,128]{1,0:T(8,128)(2,1)S(1)}, bf16[1040,128]{1,0:T(8,128)(2,1)S(1)}, u32[]{:S(2)}, u32[]{:S(2)}) collective-permute-start(bf16[1040,128]{1,0:T(8,128)(2,1)S(1)} %get-tuple-element.20), channel_id=1, source_target_pairs={{0,8},{8,0},{16,24},{24,16},{32,40},{40,32},{48,56},{56,48},{1,9},... | collective-permute-start | bytes 798728 | tf_op jit(solution)/shard_map/ppermute | solution.py:430
  9.6 23.6 %collective-permute-start.1 = (bf16[1040,128]{1,0:T(8,128)(2,1)S(1)}, bf16[1040,128]{1,0:T(8,128)(2,1)S(1)}, u32[]{:S(2)}, u32[]{:S(2)}) collective-permute-start(bf16[1040,128]{1,0:T(8,128)(2,1)S(1)} %get-tuple-element.21), channel_id=1, source_target_pairs={{0,16},{8,24},{16,0},{24,8},{32,48},{40,56},{48,32},{56,40},{1,17}... | collective-permute-start | bytes 798728 | tf_op jit(solution)/shard_map/ppermute | solution.py:430
  13.4 25.0 %collective-permute-start.2 = (bf16[1040,128]{1,0:T(8,128)(2,1)S(1)}, bf16[1040,128]{1,0:T(8,128)(2,1)S(1)}, u32[]{:S(2)}, u32[]{:S(2)}) collective-permute-start(bf16[1040,128]{1,0:T(8,128)(2,1)S(1)} %get-tuple-element.22), channel_id=1, source_target_pairs={{0,24},{8,16},{16,8},{24,0},{32,56},{40,48},{48,40},{56,32},{1,25}... | collective-permute-start | bytes 798728 | tf_op jit(solution)/shard_map/ppermute | solution.py:430
  20.4 18.6 %collective-permute-start.3 = (bf16[1040,128]{1,0:T(8,128)(2,1)S(1)}, bf16[1040,128]{1,0:T(8,128)(2,1)S(1)}, u32[]{:S(2)}, u32[]{:S(2)}) collective-permute-start(bf16[1040,128]{1,0:T(8,128)(2,1)S(1)} %get-tuple-element.23), channel_id=1, source_target_pairs={{0,32},{8,40},{16,48},{24,56},{32,0},{40,8},{48,16},{56,24},{1,33}... | collective-permute-start | bytes 798728 | tf_op jit(solution)/shard_map/ppermute | solution.py:430
  40.8 5.8 %collective-permute-start.7 = (f32[8,2,16,128]{3,2,1,0:T(8,128)S(1)}, f32[8,2,16,128]{3,2,1,0:T(8,128)S(1)}, u32[]{:S(2)}, u32[]{:S(2)}) collective-permute-start(f32[8,2,16,128]{3,2,1,0:T(8,128)S(1)} %get-tuple-element.29), channel_id=1, source_target_pairs={{0,96},{32,64},{64,32},{96,0},{1,97},{33,65},{65,33},{97,1},{2,98}... | collective-permute-start | bytes 393224 | tf_op jit(solution)/shard_map/ppermute | solution.py:516
  54.7 2.2 %collective-permute-start.8 = (f32[128]{0:T(128)S(1)}, f32[128]{0:T(128)S(1)}, u32[]{:S(2)}, u32[]{:S(2)}) collective-permute-start(f32[128]{0:T(128)S(1)} %bitcast.54), channel_id=1, source_target_pairs={{0,1},{1,0},{2,3},{3,2},{4,5},{5,4},{6,7},{7,6},{8,9},{9,8},{10,11... | collective-permute-start | bytes 1544 | tf_op jit(solution)/shard_map/ppermute | solution.py:361
  57.6 16.8 %all-to-all-start = ((f32[64,2,128]{2,1,0:T(2,128)}), f32[64,2,128]{2,1,0:T(2,128)S(1)}, u32[]{:S(2)}, u32[]{:S(2)}) async-start(f32[64,2,128]{2,1,0:T(2,128)} %broadcast_in_dim.2), calls=%async_computation | async-start | bytes 131072 | tf_op jit(solution)/shard_map/all_to_all | solution.py:372
  66.1 8.3 %copy-start.2 = (f32[128,2048]{1,0:T(8,128)S(1)}, f32[128,2048]{1,0:T(8,128)}, u32[]{:S(2)}) copy-start(f32[128,2048]{1,0:T(8,128)} %in_ref.1) | copy-start | bytes 3145732
  74.4 8.7 %copy-start.6 = (bf16[2,1152,128]{2,1,0:T(8,128)(2,1)S(1)}, bf16[2,1152,128]{2,1,0:T(8,128)(2,1)}, u32[]{:S(2)}) copy-start(bf16[2,1152,128]{2,1,0:T(8,128)(2,1)} %refs_3_.1) | copy-start | bytes 1769476
  74.4 8.7 %copy-start.8 = (f32[32,8,2,16,128]{4,3,2,1,0:T(8,128)S(1)}, f32[32,8,2,16,128]{4,3,2,1,0:T(8,128)}, u32[]{:S(2)}) copy-start(f32[32,8,2,16,128]{4,3,2,1,0:T(8,128)} %get-tuple-element.30.refs_0_.refs_1_) | copy-start | bytes 12582916
  88.4 5.6 %collective-permute-start.9 = (f32[8,2,16,128]{3,2,1,0:T(8,128)S(1)}, f32[8,2,16,128]{3,2,1,0:T(8,128)S(1)}, u32[]{:S(2)}, u32[]{:S(2)}) collective-permute-start(f32[8,2,16,128]{3,2,1,0:T(8,128)S(1)} %get-tuple-element.33), channel_id=1, source_target_pairs={{0,96},{32,64},{64,32},{96,0},{1,97},{33,65},{65,33},{97,1},{2,98}... | collective-permute-start | bytes 393224 | tf_op jit(solution)/shard_map/ppermute | solution.py:516
  99.5 4.4 %collective-permute-start.10 = (f32[2,4,144,128]{3,2,0,1:T(8,128)S(1)}, f32[2,4,144,128]{3,2,0,1:T(8,128)S(1)}, u32[]{:S(2)}, u32[]{:S(2)}) collective-permute-start(f32[2,4,144,128]{3,2,0,1:T(8,128)S(1)} %fusion.1), channel_id=1, source_target_pairs={{0,1},{1,0},{2,3},{3,2},{4,5},{5,4},{6,7},{7,6},{8,9},{9,8},{10,11... | collective-permute-start | bytes 1769480 | tf_op jit(solution)/shard_map/ppermute | solution.py:361
  104.0 3.9 %collective-permute-start.11 = (bf16[2,144,128]{2,1,0:T(8,128)(2,1)S(1)}, bf16[2,144,128]{2,1,0:T(8,128)(2,1)S(1)}, u32[]{:S(2)}, u32[]{:S(2)}) collective-permute-start(bf16[2,144,128]{2,1,0:T(8,128)(2,1)S(1)} %get-tuple-element.36), channel_id=1, source_target_pairs={{0,2},{2,0},{4,6},{6,4},{1,3},{3,1},{5,7},{7,5},{8,10},{10,8},{12,... | collective-permute-start | bytes 221192 | tf_op jit(solution)/shard_map/ppermute | solution.py:520
  104.4 5.6 %collective-permute-start.12 = (bf16[2,144,128]{2,1,0:T(8,128)(2,1)S(1)}, bf16[2,144,128]{2,1,0:T(8,128)(2,1)S(1)}, u32[]{:S(2)}, u32[]{:S(2)}) collective-permute-start(bf16[2,144,128]{2,1,0:T(8,128)(2,1)S(1)} %get-tuple-element.38), channel_id=1, source_target_pairs={{0,4},{2,6},{4,0},{6,2},{1,5},{3,7},{5,1},{7,3},{8,12},{10,14},{12... | collective-permute-start | bytes 221192 | tf_op jit(solution)/shard_map/ppermute | solution.py:520
  106.2 4.9 %collective-permute-start.13 = (bf16[2,144,128]{2,1,0:T(8,128)(2,1)S(1)}, bf16[2,144,128]{2,1,0:T(8,128)(2,1)S(1)}, u32[]{:S(2)}, u32[]{:S(2)}) collective-permute-start(bf16[2,144,128]{2,1,0:T(8,128)(2,1)S(1)} %get-tuple-element.37), channel_id=1, source_target_pairs={{0,6},{2,4},{4,2},{6,0},{1,7},{3,5},{5,3},{7,1},{8,14},{10,12},{12... | collective-permute-start | bytes 221192 | tf_op jit(solution)/shard_map/ppermute | solution.py:520
  111.2 3.9 %collective-permute-start.14 = (bf16[2,144,128]{2,1,0:T(8,128)(2,1)S(1)}, bf16[2,144,128]{2,1,0:T(8,128)(2,1)S(1)}, u32[]{:S(2)}, u32[]{:S(2)}) collective-permute-start(bf16[2,144,128]{2,1,0:T(8,128)(2,1)S(1)} %fusion.8), channel_id=1, source_target_pairs={{0,8},{8,0},{16,24},{24,16},{1,9},{9,1},{17,25},{25,17},{2,10},{10... | collective-permute-start | bytes 221192 | tf_op jit(solution)/shard_map/ppermute | solution.py:520
  111.5 4.7 %collective-permute-start.15 = (bf16[2,144,128]{2,1,0:T(8,128)(2,1)S(1)}, bf16[2,144,128]{2,1,0:T(8,128)(2,1)S(1)}, u32[]{:S(2)}, u32[]{:S(2)}) collective-permute-start(bf16[2,144,128]{2,1,0:T(8,128)(2,1)S(1)} %fusion.8), channel_id=1, source_target_pairs={{0,16},{8,24},{16,0},{24,8},{1,17},{9,25},{17,1},{25,9},{2,18},{10... | collective-permute-start | bytes 221192 | tf_op jit(solution)/shard_map/ppermute | solution.py:520
  113.3 4.7 %collective-permute-start.16 = (bf16[2,144,128]{2,1,0:T(8,128)(2,1)S(1)}, bf16[2,144,128]{2,1,0:T(8,128)(2,1)S(1)}, u32[]{:S(2)}, u32[]{:S(2)}) collective-permute-start(bf16[2,144,128]{2,1,0:T(8,128)(2,1)S(1)} %fusion.8), channel_id=1, source_target_pairs={{0,24},{8,16},{16,8},{24,0},{1,25},{9,17},{17,9},{25,1},{2,26},{10... | collective-permute-start | bytes 221192 | tf_op jit(solution)/shard_map/ppermute | solution.py:520
  118.1 4.5 %collective-permute-start.17 = (bf16[2,144,128]{2,1,0:T(8,128)(2,1)S(1)}, bf16[2,144,128]{2,1,0:T(8,128)(2,1)S(1)}, u32[]{:S(2)}, u32[]{:S(2)}) collective-permute-start(bf16[2,144,128]{2,1,0:T(8,128)(2,1)S(1)} %add_convert_fusion.2), channel_id=1, source_target_pairs={{0,96},{32,64},{64,32},{96,0},{1,97},{33,65},{65,33},{97,1},{2,98}... | collective-permute-start | bytes 221192 | tf_op jit(solution)/shard_map/ppermute | solution.py:520
  119.5 3.2 %collective-permute-start.18 = (bf16[2,144,128]{2,1,0:T(8,128)(2,1)S(1)}, bf16[2,144,128]{2,1,0:T(8,128)(2,1)S(1)}, u32[]{:S(2)}, u32[]{:S(2)}) collective-permute-start(bf16[2,144,128]{2,1,0:T(8,128)(2,1)S(1)} %add_convert_fusion.2), channel_id=1, source_target_pairs={{0,32},{32,0},{64,96},{96,64},{1,33},{33,1},{65,97},{97,65},{2,34}... | collective-permute-start | bytes 221192 | tf_op jit(solution)/shard_map/ppermute | solution.py:520
  119.5 5.1 %collective-permute-start.19 = (bf16[2,144,128]{2,1,0:T(8,128)(2,1)S(1)}, bf16[2,144,128]{2,1,0:T(8,128)(2,1)S(1)}, u32[]{:S(2)}, u32[]{:S(2)}) collective-permute-start(bf16[2,144,128]{2,1,0:T(8,128)(2,1)S(1)} %add_convert_fusion.2), channel_id=1, source_target_pairs={{0,64},{32,96},{64,0},{96,32},{1,65},{33,97},{65,1},{97,33},{2,66}... | collective-permute-start | bytes 221192 | tf_op jit(solution)/shard_map/ppermute | solution.py:520
  124.6 9.2 %collective-permute-start.20 = (bf16[2,2,144,128]{3,2,1,0:T(8,128)(2,1)S(1)}, bf16[2,2,144,128]{3,2,1,0:T(8,128)(2,1)S(1)}, u32[]{:S(2)}, u32[]{:S(2)}) collective-permute-start(bf16[2,2,144,128]{3,2,1,0:T(8,128)(2,1)S(1)} %pad_maximum_fusion.refs_0_), channel_id=1, source_target_pairs={{0,2},{2,0},{4,6},{6,4},{1,3},{3,1},{5,7},{7,5},{8,10},{10,8},{12,... | collective-permute-start | bytes 442376 | tf_op jit(solution)/shard_map/ppermute | solution.py:520
  124.7 9.5 %collective-permute-start.21 = (bf16[2,2,144,128]{3,2,1,0:T(8,128)(2,1)S(1)}, bf16[2,2,144,128]{3,2,1,0:T(8,128)(2,1)S(1)}, u32[]{:S(2)}, u32[]{:S(2)}) collective-permute-start(bf16[2,2,144,128]{3,2,1,0:T(8,128)(2,1)S(1)} %pad_maximum_fusion.refs_0_), channel_id=1, source_target_pairs={{0,4},{2,6},{4,0},{6,2},{1,5},{3,7},{5,1},{7,3},{8,12},{10,14},{12... | collective-permute-start | bytes 442376 | tf_op jit(solution)/shard_map/ppermute | solution.py:520
  127.2 10.0 %collective-permute-start.22 = (bf16[2,2,144,128]{3,2,1,0:T(8,128)(2,1)S(1)}, bf16[2,2,144,128]{3,2,1,0:T(8,128)(2,1)S(1)}, u32[]{:S(2)}, u32[]{:S(2)}) collective-permute-start(bf16[2,2,144,128]{3,2,1,0:T(8,128)(2,1)S(1)} %pad_maximum_fusion.refs_0_), channel_id=1, source_target_pairs={{0,6},{2,4},{4,2},{6,0},{1,7},{3,5},{5,3},{7,1},{8,14},{10,12},{12... | collective-permute-start | bytes 442376 | tf_op jit(solution)/shard_map/ppermute | solution.py:520
  128.6 10.3 %collective-permute-start.23 = (bf16[2,2,144,128]{3,2,1,0:T(8,128)(2,1)S(1)}, bf16[2,2,144,128]{3,2,1,0:T(8,128)(2,1)S(1)}, u32[]{:S(2)}, u32[]{:S(2)}) collective-permute-start(bf16[2,2,144,128]{3,2,1,0:T(8,128)(2,1)S(1)} %pad_maximum_fusion.refs_0_), channel_id=1, source_target_pairs={{0,1},{1,0},{2,3},{3,2},{4,5},{5,4},{6,7},{7,6},{8,9},{9,8},{10,11... | collective-permute-start | bytes 442376 | tf_op jit(solution)/shard_map/ppermute | solution.py:361
  133.8 5.1 %collective-permute-start.24 = (bf16[2,2,144,128]{3,2,1,0:T(8,128)(2,1)S(1)}, bf16[2,2,144,128]{3,2,1,0:T(8,128)(2,1)S(1)}, u32[]{:S(2)}, u32[]{:S(2)}) collective-permute-start(bf16[2,2,144,128]{3,2,1,0:T(8,128)(2,1)S(1)} %collective-permute-done.20.refs_1_), channel_id=1, source_target_pairs={{0,1},{1,0},{2,3},{3,2},{4,5},{5,4},{6,7},{7,6},{8,9},{9,8},{10,11... | collective-permute-start | bytes 442376 | tf_op jit(solution)/shard_map/ppermute | solution.py:361
  134.3 4.6 %collective-permute-start.25 = (bf16[2,2,144,128]{3,2,1,0:T(8,128)(2,1)S(1)}, bf16[2,2,144,128]{3,2,1,0:T(8,128)(2,1)S(1)}, u32[]{:S(2)}, u32[]{:S(2)}) collective-permute-start(bf16[2,2,144,128]{3,2,1,0:T(8,128)(2,1)S(1)} %collective-permute-done.21.refs_2_), channel_id=1, source_target_pairs={{0,1},{1,0},{2,3},{3,2},{4,5},{5,4},{6,7},{7,6},{8,9},{9,8},{10,11... | collective-permute-start | bytes 442376 | tf_op jit(solution)/shard_map/ppermute | solution.py:361
  137.2 2.7 %collective-permute-start.26 = (bf16[2,2,144,128]{3,2,1,0:T(8,128)(2,1)S(1)}, bf16[2,2,144,128]{3,2,1,0:T(8,128)(2,1)S(1)}, u32[]{:S(2)}, u32[]{:S(2)}) collective-permute-start(bf16[2,2,144,128]{3,2,1,0:T(8,128)(2,1)S(1)} %collective-permute-done.22.refs_3_), channel_id=1, source_target_pairs={{0,1},{1,0},{2,3},{3,2},{4,5},{5,4},{6,7},{7,6},{8,9},{9,8},{10,11... | collective-permute-start | bytes 442376 | tf_op jit(solution)/shard_map/ppermute | solution.py:361
  (6 other events, 34.6 us)
